TPU v7x, 32 devices: a whole 2x2x4 slice. The times are simulated.
32 devices in a mesh: seq: 8 (over z, y), mp: 4 (over x, core).
Axes of the slice: x: 2, y: 2, z: 4, core: 2. Of those that a mesh axis runs over, the one named last changes fastest.
Arguments:
- tokens: bfloat16 [4096, 768], P('seq'), may hold values from -6 to 6
- item_lengths: int32 [8], replicated, may hold values from 1 to 2048, 4096 in all
- w_qkv: bfloat16 [3, 768, 768], P(None, None, 'mp'), may hold values from -2 to 2
- b_qv: float32 [2, 768], P(None, 'mp'), may hold values from -2 to 2
- taps: float32 [12, 33], P('mp'), may hold values from -0.072 to 0.072
- w_out: bfloat16 [768, 768], P('mp'), may hold values from -1.75 to 1.75
- b_out: float32 [768], replicated, may hold values from -3 to 3
- ln1_gain: float32 [768], replicated, may hold values from 0.5 to 1.5
- ln1_bias: float32 [768], replicated, may hold values from -2 to 2
- w_up: bfloat16 [768, 3072], P(None, 'mp'), may hold values from -0.21875 to 0.21875
- b_up: float32 [3072], P('mp'), may hold values from -3 to 3
- w_down: bfloat16 [3072, 768], P('mp'), may hold values from -0.109375 to 0.109375
- b_down: float32 [768], replicated, may hold values from -3 to 3
- ln2_gain: float32 [768], replicated, may hold values from 0.5 to 1.5
- ln2_bias: float32 [768], replicated, may hold values from -2 to 2
- d_out: bfloat16 [4096, 768], P('seq'), may hold values from -6 to 6
Outputs:
- layer_output: bfloat16 [4096, 768], P('seq')
- d_tokens: bfloat16 [4096, 768], P('seq')
- d_w_qkv: float32 [3, 768, 768], P(None, None, 'mp')
- d_b_qv: float32 [2, 768], P(None, 'mp')
- d_taps: float32 [12, 33], P('mp')
- d_w_out: float32 [768, 768], P('mp')
- d_b_out: float32 [768], replicated
- d_ln1_gain: float32 [768], replicated
- d_ln1_bias: float32 [768], replicated
- d_w_up: float32 [768, 3072], P(None, 'mp')
- d_b_up: float32 [3072], P('mp')
- d_w_down: float32 [3072, 768], P('mp')
- d_b_down: float32 [768], replicated
- d_ln2_gain: float32 [768], replicated
- d_ln2_bias: float32 [768], replicated
Inputs may be any that keep to these rules, and one draw needn't show every extreme that they name: `item_lengths`: the lengths sum to 4096; the largest is exactly 2048, and no item is longer than 4096.
All inputs are finite; a program needn't handle non-finite values.
Results may differ from a plain program's by a relative error of at most 0.017.
Values may be sent and summed in bfloat16 or wider, within the bound.
No kernel may reach another device: no remote copies, remote signals or barrier semaphores. Data moves between devices by JAX's collectives and lax.ppermute only.
A program may use at most 192 MiB of HBM per device.

v0:
```python
import math

import jax
import jax.numpy as jnp
from jax import lax
from jax.sharding import PartitionSpec as P

SHRINK = 0.95
NORM_EPS = 1e-06
LAYER_EPS = 1e-05


def padded(cells, sides, width):
    for axis, dim in sides:
        count = lax.axis_size(axis)
        ends = count - 1
        head = lax.slice_in_dim(cells, 0, width, axis=dim)
        tail = lax.slice_in_dim(cells, cells.shape[dim] - width, cells.shape[dim], axis=dim)
        cells = jnp.concatenate(
            [
                lax.ppermute(tail, axis, [(i, (i + 1) % count) for i in range(ends)]),
                cells,
                lax.ppermute(head, axis, [((i + 1) % count, i) for i in range(ends)]),
            ],
            axis=dim,
        )
    return cells


def item_index(positions, ends):
    inside = (positions >= 0) & (positions < ends[-1])
    counted = jnp.sum((positions[:, None] >= ends[None, :]).astype(jnp.int32), axis=1)
    return jnp.where(inside, counted, -1)


def layer_norm(hidden, gain, shift):
    center = hidden - jnp.mean(hidden, axis=-1, keepdims=True)
    scale = lax.rsqrt(jnp.mean(center * center, axis=-1, keepdims=True) + LAYER_EPS)
    normed = center * scale
    return (normed * gain + shift, normed, scale)


def layer_norm_back(grad, normed, scale, gain):
    d_gain = jnp.sum(grad * normed, axis=0)
    d_shift = jnp.sum(grad, axis=0)
    d_normed = grad * gain
    centered = d_normed - jnp.mean(d_normed, axis=-1, keepdims=True)
    d_hidden = scale * (centered - normed * jnp.mean(d_normed * normed, axis=-1, keepdims=True))
    return (d_hidden, d_gain, d_shift)


def block_rows(row_count):
    bound = min(row_count, 1024)
    return max((candidate for candidate in range(1, bound + 1) if row_count % candidate == 0))


def fold_blocks(carry, arrays, start, work):
    row_count = arrays[0].shape[0]
    width = block_rows(row_count)
    stacked = tuple(
        (array.reshape((row_count // width, width) + array.shape[1:]) for array in arrays)
    )
    offsets = start + width * jnp.arange(row_count // width, dtype=jnp.int32)

    def advance(state, inputs):
        return (work(state, inputs[:-1], inputs[-1]), None)

    result, _ = lax.scan(advance, carry, stacked + (offsets,))
    return result


def collision_back(queries, keys_heads, values_heads, d_attn_heads, same):
    scores = jnp.einsum("bhe,khe->hbk", queries, keys_heads, preferred_element_type=jnp.float32)
    cosine = SHRINK * scores
    closeness = 1.0 - jnp.arccos(cosine) / math.pi
    weights = (same[None] * closeness**8).astype(jnp.bfloat16)
    d_weights = jnp.einsum(
        "bhe,khe->hbk", d_attn_heads, values_heads, preferred_element_type=jnp.float32
    )
    slope = same[None] * 8.0 * closeness**7 * SHRINK / (math.pi * jnp.sqrt(1.0 - cosine * cosine))
    d_scores = (d_weights * slope).astype(jnp.bfloat16)
    return (weights, d_scores)


def per_device(
    tokens,
    item_lengths,
    w_qkv,
    b_qv,
    taps,
    w_out,
    b_out,
    ln1_gain,
    ln1_bias,
    w_up,
    b_up,
    w_down,
    b_down,
    ln2_gain,
    ln2_bias,
    d_out,
):
    local_rows = tokens.shape[0]
    heads_here = taps.shape[0]
    kernel = taps.shape[1]
    radius = (kernel - 1) // 2
    columns = w_qkv.shape[2]
    head_size = columns // heads_here
    ends = jnp.cumsum(item_lengths)
    first_row = lax.axis_index("seq") * local_rows
    query_items = item_index(first_row + jnp.arange(local_rows, dtype=jnp.int32), ends)
    rim_items = item_index(
        first_row - radius + jnp.arange(local_rows + 2 * radius, dtype=jnp.int32), ends
    )
    tap_columns = jnp.repeat(taps, head_size, axis=0).T
    bias_rows = jnp.stack([b_qv[0], jnp.zeros_like(b_qv[0]), b_qv[1]])
    projected = (
        jnp.einsum("td,ide->ite", tokens, w_qkv, preferred_element_type=jnp.float32)
        + bias_rows[:, None, :]
    )
    query_raw = projected[0].reshape(local_rows, heads_here, head_size)
    key_raw = projected[1].reshape(local_rows, heads_here, head_size)
    query_scale = lax.rsqrt(jnp.sum(query_raw * query_raw, axis=-1, keepdims=True) + NORM_EPS)
    key_scale = lax.rsqrt(jnp.sum(key_raw * key_raw, axis=-1, keepdims=True) + NORM_EPS)
    query_unit = query_raw * query_scale
    key_unit = key_raw * key_scale
    query_low = query_unit.astype(jnp.bfloat16)
    key_low = key_unit.astype(jnp.bfloat16)
    value_low = projected[2].astype(jnp.bfloat16)
    packed = jnp.concatenate([key_low.reshape(local_rows, columns), value_low], axis=1)
    zero_heads = jnp.zeros((local_rows, heads_here, head_size), jnp.float32)

    def split_pair(block):
        count = block.shape[0]
        first = block[:, :columns].reshape(count, heads_here, head_size)
        second = block[:, columns : 2 * columns].reshape(count, heads_here, head_size)
        return (first, second)

    def attend(state, pieces, offset):
        keys_heads, values_heads = split_pair(pieces[0])
        key_items = item_index(offset + jnp.arange(keys_heads.shape[0], dtype=jnp.int32), ends)
        same = (query_items[:, None] == key_items[None, :]).astype(jnp.float32)
        scores = jnp.einsum(
            "bhe,khe->hbk", query_low, keys_heads, preferred_element_type=jnp.float32
        )
        closeness = 1.0 - jnp.arccos(SHRINK * scores) / math.pi
        weights = (same[None] * closeness**8).astype(jnp.bfloat16)
        return state + jnp.einsum(
            "hbk,khe->bhe", weights, values_heads, preferred_element_type=jnp.float32
        )

    attended = fold_blocks(
        zero_heads, (lax.all_gather(packed, "seq", axis=0, tiled=True),), jnp.int32(0), attend
    )
    attn_scale = lax.rsqrt(jnp.sum(attended * attended, axis=-1, keepdims=True) + NORM_EPS)
    attn_unit = attended * attn_scale
    value_rim = padded(value_low, (("seq", 0),), radius).astype(jnp.float32)
    convolved = jnp.zeros((local_rows, columns), jnp.float32)
    same_list = []
    for shift_at in range(kernel):
        same_rows = (rim_items[shift_at : shift_at + local_rows] == query_items).astype(
            jnp.float32
        )[:, None]
        same_list.append(same_rows)
        convolved = (
            convolved
            + tap_columns[shift_at] * same_rows * value_rim[shift_at : shift_at + local_rows]
        )
    context_low = (attn_unit.reshape(local_rows, columns) + convolved).astype(jnp.bfloat16)
    branch = lax.psum(jnp.dot(context_low, w_out, preferred_element_type=jnp.float32), "mp")
    first_sum = tokens.astype(jnp.float32) + branch + b_out
    first_out, normed_one, scale_one = layer_norm(first_sum, ln1_gain, ln1_bias)
    first_low = first_out.astype(jnp.bfloat16)
    inner = jnp.dot(first_low, w_up, preferred_element_type=jnp.float32) + b_up
    act_low = jax.nn.gelu(inner, approximate=False).astype(jnp.bfloat16)
    mixed = lax.psum(jnp.dot(act_low, w_down, preferred_element_type=jnp.float32), "mp")
    second_sum = first_out + mixed + b_down
    result, normed_two, scale_two = layer_norm(second_sum, ln2_gain, ln2_bias)
    layer_output = result.astype(jnp.bfloat16)
    d_second, d_ln2_gain, d_ln2_bias = layer_norm_back(
        d_out.astype(jnp.float32), normed_two, scale_two, ln2_gain
    )
    d_second_low = d_second.astype(jnp.bfloat16)
    d_b_down = jnp.sum(d_second, axis=0)
    d_w_down = jnp.einsum("tf,td->fd", act_low, d_second_low, preferred_element_type=jnp.float32)
    d_act = jnp.einsum("td,fd->tf", d_second_low, w_down, preferred_element_type=jnp.float32)
    normal_cdf = 0.5 * (1.0 + lax.erf(inner / math.sqrt(2.0)))
    normal_pdf = jnp.exp(-0.5 * inner * inner) / math.sqrt(2.0 * math.pi)
    d_inner_low = (d_act * (normal_cdf + inner * normal_pdf)).astype(jnp.bfloat16)
    d_b_up = jnp.sum(d_inner_low.astype(jnp.float32), axis=0)
    d_w_up = jnp.einsum("td,tf->df", first_low, d_inner_low, preferred_element_type=jnp.float32)
    d_first_part = jnp.einsum("tf,df->td", d_inner_low, w_up, preferred_element_type=jnp.float32)
    d_first_out = d_second + lax.psum(d_first_part, "mp")
    d_first, d_ln1_gain, d_ln1_bias = layer_norm_back(d_first_out, normed_one, scale_one, ln1_gain)
    d_first_low = d_first.astype(jnp.bfloat16)
    d_b_out = jnp.sum(d_first, axis=0)
    d_w_out = jnp.einsum("tc,td->cd", context_low, d_first_low, preferred_element_type=jnp.float32)
    d_context_low = jnp.einsum(
        "td,cd->tc", d_first_low, w_out, preferred_element_type=jnp.float32
    ).astype(jnp.bfloat16)
    d_context = d_context_low.astype(jnp.float32)
    d_context_heads = d_context.reshape(local_rows, heads_here, head_size)
    d_attn = attn_scale * (
        d_context_heads - attn_unit * jnp.sum(attn_unit * d_context_heads, axis=-1, keepdims=True)
    )
    d_attn_low = d_attn.astype(jnp.bfloat16)
    tap_terms = []
    for shift_at in range(kernel):
        summed = jnp.sum(
            d_context * same_list[shift_at] * value_rim[shift_at : shift_at + local_rows], axis=0
        )
        tap_terms.append(jnp.sum(summed.reshape(heads_here, head_size), axis=1))
    d_taps = jnp.stack(tap_terms, axis=1)
    context_rim = padded(d_context_low, (("seq", 0),), radius).astype(jnp.float32)
    d_value_conv = jnp.zeros((local_rows, columns), jnp.float32)
    for shift_at in range(kernel):
        lower = 2 * radius - shift_at
        same_rows = (rim_items[lower : lower + local_rows] == query_items).astype(jnp.float32)[
            :, None
        ]
        d_value_conv = (
            d_value_conv
            + tap_columns[shift_at] * same_rows * context_rim[lower : lower + local_rows]
        )
    value_heads = value_low.reshape(local_rows, heads_here, head_size)
    both_packed = jnp.concatenate(
        [packed, query_low.reshape(local_rows, columns), d_attn_low.reshape(local_rows, columns)],
        axis=1,
    )

    def pair_block(state, pieces, offset):
        d_query, d_keys, d_values = state
        block = pieces[0]
        count = block.shape[0]
        keys_block, values_block = split_pair(block[:, : 2 * columns])
        queries_block, d_attn_block = split_pair(block[:, 2 * columns :])
        other_items = item_index(offset + jnp.arange(count, dtype=jnp.int32), ends)
        same = (query_items[:, None] == other_items[None, :]).astype(jnp.float32)
        weights, d_scores = collision_back(query_low, keys_block, values_block, d_attn_low, same)
        d_query = d_query + jnp.einsum(
            "hbk,khe->bhe", d_scores, keys_block, preferred_element_type=jnp.float32
        )
        weights_own, d_scores_own = collision_back(
            queries_block, key_low, value_heads, d_attn_block, same.T
        )
        d_keys = d_keys + jnp.einsum(
            "hbk,bhe->khe", d_scores_own, queries_block, preferred_element_type=jnp.float32
        )
        d_values = d_values + jnp.einsum(
            "hbk,bhe->khe", weights_own, d_attn_block, preferred_element_type=jnp.float32
        )
        return (d_query, d_keys, d_values)

    zero_state = (zero_heads, zero_heads, zero_heads)
    d_query, d_key_unit, d_value_heads = fold_blocks(
        zero_state,
        (lax.all_gather(both_packed, "seq", axis=0, tiled=True),),
        jnp.int32(0),
        pair_block,
    )
    d_value_attn = d_value_heads.reshape(local_rows, columns)
    d_query_raw = query_scale * (
        d_query - query_unit * jnp.sum(query_unit * d_query, axis=-1, keepdims=True)
    )
    d_key_raw = key_scale * (
        d_key_unit - key_unit * jnp.sum(key_unit * d_key_unit, axis=-1, keepdims=True)
    )
    d_value = d_value_attn + d_value_conv
    d_projected_low = jnp.stack(
        [d_query_raw.reshape(local_rows, columns), d_key_raw.reshape(local_rows, columns), d_value]
    ).astype(jnp.bfloat16)
    d_bias_all = jnp.sum(d_projected_low.astype(jnp.float32), axis=1)
    d_b_qv = jnp.stack([d_bias_all[0], d_bias_all[2]])
    d_w_qkv = jnp.einsum("td,ite->ide", tokens, d_projected_low, preferred_element_type=jnp.float32)
    d_tokens_part = jnp.einsum(
        "ite,ide->td", d_projected_low, w_qkv, preferred_element_type=jnp.float32
    )
    d_tokens = (
        d_first + lax.psum(d_tokens_part.astype(jnp.bfloat16), "mp").astype(jnp.float32)
    ).astype(jnp.bfloat16)
    summed_grads = (
        lax.psum(d_w_qkv.astype(jnp.bfloat16), "seq").astype(jnp.float32),
        lax.psum(d_b_qv.astype(jnp.bfloat16), "seq").astype(jnp.float32),
        lax.psum(d_taps.astype(jnp.bfloat16), "seq").astype(jnp.float32),
        lax.psum(d_w_out.astype(jnp.bfloat16), "seq").astype(jnp.float32),
        lax.psum(d_b_out.astype(jnp.bfloat16), "seq").astype(jnp.float32),
        lax.psum(d_ln1_gain.astype(jnp.bfloat16), "seq").astype(jnp.float32),
        lax.psum(d_ln1_bias.astype(jnp.bfloat16), "seq").astype(jnp.float32),
        lax.psum(d_w_up.astype(jnp.bfloat16), "seq").astype(jnp.float32),
        lax.psum(d_b_up.astype(jnp.bfloat16), "seq").astype(jnp.float32),
        lax.psum(d_w_down.astype(jnp.bfloat16), "seq").astype(jnp.float32),
        lax.psum(d_b_down.astype(jnp.bfloat16), "seq").astype(jnp.float32),
        lax.psum(d_ln2_gain.astype(jnp.bfloat16), "seq").astype(jnp.float32),
        lax.psum(d_ln2_bias.astype(jnp.bfloat16), "seq").astype(jnp.float32),
    )
    return (layer_output, d_tokens) + tuple(summed_grads)


def solution(mesh):
    placed = (
        P("seq", None),
        P(),
        P(None, None, "mp"),
        P(None, "mp"),
        P("mp", None),
        P("mp", None),
        P(),
        P(),
        P(),
        P(None, "mp"),
        P("mp"),
        P("mp", None),
        P(),
        P(),
        P(),
        P("seq", None),
    )
    return jax.shard_map(
        per_device,
        mesh=mesh,
        in_specs=placed,
        out_specs=(
            P("seq", None),
            P("seq", None),
            P(None, None, "mp"),
            P(None, "mp"),
            P("mp", None),
            P("mp", None),
            P(),
            P(),
            P(),
            P(None, "mp"),
            P("mp"),
            P("mp", None),
            P(),
            P(),
            P(),
        ),
        check_vma=False,
    )
```

profile of v0, /device:TPU:0, one launch (start us, length us, event | category | flops | bytes accessed | tf_op | source)
XLA Modules:
  0.0 956.8 jit_solution(4926142767283352020)
XLA Ops:
  8.2 2.0 fusion.101
  14.3 4.9 collective-permute-start
  26.7 52.4 %all-gather.3.cloned.1.call-done = bf16[4096,384]{0,1:T(8,128)(2,1)} async-done(((bf16[512,384]{0,1:T(8,128)(2,1)}), bf16[4096,384]{0,1:T(8,128)(2,1)}) %all-gather.3.cloned.1.call-update) | async-done | bytes 3145744 | tf_op jit(solution)/shard_map/all_gather | solution.py:153
  79.1 4.0 copy.145
  83.5 89.9 %while.26 = (s32[]{:T(128)}, f32[512,3,64]{0,2,1:T(8,128)S(1)}, bf16[4,1024,384]{1,2,0:T(8,128)(2,1)}, s32[512]{0:T(512)S(1)}, s32[4]{0:T(128)S(1)}, /*index=5*/...) while((s32[]{:T(128)}, f32[512,3,64]{0,2,1:T(8,128)S(1)}, ...), condition=%wide.region_6.7_spmd.clone, body=%wide.region_4.6_spmd.clone.sunk | while | flops 421229568 | bytes 9136299 | solution.py:68
  86.9 1.5 compare_convert_fusion.4
  89.7 16.3 %fusion.364 = f32[512,3,64]{0,2,1:T(8,128)S(1)} fusion(bf16[1024,3,64]{0,2,1:T(8,128)(2,1)S(1)} %bitcast.400, f32[512,1024]{0,1:T(8,128)} %compare_convert_fusion.4, bf16[1024,3,64]{0,2,1:T(8,128)(2,1)S(1)} %bitcast.399, bf16[512,3,64]{0,2,1:T(8,128)(2,1)S(1)} %get-tuple-element.668, f32[512,3,64]{0,2,1:T(8,128)S(1)} %get-tuple-element.654, ...), kind=kOutput, calls=%fused_computation.16.clone.1 | convolution fusion | flops 420151296 | bytes 3866625 | tf_op jit(solution)/shard_map/while/body/eval_jaxpr/hbk,khe->bhe/dot_general | solution.py:148
  109.2 1.5 compare_convert_fusion.4
  112.0 16.3 %fusion.364 = f32[512,3,64]{0,2,1:T(8,128)S(1)} fusion(bf16[1024,3,64]{0,2,1:T(8,128)(2,1)S(1)} %bitcast.400, f32[512,1024]{0,1:T(8,128)} %compare_convert_fusion.4, bf16[1024,3,64]{0,2,1:T(8,128)(2,1)S(1)} %bitcast.399, bf16[512,3,64]{0,2,1:T(8,128)(2,1)S(1)} %get-tuple-element.668, f32[512,3,64]{0,2,1:T(8,128)S(1)} %get-tuple-element.654, ...), kind=kOutput, calls=%fused_computation.16.clone.1 | convolution fusion | flops 420151296 | bytes 3866625 | tf_op jit(solution)/shard_map/while/body/eval_jaxpr/hbk,khe->bhe/dot_general | solution.py:148
  134.3 16.3 %fusion.364 = f32[512,3,64]{0,2,1:T(8,128)S(1)} fusion(bf16[1024,3,64]{0,2,1:T(8,128)(2,1)S(1)} %bitcast.400, f32[512,1024]{0,1:T(8,128)} %compare_convert_fusion.4, bf16[1024,3,64]{0,2,1:T(8,128)(2,1)S(1)} %bitcast.399, bf16[512,3,64]{0,2,1:T(8,128)(2,1)S(1)} %get-tuple-element.668, f32[512,3,64]{0,2,1:T(8,128)S(1)} %get-tuple-element.654, ...), kind=kOutput, calls=%fused_computation.16.clone.1 | convolution fusion | flops 420151296 | bytes 3866625 | tf_op jit(solution)/shard_map/while/body/eval_jaxpr/hbk,khe->bhe/dot_general | solution.py:148
  156.7 16.3 %fusion.364 = f32[512,3,64]{0,2,1:T(8,128)S(1)} fusion(bf16[1024,3,64]{0,2,1:T(8,128)(2,1)S(1)} %bitcast.400, f32[512,1024]{0,1:T(8,128)} %compare_convert_fusion.4, bf16[1024,3,64]{0,2,1:T(8,128)(2,1)S(1)} %bitcast.399, bf16[512,3,64]{0,2,1:T(8,128)(2,1)S(1)} %get-tuple-element.668, f32[512,3,64]{0,2,1:T(8,128)S(1)} %get-tuple-element.654, ...), kind=kOutput, calls=%fused_computation.16.clone.1 | convolution fusion | flops 420151296 | bytes 3866625 | tf_op jit(solution)/shard_map/while/body/eval_jaxpr/hbk,khe->bhe/dot_general | solution.py:148
  174.7 5.9 fusion.241
  181.3 1.6 fusion.303
  183.0 41.1 %all-reduce.8.cloned.1.call-done = f32[512,768]{1,0:T(8,128)} async-done(((f32[512,768]{1,0:T(8,128)}), f32[512,768]{1,0:T(8,128)}) %all-reduce.8.cloned.1.call-update) | async-done | bytes 1572880 | tf_op jit(solution)/shard_map/psum | solution.py:170
  224.1 1.9 fusion.290
  226.7 5.1 fusion.87
  232.7 1.9 fusion.304
  234.7 43.0 %all-reduce.10.cloned.1.call-done = f32[512,768]{1,0:T(8,128)} async-done(((f32[512,768]{1,0:T(8,128)}), f32[512,768]{1,0:T(8,128)}) %all-reduce.10.cloned.1.call-update) | async-done | bytes 1572880 | tf_op jit(solution)/shard_map/psum | solution.py:176
  277.7 2.0 fusion.289
  282.2 2.1 fusion.286
  284.3 1.7 fusion.299
  286.9 2.0 fusion.305
  289.0 43.0 %all-reduce.12.cloned.1.call-done = f32[512,768]{1,0:T(8,128)} async-done(((f32[512,768]{1,0:T(8,128)}), f32[512,768]{1,0:T(8,128)}) %all-reduce.12.cloned.1.call-update) | async-done | bytes 1572880 | tf_op jit(solution)/shard_map/psum | solution.py:193
  332.0 3.3 multiply_reduce_fusion
  336.4 1.9 fusion.219
  340.3 3.3 convolution_convert_fusion.1
  343.6 3.4 collective-permute-start.2
  348.3 1.8 convolution_convert_fusion
  350.2 3.8 collective-permute-done.3
  354.9 85.7 %all-gather.5.cloned.1.call-done = bf16[4096,768]{0,1:T(8,128)(2,1)} async-done(((bf16[512,768]{0,1:T(8,128)(2,1)}), bf16[4096,768]{0,1:T(8,128)(2,1)}) %all-gather.5.cloned.1.call-update) | async-done | bytes 6291472 | tf_op jit(solution)/shard_map/all_gather | solution.py:257
  440.7 6.4 copy.144
  447.1 304.2 %while.27 = (s32[]{:T(128)}, f32[512,3,64]{0,2,1:T(8,128)}, f32[512,3,64]{0,2,1:T(8,128)}, f32[512,3,64]{0,2,1:T(8,128)}, bf16[4,1024,768]{1,2,0:T(8,128)(2,1)},...) while((s32[]{:T(128)}, f32[512,3,64]{0,2,1:T(8,128)}, ...), condition=%wide.region_23.24_spmd.clone, body=%wide.region_21.23_spmd.clone.sunk | while | flops 1486976000 | bytes 64526712 | solution.py:68
  450.8 1.5 dynamic-slice_bitcast_fusion.5
  453.3 3.7 fusion.381
  457.0 21.5 %fusion.382 = f32[512,3,64]{0,2,1:T(8,128)} fusion(bf16[1024,3,64]{0,2,1:T(8,128)(2,1)S(1)} %bitcast.393, f32[3,1024,512]{2,1,0:T(8,128)} %fusion.381, f32[1024,512]{1,0:T(8,128)S(1)} %compare_select_fusion.5, bf16[1024,3,64]{0,2,1:T(8,128)(2,1)} %bitcast.397, bf16[512,3,64]{0,2,1:T(8,128)(2,1)} %get-tuple-element.709, ...), kind=kOutput, calls=%fused_computation.66.clone.1 | convolution fusion | flops 431161344 | bytes 10158081 | tf_op jit(solution)/shard_map/while/body/eval_jaxpr/hbk,bhe->khe/dot_general | solution.py:246
  479.6 15.2 %fusion.383 = f32[512,3,64]{0,2,1:T(8,128)S(1)} fusion(bf16[1024,3,64]{0,2,1:T(8,128)(2,1)S(1)} %bitcast.398, f32[3,1024,512]{2,1,0:T(8,128)} %fusion.381, f32[1024,512]{1,0:T(8,128)S(1)} %compare_convert_fusion.5, f32[512,3,64]{0,2,1:T(8,128)S(1)} %copy-done.37, pred[]{:T(512)S(6)} %compare.7), kind=kOutput, calls=%fused_computation.65.clone.1 | convolution fusion | flops 218824704 | bytes 9568257 | tf_op jit(solution)/shard_map/while/body/eval_jaxpr/hbk,bhe->khe/dot_general | solution.py:249
  495.0 3.7 fusion.379
  498.7 21.1 %fusion.380 = f32[512,3,64]{0,2,1:T(8,128)S(1)} fusion(bf16[1024,3,64]{0,2,1:T(8,128)(2,1)S(1)} %bitcast.396, f32[3,1024,512]{2,1,0:T(8,128)} %fusion.379, f32[512,1024]{0,1:T(8,128)S(1)} %compare_select_fusion.4, bf16[512,3,64]{0,2,1:T(8,128)(2,1)} %get-tuple-element.708, f32[512,3,64]{0,2,1:T(8,128)S(1)} %copy-done.40, pred[]{:T(512)S(6)} %compare.7), kind=kOutput, calls=%fused_computation.67.clone.1 | convolution fusion | flops 431161344 | bytes 9764865 | tf_op jit(solution)/shard_map/while/body/eval_jaxpr/hbk,khe->bhe/dot_general | solution.py:240
  524.9 1.5 dynamic-slice_bitcast_fusion.5
  527.4 3.7 fusion.381
  531.1 21.3 %fusion.382 = f32[512,3,64]{0,2,1:T(8,128)} fusion(bf16[1024,3,64]{0,2,1:T(8,128)(2,1)S(1)} %bitcast.393, f32[3,1024,512]{2,1,0:T(8,128)} %fusion.381, f32[1024,512]{1,0:T(8,128)S(1)} %compare_select_fusion.5, bf16[1024,3,64]{0,2,1:T(8,128)(2,1)} %bitcast.397, bf16[512,3,64]{0,2,1:T(8,128)(2,1)} %get-tuple-element.709, ...), kind=kOutput, calls=%fused_computation.66.clone.1 | convolution fusion | flops 431161344 | bytes 10158081 | tf_op jit(solution)/shard_map/while/body/eval_jaxpr/hbk,bhe->khe/dot_general | solution.py:246
  553.5 15.2 %fusion.383 = f32[512,3,64]{0,2,1:T(8,128)S(1)} fusion(bf16[1024,3,64]{0,2,1:T(8,128)(2,1)S(1)} %bitcast.398, f32[3,1024,512]{2,1,0:T(8,128)} %fusion.381, f32[1024,512]{1,0:T(8,128)S(1)} %compare_convert_fusion.5, f32[512,3,64]{0,2,1:T(8,128)S(1)} %copy-done.37, pred[]{:T(512)S(6)} %compare.7), kind=kOutput, calls=%fused_computation.65.clone.1 | convolution fusion | flops 218824704 | bytes 9568257 | tf_op jit(solution)/shard_map/while/body/eval_jaxpr/hbk,bhe->khe/dot_general | solution.py:249
  568.9 3.7 fusion.379
  572.6 21.3 %fusion.380 = f32[512,3,64]{0,2,1:T(8,128)S(1)} fusion(bf16[1024,3,64]{0,2,1:T(8,128)(2,1)S(1)} %bitcast.396, f32[3,1024,512]{2,1,0:T(8,128)} %fusion.379, f32[512,1024]{0,1:T(8,128)S(1)} %compare_select_fusion.4, bf16[512,3,64]{0,2,1:T(8,128)(2,1)} %get-tuple-element.708, f32[512,3,64]{0,2,1:T(8,128)S(1)} %copy-done.40, pred[]{:T(512)S(6)} %compare.7), kind=kOutput, calls=%fused_computation.67.clone.1 | convolution fusion | flops 431161344 | bytes 9764865 | tf_op jit(solution)/shard_map/while/body/eval_jaxpr/hbk,khe->bhe/dot_general | solution.py:240
  598.8 1.5 dynamic-slice_bitcast_fusion.5
  601.3 3.7 fusion.381
  604.9 21.5 %fusion.382 = f32[512,3,64]{0,2,1:T(8,128)} fusion(bf16[1024,3,64]{0,2,1:T(8,128)(2,1)S(1)} %bitcast.393, f32[3,1024,512]{2,1,0:T(8,128)} %fusion.381, f32[1024,512]{1,0:T(8,128)S(1)} %compare_select_fusion.5, bf16[1024,3,64]{0,2,1:T(8,128)(2,1)} %bitcast.397, bf16[512,3,64]{0,2,1:T(8,128)(2,1)} %get-tuple-element.709, ...), kind=kOutput, calls=%fused_computation.66.clone.1 | convolution fusion | flops 431161344 | bytes 10158081 | tf_op jit(solution)/shard_map/while/body/eval_jaxpr/hbk,bhe->khe/dot_general | solution.py:246
  627.6 15.2 %fusion.383 = f32[512,3,64]{0,2,1:T(8,128)S(1)} fusion(bf16[1024,3,64]{0,2,1:T(8,128)(2,1)S(1)} %bitcast.398, f32[3,1024,512]{2,1,0:T(8,128)} %fusion.381, f32[1024,512]{1,0:T(8,128)S(1)} %compare_convert_fusion.5, f32[512,3,64]{0,2,1:T(8,128)S(1)} %copy-done.37, pred[]{:T(512)S(6)} %compare.7), kind=kOutput, calls=%fused_computation.65.clone.1 | convolution fusion | flops 218824704 | bytes 9568257 | tf_op jit(solution)/shard_map/while/body/eval_jaxpr/hbk,bhe->khe/dot_general | solution.py:249
  643.0 3.7 fusion.379
  646.7 21.1 %fusion.380 = f32[512,3,64]{0,2,1:T(8,128)S(1)} fusion(bf16[1024,3,64]{0,2,1:T(8,128)(2,1)S(1)} %bitcast.396, f32[3,1024,512]{2,1,0:T(8,128)} %fusion.379, f32[512,1024]{0,1:T(8,128)S(1)} %compare_select_fusion.4, bf16[512,3,64]{0,2,1:T(8,128)(2,1)} %get-tuple-element.708, f32[512,3,64]{0,2,1:T(8,128)S(1)} %copy-done.40, pred[]{:T(512)S(6)} %compare.7), kind=kOutput, calls=%fused_computation.67.clone.1 | convolution fusion | flops 431161344 | bytes 9764865 | tf_op jit(solution)/shard_map/while/body/eval_jaxpr/hbk,khe->bhe/dot_general | solution.py:240
  672.9 1.5 dynamic-slice_bitcast_fusion.5
  675.4 3.7 fusion.381
  679.1 21.3 %fusion.382 = f32[512,3,64]{0,2,1:T(8,128)} fusion(bf16[1024,3,64]{0,2,1:T(8,128)(2,1)S(1)} %bitcast.393, f32[3,1024,512]{2,1,0:T(8,128)} %fusion.381, f32[1024,512]{1,0:T(8,128)S(1)} %compare_select_fusion.5, bf16[1024,3,64]{0,2,1:T(8,128)(2,1)} %bitcast.397, bf16[512,3,64]{0,2,1:T(8,128)(2,1)} %get-tuple-element.709, ...), kind=kOutput, calls=%fused_computation.66.clone.1 | convolution fusion | flops 431161344 | bytes 10158081 | tf_op jit(solution)/shard_map/while/body/eval_jaxpr/hbk,bhe->khe/dot_general | solution.py:246
  701.5 15.2 %fusion.383 = f32[512,3,64]{0,2,1:T(8,128)S(1)} fusion(bf16[1024,3,64]{0,2,1:T(8,128)(2,1)S(1)} %bitcast.398, f32[3,1024,512]{2,1,0:T(8,128)} %fusion.381, f32[1024,512]{1,0:T(8,128)S(1)} %compare_convert_fusion.5, f32[512,3,64]{0,2,1:T(8,128)S(1)} %copy-done.37, pred[]{:T(512)S(6)} %compare.7), kind=kOutput, calls=%fused_computation.65.clone.1 | convolution fusion | flops 218824704 | bytes 9568257 | tf_op jit(solution)/shard_map/while/body/eval_jaxpr/hbk,bhe->khe/dot_general | solution.py:249
  716.9 3.7 fusion.379
  720.6 21.3 %fusion.380 = f32[512,3,64]{0,2,1:T(8,128)S(1)} fusion(bf16[1024,3,64]{0,2,1:T(8,128)(2,1)S(1)} %bitcast.396, f32[3,1024,512]{2,1,0:T(8,128)} %fusion.379, f32[512,1024]{0,1:T(8,128)S(1)} %compare_select_fusion.4, bf16[512,3,64]{0,2,1:T(8,128)(2,1)} %get-tuple-element.708, f32[512,3,64]{0,2,1:T(8,128)S(1)} %copy-done.40, pred[]{:T(512)S(6)} %compare.7), kind=kOutput, calls=%fused_computation.67.clone.1 | convolution fusion | flops 431161344 | bytes 9764865 | tf_op jit(solution)/shard_map/while/body/eval_jaxpr/hbk,khe->bhe/dot_general | solution.py:240
  755.1 6.0 fusion.242
  761.2 3.0 bitcast_convert_fusion
  765.3 1.5 fusion.103
  783.4 34.6 %all-reduce = (bf16[2,192]{1,0:T(2,128)(2,1)S(1)}, bf16[3,33]{1,0:T(4,128)(2,1)S(1)}, bf16[768]{0:T(1024)(128)(2,1)S(1)}, bf16[768]{0:T(1024)(128)(2,1)S(1)}, bf...) all-reduce(bf16[2,192]{1,0:T(2,128)(2,1)S(1)} %pad_maximum_fusion.4, ...), channel_id=1, replica_groups=mesh['seq'=8,'mp'=4] {'seq'}, use_global_device_ids=true, to_apply=%region_29.30 | all-reduce | flops 5859 | bytes 23436 | tf_op jit(solution)/shard_map/psum | solution.py:283
  823.3 2.2 add_convert_fusion
  825.5 117.4 %all-reduce.16.cloned.1.call-done = (bf16[3,768,192]{1,2,0:T(8,128)(2,1)}, bf16[192,768]{1,0:T(8,128)(2,1)}, bf16[768,768]{1,0:T(8,128)(2,1)}, bf16[768,768]{1,0:T(8,128)(2,1)}) async-done(((bf16[3,768,192]{1,2,0:T(8,128)(2,1)}, bf16[192,768]{1,0:T(8,128)(2,1)}, bf16[768,768]{1,0:T(8,128)(2,1)}, bf16[768,768]{1,0:T(8,128)(2,1)}), (bf16[3,768,192]{1,2,0:T(8,128)(2,1)}, bf16[192,768]{1,0:T(8,128)(2,1)}, ...) | async-done | bytes 3538960 | tf_op jit(solution)/shard_map/psum | solution.py:282
  942.9 2.9 convert_element_type.398
  945.9 1.6 convert_element_type.401
  (689 shorter events, 98.8 us)
Async XLA Ops:
  7.2 219.2 %copy-start = (bf16[768,768]{1,0:T(8,128)(2,1)S(1)}, bf16[768,768]{1,0:T(8,128)(2,1)}, u32[]{:S(2)}) copy-start(bf16[768,768]{1,0:T(8,128)(2,1)} %param.29) | copy-start | bytes 3538948
  7.2 71.9 %all-gather.3.cloned.1.call-start = ((), (), s32[]{:S(2)}) async-start(), calls=%async_computation | async-start | bytes 3538944 | tf_op jit(solution)/shard_map/all_gather | solution.py:153
  11.2 328.3 %copy-start.46 = (f32[512,3]{0,1:T(4,128)}, f32[512,3]{0,1:T(4,128)S(1)}, u32[]{:S(2)}) copy-start(f32[512,3]{0,1:T(4,128)S(1)} %get-tuple-element.515) | copy-start | bytes 18436
  13.4 210.7 %all-reduce.8.cloned.1.call-start = ((), (), s32[]{:S(2)}) async-start(), calls=%async_computation.1 | async-start | bytes 3145728 | tf_op jit(solution)/shard_map/psum | solution.py:170
  14.3 12.2 %collective-permute-start = (bf16[16,192]{0,1:T(8,128)(2,1)S(1)}, bf16[16,192]{0,1:T(8,128)(2,1)S(1)}, u32[]{:S(2)}, u32[]{:S(2)}) collective-permute-start(bf16[16,192]{0,1:T(8,128)(2,1)S(1)} %get-tuple-element.438), channel_id=1, source_target_pairs={{0,4},{4,8},{8,12},{12,16},{16,20},{20,24},{24,28},{1,5},{5,9},{9,... | collective-permute-start | bytes 18440 | tf_op jit(solution)/shard_map/ppermute | solution.py:21
  19.2 7.4 collective-permute-start.1
  25.6 148.5 %copy-start.77 = (f32[512]{0:T(512)}, f32[512]{0:T(512)S(1)}, u32[]{:S(2)}) copy-start(f32[512]{0:T(512)S(1)} %get-tuple-element.492) | copy-start | bytes 6148
  25.6 148.5 %copy-start.80 = (f32[512]{0:T(512)}, f32[512]{0:T(512)S(1)}, u32[]{:S(2)}) copy-start(f32[512]{0:T(512)S(1)} %get-tuple-element.493) | copy-start | bytes 6148
  25.6 148.6 %copy-start.83 = (f32[512]{0:T(512)}, f32[512]{0:T(512)S(1)}, u32[]{:S(2)}) copy-start(f32[512]{0:T(512)S(1)} %get-tuple-element.494) | copy-start | bytes 6148
  25.6 148.6 %copy-start.86 = (f32[512]{0:T(512)}, f32[512]{0:T(512)S(1)}, u32[]{:S(2)}) copy-start(f32[512]{0:T(512)S(1)} %get-tuple-element.495) | copy-start | bytes 6148
  25.6 148.6 %copy-start.89 = (f32[512]{0:T(512)}, f32[512]{0:T(512)S(1)}, u32[]{:S(2)}) copy-start(f32[512]{0:T(512)S(1)} %get-tuple-element.496) | copy-start | bytes 6148
  25.6 148.6 %copy-start.92 = (f32[512]{0:T(512)}, f32[512]{0:T(512)S(1)}, u32[]{:S(2)}) copy-start(f32[512]{0:T(512)S(1)} %get-tuple-element.497) | copy-start | bytes 6148
  25.6 148.6 %copy-start.95 = (f32[512]{0:T(512)}, f32[512]{0:T(512)S(1)}, u32[]{:S(2)}) copy-start(f32[512]{0:T(512)S(1)} %get-tuple-element.498) | copy-start | bytes 6148
  25.6 148.6 %copy-start.98 = (f32[512]{0:T(512)}, f32[512]{0:T(512)S(1)}, u32[]{:S(2)}) copy-start(f32[512]{0:T(512)S(1)} %get-tuple-element.499) | copy-start | bytes 6148
  26.3 147.9 %copy-start.51 = (f32[512]{0:T(512)}, f32[512]{0:T(512)S(1)}, u32[]{:S(2)}) copy-start(f32[512]{0:T(512)S(1)} %get-tuple-element.475) | copy-start | bytes 6148
  26.3 147.9 %copy-start.53 = (f32[512]{0:T(512)}, f32[512]{0:T(512)S(1)}, u32[]{:S(2)}) copy-start(f32[512]{0:T(512)S(1)} %get-tuple-element.476) | copy-start | bytes 6148
  26.4 147.9 %copy-start.55 = (f32[512]{0:T(512)}, f32[512]{0:T(512)S(1)}, u32[]{:S(2)}) copy-start(f32[512]{0:T(512)S(1)} %get-tuple-element.483) | copy-start | bytes 6148
  26.4 147.9 %copy-start.57 = (f32[512]{0:T(512)}, f32[512]{0:T(512)S(1)}, u32[]{:S(2)}) copy-start(f32[512]{0:T(512)S(1)} %get-tuple-element.484) | copy-start | bytes 6148
  26.4 147.9 %copy-start.59 = (f32[512]{0:T(512)}, f32[512]{0:T(512)S(1)}, u32[]{:S(2)}) copy-start(f32[512]{0:T(512)S(1)} %get-tuple-element.485) | copy-start | bytes 6148
  26.4 147.9 %copy-start.62 = (f32[512]{0:T(512)}, f32[512]{0:T(512)S(1)}, u32[]{:S(2)}) copy-start(f32[512]{0:T(512)S(1)} %get-tuple-element.486) | copy-start | bytes 6148
  26.4 147.9 %copy-start.65 = (f32[512]{0:T(512)}, f32[512]{0:T(512)S(1)}, u32[]{:S(2)}) copy-start(f32[512]{0:T(512)S(1)} %get-tuple-element.487) | copy-start | bytes 6148
  26.4 147.9 %copy-start.68 = (f32[512]{0:T(512)}, f32[512]{0:T(512)S(1)}, u32[]{:S(2)}) copy-start(f32[512]{0:T(512)S(1)} %get-tuple-element.488) | copy-start | bytes 6148
  26.4 147.9 %copy-start.71 = (f32[512]{0:T(512)}, f32[512]{0:T(512)S(1)}, u32[]{:S(2)}) copy-start(f32[512]{0:T(512)S(1)} %get-tuple-element.489) | copy-start | bytes 6148
  26.4 147.9 %copy-start.74 = (f32[512]{0:T(512)}, f32[512]{0:T(512)S(1)}, u32[]{:S(2)}) copy-start(f32[512]{0:T(512)S(1)} %get-tuple-element.490) | copy-start | bytes 6148
  26.4 147.9 %copy-start.101 = (f32[512]{0:T(512)}, f32[512]{0:T(512)S(1)}, u32[]{:S(2)}) copy-start(f32[512]{0:T(512)S(1)} %get-tuple-element.477) | copy-start | bytes 6148
  26.4 147.9 %copy-start.104 = (f32[512]{0:T(512)}, f32[512]{0:T(512)S(1)}, u32[]{:S(2)}) copy-start(f32[512]{0:T(512)S(1)} %get-tuple-element.478) | copy-start | bytes 6148
  26.5 147.9 %copy-start.107 = (f32[512]{0:T(512)}, f32[512]{0:T(512)S(1)}, u32[]{:S(2)}) copy-start(f32[512]{0:T(512)S(1)} %get-tuple-element.479) | copy-start | bytes 6148
  26.5 147.9 %copy-start.110 = (f32[512]{0:T(512)}, f32[512]{0:T(512)S(1)}, u32[]{:S(2)}) copy-start(f32[512]{0:T(512)S(1)} %get-tuple-element.480) | copy-start | bytes 6148
  26.7 309.6 %copy-start.2 = (f32[544,192]{0,1:T(8,128)}, f32[544,192]{0,1:T(8,128)S(1)}, u32[]{:S(2)}) copy-start(f32[544,192]{0,1:T(8,128)S(1)} %maximum_convert_fusion) | copy-start | bytes 1253380
  83.1 91.3 %copy-start.121 = (f32[512]{0:T(512)S(1)}, f32[512]{0:T(512)}, u32[]{:S(2)}) copy-start(f32[512]{0:T(512)} %get-tuple-element.474) | copy-start | bytes 6148
  83.1 91.3 %copy-start.123 = (f32[512]{0:T(512)S(1)}, f32[512]{0:T(512)}, u32[]{:S(2)}) copy-start(f32[512]{0:T(512)} %get-tuple-element.423) | copy-start | bytes 6148
  83.1 91.3 %copy-start.125 = (f32[512]{0:T(512)S(1)}, f32[512]{0:T(512)}, u32[]{:S(2)}) copy-start(f32[512]{0:T(512)} %get-tuple-element.491) | copy-start | bytes 6148
  83.2 91.3 %copy-start.127 = (f32[512]{0:T(512)S(1)}, f32[512]{0:T(512)}, u32[]{:S(2)}) copy-start(f32[512]{0:T(512)} %get-tuple-element.500) | copy-start | bytes 6148
  83.2 91.3 %copy-start.129 = (f32[512]{0:T(512)S(1)}, f32[512]{0:T(512)}, u32[]{:S(2)}) copy-start(f32[512]{0:T(512)} %get-tuple-element.501) | copy-start | bytes 6148
  83.2 91.3 %copy-start.131 = (f32[512]{0:T(512)S(1)}, f32[512]{0:T(512)}, u32[]{:S(2)}) copy-start(f32[512]{0:T(512)} %get-tuple-element.502) | copy-start | bytes 6148
  83.2 91.3 %copy-start.133 = (f32[512]{0:T(512)S(1)}, f32[512]{0:T(512)}, u32[]{:S(2)}) copy-start(f32[512]{0:T(512)} %get-tuple-element.503) | copy-start | bytes 6148
  83.2 91.3 %copy-start.135 = (f32[512]{0:T(512)S(1)}, f32[512]{0:T(512)}, u32[]{:S(2)}) copy-start(f32[512]{0:T(512)} %get-tuple-element.504) | copy-start | bytes 6148
  83.2 91.3 %copy-start.138 = (f32[1,192]{1,0:T(1,128)S(1)}, f32[1,192]{1,0:T(1,128)}, u32[]{:S(2)}) copy-start(f32[1,192]{1,0:T(1,128)} %get-tuple-element.459) | copy-start | bytes 2308
  83.2 91.3 %copy-start.140 = (f32[1,192]{1,0:T(1,128)S(1)}, f32[1,192]{1,0:T(1,128)}, u32[]{:S(2)}) copy-start(f32[1,192]{1,0:T(1,128)} %get-tuple-element.460) | copy-start | bytes 2308
  83.2 91.3 %copy-start.142 = (f32[1,192]{1,0:T(1,128)S(1)}, f32[1,192]{1,0:T(1,128)}, u32[]{:S(2)}) copy-start(f32[1,192]{1,0:T(1,128)} %get-tuple-element.461) | copy-start | bytes 2308
  83.2 91.3 %copy-start.144 = (f32[1,192]{1,0:T(1,128)S(1)}, f32[1,192]{1,0:T(1,128)}, u32[]{:S(2)}) copy-start(f32[1,192]{1,0:T(1,128)} %get-tuple-element.462) | copy-start | bytes 2308
  83.2 91.3 %copy-start.145 = (f32[1,192]{1,0:T(1,128)S(1)}, f32[1,192]{1,0:T(1,128)}, u32[]{:S(2)}) copy-start(f32[1,192]{1,0:T(1,128)} %get-tuple-element.463) | copy-start | bytes 2308
  83.3 91.3 %copy-start.146 = (f32[1,192]{1,0:T(1,128)S(1)}, f32[1,192]{1,0:T(1,128)}, u32[]{:S(2)}) copy-start(f32[1,192]{1,0:T(1,128)} %get-tuple-element.464) | copy-start | bytes 2308
  83.3 91.3 %copy-start.147 = (f32[1,192]{1,0:T(1,128)S(1)}, f32[1,192]{1,0:T(1,128)}, u32[]{:S(2)}) copy-start(f32[1,192]{1,0:T(1,128)} %get-tuple-element.465) | copy-start | bytes 2308
  83.3 91.3 %copy-start.148 = (f32[1,192]{1,0:T(1,128)S(1)}, f32[1,192]{1,0:T(1,128)}, u32[]{:S(2)}) copy-start(f32[1,192]{1,0:T(1,128)} %get-tuple-element.466) | copy-start | bytes 2308
  83.3 91.3 %copy-start.149 = (f32[1,192]{1,0:T(1,128)S(1)}, f32[1,192]{1,0:T(1,128)}, u32[]{:S(2)}) copy-start(f32[1,192]{1,0:T(1,128)} %get-tuple-element.467) | copy-start | bytes 2308
  83.3 91.3 %copy-start.150 = (f32[1,192]{1,0:T(1,128)S(1)}, f32[1,192]{1,0:T(1,128)}, u32[]{:S(2)}) copy-start(f32[1,192]{1,0:T(1,128)} %get-tuple-element.468) | copy-start | bytes 2308
  83.3 91.3 %copy-start.151 = (f32[1,192]{1,0:T(1,128)S(1)}, f32[1,192]{1,0:T(1,128)}, u32[]{:S(2)}) copy-start(f32[1,192]{1,0:T(1,128)} %get-tuple-element.469) | copy-start | bytes 2308
  83.3 91.3 %copy-start.152 = (f32[1,192]{1,0:T(1,128)S(1)}, f32[1,192]{1,0:T(1,128)}, u32[]{:S(2)}) copy-start(f32[1,192]{1,0:T(1,128)} %get-tuple-element.470) | copy-start | bytes 2308
  83.3 91.3 %copy-start.153 = (f32[1,192]{1,0:T(1,128)S(1)}, f32[1,192]{1,0:T(1,128)}, u32[]{:S(2)}) copy-start(f32[1,192]{1,0:T(1,128)} %get-tuple-element.471) | copy-start | bytes 2308
  83.3 91.3 %copy-start.154 = (f32[1,192]{1,0:T(1,128)S(1)}, f32[1,192]{1,0:T(1,128)}, u32[]{:S(2)}) copy-start(f32[1,192]{1,0:T(1,128)} %get-tuple-element.472) | copy-start | bytes 2308
  83.3 91.3 %copy-start.155 = (f32[1,192]{1,0:T(1,128)S(1)}, f32[1,192]{1,0:T(1,128)}, u32[]{:S(2)}) copy-start(f32[1,192]{1,0:T(1,128)} %get-tuple-element.440) | copy-start | bytes 2308
  83.4 91.3 %copy-start.156 = (f32[1,192]{1,0:T(1,128)S(1)}, f32[1,192]{1,0:T(1,128)}, u32[]{:S(2)}) copy-start(f32[1,192]{1,0:T(1,128)} %get-tuple-element.441) | copy-start | bytes 2308
  83.4 91.3 %copy-start.157 = (f32[1,192]{1,0:T(1,128)S(1)}, f32[1,192]{1,0:T(1,128)}, u32[]{:S(2)}) copy-start(f32[1,192]{1,0:T(1,128)} %get-tuple-element.442) | copy-start | bytes 2308
  83.4 91.3 %copy-start.158 = (f32[1,192]{1,0:T(1,128)S(1)}, f32[1,192]{1,0:T(1,128)}, u32[]{:S(2)}) copy-start(f32[1,192]{1,0:T(1,128)} %get-tuple-element.443) | copy-start | bytes 2308
  182.9 94.8 %all-reduce.10.cloned.1.call-start = ((), (), s32[]{:S(2)}) async-start(), calls=%async_computation.2 | async-start | bytes 3145728 | tf_op jit(solution)/shard_map/psum | solution.py:176
  234.7 97.3 %all-reduce.12.cloned.1.call-start = ((), (), s32[]{:S(2)}) async-start(), calls=%async_computation.3 | async-start | bytes 3145728 | tf_op jit(solution)/shard_map/psum | solution.py:193
  288.9 151.7 %all-gather.5.cloned.1.call-start = ((), (), s32[]{:S(2)}) async-start(), calls=%async_computation.4 | async-start | bytes 7077888 | tf_op jit(solution)/shard_map/all_gather | solution.py:257
  339.4 483.9 %all-reduce.14.cloned.1.call-start = ((), (), s32[]{:S(2)}) async-start(), calls=%async_computation.5 | async-start | bytes 1572864 | tf_op jit(solution)/shard_map/psum | solution.py:279
  343.6 6.5 collective-permute-start.2
  347.0 7.0 collective-permute-start.3
  447.1 304.6 %copy-start.49 = (f32[512,3]{0,1:T(4,128)S(1)}, f32[512,3]{0,1:T(4,128)}, u32[]{:S(2)}) copy-start(f32[512,3]{0,1:T(4,128)} %copy-done.48) | copy-start | bytes 18436
  447.1 306.1 %copy-start.47 = (f32[512,3]{0,1:T(4,128)S(1)}, f32[512,3]{0,1:T(4,128)}, u32[]{:S(2)}) copy-start(f32[512,3]{0,1:T(4,128)} %copy-done.46) | copy-start | bytes 18436
  764.2 178.7 %all-reduce.16.cloned.1.call-start = ((), (), s32[]{:S(2)}) async-start(), calls=%async_computation.6 | async-start | bytes 7077888 | tf_op jit(solution)/shard_map/psum | solution.py:282
  (161 other events, 1739.2 us)
Sparse Core Ops, SparseCore 0:
  13.6 65.5 all-gather.2
  183.0 41.0 all-reduce.7
  234.8 42.8 all-reduce.9
  289.0 42.9 all-reduce.11
  339.6 101.0 all-gather.4
  764.3 32.8 all-reduce.13
  802.3 140.5 all-reduce.15
where the time goes:
time: 961 us; the launch traced here: 957 us
  waiting for transfers between devices  387 us (40%)
  matrix products  353 us (37%)
  other arithmetic  82.8 us (9%)
  local copies, waits for them, and re-layouts  59.3 us (6%)
  blocking collectives  34.6 us (4%)
  between operations  17.1 us (2%)
  loops' own time  12.2 us (1%)
  starting transfers between devices  11.1 us (1%)
    psum x1, waiting for transfers between devices, per_device(): lax.psum(d_w_qkv.astype(jnp.bfloat16), 'seq').astype(jnp.float32)  117 us
    all_gather x1, waiting for transfers between devices, per_device(): lax.all_gather(both_packed, 'seq', axis=0, tiled=True)  85.7 us
    dot_general x4, matrix products, pair_block(): jnp.einsum('hbk,bhe->khe', d_scores_own, queries_block, preferred_element...  85.6 us
    dot_general x4, matrix products, pair_block(): jnp.einsum('hbk,khe->bhe', d_scores, keys_block, preferred_element_type=j...  84.9 us
    dot_general x4, matrix products, attend(): jnp.einsum('hbk,khe->bhe', weights, values_heads, preferred_element_type=...  65.3 us
    dot_general x4, matrix products, pair_block(): jnp.einsum('hbk,bhe->khe', weights_own, d_attn_block, preferred_element_t...  60.7 us
    all_gather x1, waiting for transfers between devices, per_device(): lax.all_gather(packed, 'seq', axis=0, tiled=True)  52.4 us
    psum x1, waiting for transfers between devices, per_device(): d_first_out = d_second + lax.psum(d_first_part, 'mp')  43 us
  transfers between devices with their start and end apart: 11, of which 7 were waited for; matrix products, arithmetic and copies ran while one was open for 4% of the time, Pallas kernels for 0%

commit v1 on v0

v1 whole, which is shorter than its diff:
```python
import functools
import math

import jax
import jax.numpy as jnp
from jax import lax
from jax.experimental import pallas as pl
from jax.experimental.pallas import tpu as pltpu
from jax.sharding import PartitionSpec as P

SHRINK = 0.95
NORM_EPS = 1e-06
LAYER_EPS = 1e-05
F32 = jnp.float32
BF16 = jnp.bfloat16
ROWS = 128
KEYS = 256
BAND = 384
VMEM_BYTES = 56 * 1024 * 1024
SQUARE = (
    0.9999936361319989,
    -1.2731008162270503,
    0.4040306859655804,
    -0.20598641392473288,
    0.11615118744625774,
    -0.05772567810293111,
    0.02001158958170149,
    -0.00337422878652264,
)
SLOPE = 4.0 * SHRINK / math.pi


def dot(left, right, left_dim=1, right_dim=0):
    return lax.dot_general(
        left, right, (((left_dim,), (right_dim,)), ((), ())), preferred_element_type=F32
    )


def flips(axis):
    size = lax.axis_size(axis)
    mask = size // 2
    while mask:
        yield [(i, i ^ mask) for i in range(size)]
        mask //= 2


def gathered(cells, axis):
    cells = cells[None]
    for pairs in flips(axis):
        cells = jnp.concatenate([cells, lax.ppermute(cells, axis, pairs)], axis=0)
    return cells


def block_places(axis):
    size = lax.axis_size(axis)
    apart = jnp.arange(size, dtype=jnp.int32) ^ lax.axis_index(axis).astype(jnp.int32)
    place = jnp.zeros_like(apart)
    mask, bit = size // 2, 0
    while mask:
        place = place | (jnp.where((apart & mask) != 0, 1, 0) << bit)
        mask, bit = mask // 2, bit + 1
    return place


def all_sum(cells, axis):
    size = lax.axis_size(axis)
    index = lax.axis_index(axis)
    masks = [1 << bit for bit in range(size.bit_length() - 1)]
    pairs_of = lambda mask: [(i, i ^ mask) for i in range(size)]
    for mask in masks[:-1]:
        half = cells.shape[0] // 2
        upper = (index & mask) != 0
        sent = lax.dynamic_slice_in_dim(cells, jnp.where(upper, 0, half), half)
        kept = lax.dynamic_slice_in_dim(cells, jnp.where(upper, half, 0), half)
        got = lax.ppermute(sent, axis, pairs_of(mask))
        cells = (kept.astype(F32) + got.astype(F32)).astype(BF16)
    got = lax.ppermute(cells, axis, pairs_of(masks[-1]))
    cells = (cells.astype(F32) + got.astype(F32)).astype(BF16)
    for mask in masks[-2::-1]:
        upper = (index & mask) != 0
        got = lax.ppermute(cells, axis, pairs_of(mask))
        cells = jnp.concatenate([jnp.where(upper, got, cells), jnp.where(upper, cells, got)], axis=0)
    return cells


def item_index(positions, ends):
    inside = (positions >= 0) & (positions < ends[-1])
    counted = jnp.sum((positions[:, None] >= ends[None, :]).astype(jnp.int32), axis=1)
    return jnp.where(inside, counted, -1)


def layer_norm(hidden, gain, shift):
    center = hidden - jnp.mean(hidden, axis=-1, keepdims=True)
    scale = lax.rsqrt(jnp.mean(center * center, axis=-1, keepdims=True) + LAYER_EPS)
    normed = center * scale
    return (normed * gain + shift, normed, scale)


def layer_norm_back(grad, normed, scale, gain):
    d_gain = jnp.sum(grad * normed, axis=0)
    d_shift = jnp.sum(grad, axis=0)
    d_normed = grad * gain
    centered = d_normed - jnp.mean(d_normed, axis=-1, keepdims=True)
    d_hidden = scale * (centered - normed * jnp.mean(d_normed * normed, axis=-1, keepdims=True))
    return (d_hidden, d_gain, d_shift)


def call(kernel, out_shape, *args, grid=(), in_specs=None, out_specs=None, scalars=0, flops=0, scratch=()):
    whole = lambda a: pl.BlockSpec(a.shape, lambda *_, n=len(a.shape): (0,) * n)
    ins = [whole(a) if s is None else s for a, s in zip(args[scalars:], in_specs or [None] * 99)]
    outs = [whole(a) if s is None else s for a, s in zip(out_shape, out_specs or [None] * 99)]
    moved = sum(a.size * a.dtype.itemsize for a in (*args, *out_shape))
    return pl.pallas_call(
        kernel,
        out_shape=out_shape,
        grid_spec=pltpu.PrefetchScalarGridSpec(
            num_scalar_prefetch=scalars,
            grid=grid,
            in_specs=ins,
            out_specs=outs,
            scratch_shapes=list(scratch),
        ),
        compiler_params=pltpu.CompilerParams(vmem_limit_bytes=VMEM_BYTES),
        cost_estimate=pl.CostEstimate(flops=flops, bytes_accessed=moved, transcendentals=0),
    )(*args)


def project_kernel(heads, unit, tokens_ref, w_ref, bias_ref, raw_ref, own_ref, turned_ref):
    product = dot(tokens_ref[...], w_ref[...], 1, 1) + bias_ref[...]
    size = product.shape[1] // heads
    rounded = []
    for head in range(heads):
        raw = product[:, head * size : (head + 1) * size]
        if unit:
            raw_ref[head] = raw
            raw = raw * lax.rsqrt(jnp.sum(raw * raw, axis=-1, keepdims=True) + NORM_EPS)
        own_ref[head] = raw.astype(BF16)
        rounded.append(raw)
    turned_ref[...] = jnp.concatenate(rounded, axis=1).T.astype(BF16)


def project(tokens, w, bias, heads, unit):
    rows, columns = tokens.shape[0], w.shape[0]
    size = columns // heads
    shapes = [
        jax.ShapeDtypeStruct((heads, rows, size), F32 if unit else BF16),
        jax.ShapeDtypeStruct((heads, rows, size), BF16),
        jax.ShapeDtypeStruct((columns, rows), BF16),
    ]
    if unit:
        kernel = functools.partial(project_kernel, heads, True)
    else:
        kernel = lambda t, w_, b, own, turned: project_kernel(heads, False, t, w_, b, None, own, turned)
        shapes = shapes[1:]
    return call(kernel, shapes, tokens, w, bias.reshape(1, columns), flops=2 * rows * w.size)


def item_range(lengths_ref, first, last):
    end = jnp.int32(0)
    low = jnp.int32(0)
    high = jnp.int32(0)
    found = jnp.int32(0)
    for item in range(lengths_ref.shape[0]):
        end = end + lengths_ref[item]
        low = jnp.where(end <= first, end, low)
        past = (end > last).astype(jnp.int32)
        high = jnp.where((past == 1) & (found == 0), end, high)
        found = found | past
    return low, high


def square_of(scores):
    half = 0.5 - (0.5 * SHRINK) * scores
    inverse = lax.rsqrt(half)
    root = half * inverse
    square = jnp.full_like(root, SQUARE[-1])
    for factor in SQUARE[-2::-1]:
        square = square * root + factor
    return square, inverse


def slope_of(scores, square, inverse):
    other = lax.rsqrt(0.5 + (0.5 * SHRINK) * scores)
    cube = square * square * square
    return cube * (square * lax.rsqrt(square)) * (inverse * (other * SLOPE))


def band_of(taps_row, flip):
    wide = jnp.broadcast_to(taps_row, (ROWS, BAND))
    return pltpu.roll(wide, 0, 1, stride=1, stride_axis=0)


def split_low(wide):
    high = wide.astype(BF16)
    return high, (wide - high.astype(F32)).astype(BF16)


def near(turned_ref, head_rows, place_ref, tile, width, tiles):
    parts = []
    per = width // ROWS
    for at in (tile - 1, tile, tile + 1):
        at = jnp.clip(at, 0, tiles - 1)
        start = pl.multiple_of((at % per) * ROWS, ROWS)
        parts.append(turned_ref[place_ref[at // per], head_rows, pl.ds(start, ROWS)])
    return jnp.concatenate(parts, axis=1)


def forward_kernel(
    lengths_ref, place_ref, index_ref, mine_ref, items_ref, edge_ref, taps_ref, q_ref, k_ref, v_ref,
    context_ref, raw_ref,
):
    heads, rows, size = q_ref.shape
    blocks, _, width = k_ref.shape
    tile = index_ref[0] * (width // ROWS) + pl.program_id(0)
    first = tile * ROWS
    low, high = item_range(lengths_ref, first, first + rows - 1)
    per = width // KEYS
    mine = mine_ref[...]

    def step(at, sums):
        place = place_ref[at // per]
        start = pl.multiple_of((at % per) * KEYS, KEYS)
        same = mine == items_ref[at // per, :, pl.ds(start, KEYS)]
        out = []
        for head in range(heads):
            group = slice(head * size, (head + 1) * size)
            scores = dot(q_ref[head], k_ref[place, group, pl.ds(start, KEYS)])
            square, _ = square_of(scores)
            fourth = square * square
            weights = jnp.where(same, fourth * fourth, 0.0).astype(BF16)
            out.append(sums[head] + dot(weights, v_ref[place, group, pl.ds(start, KEYS)], 1, 1))
        return tuple(out)

    zero = tuple(jnp.zeros((rows, size), F32) for _ in range(heads))
    sums = lax.fori_loop(low // KEYS, (high + KEYS - 1) // KEYS, step, zero)
    around = mine == edge_ref[pl.ds(pl.program_id(0), 1), :]
    context = []
    for head in range(heads):
        group = slice(head * size, (head + 1) * size)
        raw = sums[head]
        raw_ref[head] = raw
        unit = raw * lax.rsqrt(jnp.sum(raw * raw, axis=-1, keepdims=True) + NORM_EPS)
        values = near(v_ref, group, place_ref, tile, width, blocks * (width // ROWS))
        band = jnp.where(around, band_of(taps_ref[head : head + 1, :], False), 0.0)
        band_high, band_low = split_low(band)
        context.append(unit + (dot(band_high, values, 1, 1) + dot(band_low, values, 1, 1)))
    context_ref[...] = jnp.concatenate(context, axis=1).astype(BF16)


def query_back_kernel(
    lengths_ref, place_ref, index_ref, mine_ref, items_ref, q_ref, da_ref, q_raw_ref, k_ref, v_ref, dq_ref
):
    heads, rows, size = q_ref.shape
    blocks, _, width = k_ref.shape
    first = index_ref[0] * width + pl.program_id(0) * rows
    low, high = item_range(lengths_ref, first, first + rows - 1)
    per = width // KEYS
    mine = mine_ref[...]

    def step(at, sums):
        place = place_ref[at // per]
        start = pl.multiple_of((at % per) * KEYS, KEYS)
        same = mine == items_ref[at // per, :, pl.ds(start, KEYS)]
        out = []
        for head in range(heads):
            group = slice(head * size, (head + 1) * size)
            keys = k_ref[place, group, pl.ds(start, KEYS)]
            scores = dot(q_ref[head], keys)
            d_weights = dot(da_ref[head], v_ref[place, group, pl.ds(start, KEYS)])
            square, inverse = square_of(scores)
            d_scores = jnp.where(same, d_weights * slope_of(scores, square, inverse), 0.0).astype(BF16)
            out.append(sums[head] + dot(d_scores, keys, 1, 1))
        return tuple(out)

    zero = tuple(jnp.zeros((rows, size), F32) for _ in range(heads))
    sums = lax.fori_loop(low // KEYS, (high + KEYS - 1) // KEYS, step, zero)
    dq_ref[...] = jnp.concatenate(
        [unit_back(sums[head], q_raw_ref[head]) for head in range(heads)], axis=1
    ).astype(BF16)


def unit_back(grad, raw):
    scale = lax.rsqrt(jnp.sum(raw * raw, axis=-1, keepdims=True) + NORM_EPS)
    unit = raw * scale
    return scale * (grad - unit * jnp.sum(unit * grad, axis=-1, keepdims=True))


def key_back_kernel(
    lengths_ref, place_ref, index_ref, mine_ref, items_ref, k_ref, v_ref, k_raw_ref, dv_conv_ref, q_ref, da_ref,
    dk_ref, dv_ref,
):
    heads, rows, size = k_ref.shape
    blocks, _, width = q_ref.shape
    first = index_ref[0] * width + pl.program_id(0) * rows
    low, high = item_range(lengths_ref, first, first + rows - 1)
    per = width // KEYS
    mine = mine_ref[...]

    def step(at, sums):
        place = place_ref[at // per]
        start = pl.multiple_of((at % per) * KEYS, KEYS)
        same = mine == items_ref[at // per, :, pl.ds(start, KEYS)]
        out = []
        for head in range(heads):
            group = slice(head * size, (head + 1) * size)
            queries = q_ref[at // per, group, pl.ds(start, KEYS)]
            d_attn = da_ref[place, group, pl.ds(start, KEYS)]
            scores = dot(k_ref[head], queries)
            d_weights = dot(v_ref[head], d_attn)
            square, inverse = square_of(scores)
            fourth = square * square
            weights = jnp.where(same, fourth * fourth, 0.0).astype(BF16)
            d_scores = jnp.where(same, d_weights * slope_of(scores, square, inverse), 0.0).astype(BF16)
            d_keys, d_values = sums[head]
            out.append((d_keys + dot(d_scores, queries, 1, 1), d_values + dot(weights, d_attn, 1, 1)))
        return tuple(out)

    zero = tuple((jnp.zeros((rows, size), F32), jnp.zeros((rows, size), F32)) for _ in range(heads))
    sums = lax.fori_loop(low // KEYS, (high + KEYS - 1) // KEYS, step, zero)
    dk_ref[...] = jnp.concatenate(
        [unit_back(sums[head][0], k_raw_ref[head]) for head in range(heads)], axis=1
    ).astype(BF16)
    dv_ref[...] = jnp.concatenate(
        [sums[head][1] + dv_conv_ref[head] for head in range(heads)], axis=1
    ).astype(BF16)


def attention_back_kernel(d_first_ref, w_out_ref, raw_ref, d_context_ref, turned_ref, da_ref, da_turned_ref):
    heads, rows, size = raw_ref.shape
    d_context = dot(d_first_ref[...], w_out_ref[...], 1, 1).astype(BF16).astype(F32)
    turned_ref[...] = d_context.T.astype(BF16)
    grads = []
    for head in range(heads):
        grad = d_context[:, head * size : (head + 1) * size]
        d_context_ref[head] = grad.astype(BF16)
        grad = unit_back(grad, raw_ref[head])
        da_ref[head] = grad.astype(BF16)
        grads.append(grad)
    da_turned_ref[...] = jnp.concatenate(grads, axis=1).T.astype(BF16)


def conv_back_kernel(
    place_ref, index_ref, mine_ref, edge_ref, taps_ref, mirrored_ref, v_ref, d_context_ref, turned_ref,
    dv_ref, d_taps_ref,
):
    heads, rows, size = d_context_ref.shape
    blocks, _, width = v_ref.shape
    here = pl.program_id(0)
    tile = index_ref[0] * (width // ROWS) + here
    around = mine_ref[...] == edge_ref[pl.ds(here, 1), :]
    start = pl.multiple_of(here * ROWS, ROWS)

    @pl.when(here == 0)
    def _():
        d_taps_ref[...] = jnp.zeros_like(d_taps_ref)

    for head in range(heads):
        group = slice(head * size, (head + 1) * size)
        band = jnp.where(around, band_of(mirrored_ref[head : head + 1, :], False), 0.0)
        band_high, band_low = split_low(band)
        grads = turned_ref[group, pl.ds(start, BAND)]
        dv_ref[head] = dot(band_high, grads, 1, 1) + dot(band_low, grads, 1, 1)
        values = near(v_ref, group, place_ref, tile, width, blocks * (width // ROWS))
        pairs = jnp.where(around, dot(d_context_ref[head], values), 0.0)
        lined = pairs[:8, :]
        for row in range(8, rows, 8):
            lined = lined + pltpu.roll(pairs[row : row + 8, :], BAND - row, 1)
        total = lined[0:1, :]
        for row in range(1, 8):
            total = total + pltpu.roll(lined[row : row + 1, :], BAND - row, 1)
        d_taps_ref[head : head + 1, :] += total


def per_device(
    tokens, item_lengths, w_qkv, b_qv, taps, w_out, b_out, ln1_gain, ln1_bias, w_up, b_up, w_down, b_down,
    ln2_gain, ln2_bias, d_out,
):
    rows, features = tokens.shape
    heads, kernel = taps.shape
    radius = (kernel - 1) // 2
    columns = w_qkv.shape[2]
    size = columns // heads
    blocks = lax.axis_size("seq")
    total = blocks * rows
    index = lax.axis_index("seq").astype(jnp.int32)
    first_row = index * rows

    count = item_lengths.shape[0]
    upto = jnp.arange(count)[None, :] <= jnp.arange(count)[:, None]
    ends = jnp.sum(jnp.where(upto, item_lengths[None, :], 0), axis=1)
    items = item_index(jnp.arange(total, dtype=jnp.int32), ends).reshape(blocks, 1, rows)
    tiles = rows // ROWS
    edge_at = (
        first_row - ROWS + ROWS * jnp.arange(tiles, dtype=jnp.int32)[:, None]
        + jnp.arange(BAND, dtype=jnp.int32)[None, :]
    )
    edge = item_index(edge_at.reshape(-1), ends).reshape(tiles, BAND)
    mine = item_index(first_row + jnp.arange(rows, dtype=jnp.int32), ends)[:, None]
    place = block_places("seq")
    scalars = (item_lengths, place, index[None])
    reach = ROWS - radius
    banded = jnp.pad(taps, ((0, 0), (reach, BAND - reach - kernel)))
    mirrored = jnp.pad(taps[:, ::-1], ((0, 0), (reach, BAND - reach - kernel)))
    mine_spec = pl.BlockSpec((ROWS, 1), lambda i, *_: (i, 0))
    head_spec = pl.BlockSpec((heads, ROWS, size), lambda i, *_: (0, i, 0))
    row_spec = pl.BlockSpec((ROWS, columns), lambda i, *_: (i, 0))

    w_turned = jnp.swapaxes(w_qkv, 1, 2)
    zeros = jnp.zeros((columns,), F32)
    k_raw, k_own, k_turned = project(tokens, w_turned[1], zeros, heads, True)
    keys = gathered(k_turned, "seq")
    k_turned, w_out_late, w_up_late, w_down_late, b_up_late = lax.optimization_barrier(
        (k_turned, w_out, w_up, w_down, b_up)
    )
    v_own, v_turned = project(tokens, w_turned[2], b_qv[1], heads, False)
    values = gathered(v_turned, "seq")
    q_raw, q_own, q_turned = project(tokens, w_turned[0], b_qv[0], heads, True)
    q_turned, values = lax.optimization_barrier((q_turned, values))
    queries = lax.all_gather(q_turned, "seq")
    out_all = gathered(w_out_late, "mp")
    up_all = gathered(w_up_late, "mp")
    b_up_all = gathered(b_up_late, "mp")
    down_all = gathered(w_down_late, "mp")
    parts = up_all.shape[0]

    shape = jax.ShapeDtypeStruct
    pair_flops = 4 * 2 * rows * (total // 2) * columns
    context, attended = call(
        forward_kernel,
        [shape((rows, columns), BF16), shape((heads, rows, size), F32)],
        *scalars, mine, items, edge, banded, q_own, keys, values,
        grid=(tiles,),
        scalars=3,
        in_specs=[mine_spec, None, None, None, head_spec, None, None],
        out_specs=[row_spec, head_spec],
        flops=pair_flops,
    )
    contexts = gathered(context, "mp")
    branch = jnp.einsum("ptc,pcd->td", contexts, out_all, preferred_element_type=F32)
    first_sum = tokens.astype(F32) + branch + b_out
    first_out, normed_one, scale_one = layer_norm(first_sum, ln1_gain, ln1_bias)
    first_low = first_out.astype(BF16)
    mixed = jnp.zeros((rows, features), F32)
    inner_all, act_all = [], []
    for part in range(parts):
        inner = jnp.dot(first_low, up_all[part], preferred_element_type=F32) + b_up_all[part]
        act = jax.nn.gelu(inner, approximate=False).astype(BF16)
        mixed = mixed + jnp.dot(act, down_all[part], preferred_element_type=F32)
        inner_all.append(inner)
        act_all.append(act)
    second_sum = first_out + mixed + b_down
    result, normed_two, scale_two = layer_norm(second_sum, ln2_gain, ln2_bias)
    layer_output = result.astype(BF16)
    d_second, d_ln2_gain, d_ln2_bias = layer_norm_back(d_out.astype(F32), normed_two, scale_two, ln2_gain)
    d_second_low = d_second.astype(BF16)
    d_b_down = jnp.sum(d_second, axis=0)
    d_w_down = jnp.einsum("tf,td->fd", act_all[0], d_second_low, preferred_element_type=F32)
    d_first_out = d_second
    d_inner_all = []
    for part in range(parts):
        inner = inner_all[part]
        d_act = jnp.einsum("td,fd->tf", d_second_low, down_all[part], preferred_element_type=F32)
        normal_cdf = 0.5 * (1.0 + lax.erf(inner / math.sqrt(2.0)))
        normal_pdf = jnp.exp(-0.5 * inner * inner) / math.sqrt(2.0 * math.pi)
        d_inner = (d_act * (normal_cdf + inner * normal_pdf)).astype(BF16)
        d_first_out = d_first_out + jnp.einsum("tf,df->td", d_inner, up_all[part], preferred_element_type=F32)
        d_inner_all.append(d_inner)
    d_b_up = jnp.sum(d_inner_all[0].astype(F32), axis=0)
    d_w_up = jnp.einsum("td,tf->df", first_low, d_inner_all[0], preferred_element_type=F32)
    d_first, d_ln1_gain, d_ln1_bias = layer_norm_back(d_first_out, normed_one, scale_one, ln1_gain)
    d_first_low = d_first.astype(BF16)
    d_b_out = jnp.sum(d_first, axis=0)
    d_w_out = jnp.einsum("tc,td->cd", context, d_first_low, preferred_element_type=F32)

    early = lax.psum(
        tuple(
            grad.astype(BF16)
            for grad in (
                d_w_out, d_b_out, d_ln1_gain, d_ln1_bias, d_w_up, d_b_up, d_w_down, d_b_down, d_ln2_gain, d_ln2_bias,
            )
        ),
        "seq",
    )

    d_context, d_context_turned, da_own, da_turned = call(
        attention_back_kernel,
        [
            shape((heads, rows, size), BF16), shape((columns, rows), BF16),
            shape((heads, rows, size), BF16), shape((columns, rows), BF16),
        ],
        d_first_low, w_out, attended,
        flops=2 * rows * w_out.size,
    )
    d_attended = gathered(da_turned, "seq")
    ahead = [(i, i + 1) for i in range(blocks - 1)]
    behind = [(i + 1, i) for i in range(blocks - 1)]
    context_rim = jnp.concatenate(
        [
            lax.ppermute(d_context_turned[:, rows - ROWS :], "seq", ahead),
            d_context_turned,
            lax.ppermute(d_context_turned[:, :ROWS], "seq", behind),
        ],
        axis=1,
    )
    dv_conv, d_taps_wide = call(
        conv_back_kernel,
        [shape((heads, rows, size), F32), shape((heads, BAND), F32)],
        place, index[None], mine, edge, banded, mirrored, values, d_context, context_rim,
        grid=(tiles,),
        scalars=2,
        in_specs=[mine_spec, None, None, None, None, head_spec, None],
        out_specs=[head_spec, None],
        flops=2 * rows * BAND * columns,
    )
    d_taps = d_taps_wide[:, reach : reach + kernel]
    [dq] = call(
        query_back_kernel,
        [shape((rows, columns), BF16)],
        *scalars, mine, items, q_own, da_own, q_raw, keys, values,
        grid=(tiles,),
        scalars=3,
        in_specs=[mine_spec, None, head_spec, head_spec, head_spec, None, None],
        out_specs=[row_spec],
        flops=2 * pair_flops,
    )
    dk, dv = call(
        key_back_kernel,
        [shape((rows, columns), BF16), shape((rows, columns), BF16)],
        *scalars, mine, items, k_own, v_own, k_raw, dv_conv, queries, d_attended,
        grid=(tiles,),
        scalars=3,
        in_specs=[mine_spec, None, head_spec, head_spec, head_spec, head_spec, None, None],
        out_specs=[row_spec, row_spec],
        flops=3 * pair_flops,
    )
    d_bias = [jnp.sum(part.astype(F32), axis=0) for part in (dq, dv)]
    small = jnp.concatenate([d_bias[0], d_bias[1], d_taps.reshape(-1)]).astype(BF16)
    spare = 64 * features - small.shape[0]
    d_w_turned = [jnp.einsum("te,td->ed", part, tokens, preferred_element_type=F32).astype(BF16) for part in (dq, dk, dv)]
    late = jnp.concatenate(d_w_turned + [jnp.pad(small, (0, spare)).reshape(64, features)], axis=0)
    late = all_sum(late, "seq")
    d_tokens_part = sum(
        jnp.dot(part, w_turned[i], preferred_element_type=F32) for i, part in enumerate((dq, dk, dv))
    )
    d_tokens = (d_first + all_sum(d_tokens_part.astype(BF16), "mp").astype(F32)).astype(BF16)
    d_w_qkv = jnp.swapaxes(late[: 3 * columns].reshape(3, columns, features), 1, 2).astype(F32)
    small = late[3 * columns :].reshape(-1).astype(F32)
    d_b_qv = small[: 2 * columns].reshape(2, columns)
    d_taps = small[2 * columns : 2 * columns + heads * kernel].reshape(heads, kernel)
    d_w_out, d_b_out, d_ln1_gain, d_ln1_bias, d_w_up, d_b_up, d_w_down, d_b_down, d_ln2_gain, d_ln2_bias = [
        grad.astype(F32) for grad in early
    ]
    return (
        layer_output, d_tokens, d_w_qkv, d_b_qv, d_taps, d_w_out, d_b_out, d_ln1_gain, d_ln1_bias, d_w_up, d_b_up,
        d_w_down, d_b_down, d_ln2_gain, d_ln2_bias,
    )


def solution(mesh):
    placed = (
        P("seq", None), P(), P(None, None, "mp"), P(None, "mp"), P("mp", None), P("mp", None), P(), P(), P(),
        P(None, "mp"), P("mp"), P("mp", None), P(), P(), P(), P("seq", None),
    )
    given = (
        P("seq", None), P("seq", None), P(None, None, "mp"), P(None, "mp"), P("mp", None), P("mp", None), P(),
        P(), P(), P(None, "mp"), P("mp"), P("mp", None), P(), P(), P(),
    )
    return jax.shard_map(per_device, mesh=mesh, in_specs=placed, out_specs=given, check_vma=False)
```

time: 961 us -> 452 us (0.47)
  waiting for transfers between devices: 387 us -> 103 us
  matrix products: 353 us -> 69.1 us
  starting transfers between devices: 11.1 us -> 96.3 us
  Pallas kernels: 0 us -> 55.4 us
  local copies, waits for them, and re-layouts: 59.3 us -> 16.2 us
  other arithmetic: 82.8 us -> 55.6 us
  loops' own time: 12.2 us -> 0 us
    dot_general x36 -> x23, matrix products: 353 us -> 69.1 us  [the longest x4 22.1 us: per_device(): jnp.einsum('tf,df->td', d_inner, up_all[part], preferred_element_type=F32)]
    psum x5 -> x1, waiting for transfers between devices: 245 us -> 0.01 us  [per_device(): lax.psum(tuple((grad.astype(BF16) for grad in (d_w_out, d_b_out, d_ln1_ga...]
    all_gather x2 -> x1, waiting for transfers between devices: 138 us -> 0.01 us  [per_device(): queries = lax.all_gather(q_turned, 'seq')]
    ppermute x4 -> x29, waiting for transfers between devices: 3.83 us -> 103 us  [the longest x19 45.8 us: gathered(): cells = jnp.concatenate([cells, lax.ppermute(cells, axis, pairs)], axis=0)]
    ppermute x4 -> x29, starting transfers between devices: 10.8 us -> 96.3 us  [the longest x19 57.3 us: gathered(): cells = jnp.concatenate([cells, lax.ppermute(cells, axis, pairs)], axis=0)]
    pallas_call x0 -> x8, Pallas kernels: none -> 55.4 us  [call(): pl.pallas_call(kernel, out_shape=out_shape, grid_spec=pltpu.PrefetchScala...]
    concatenate x2 -> x19, other arithmetic: 1.7 us -> 25 us  [the longest x14 20.5 us: gathered(): cells = jnp.concatenate([cells, lax.ppermute(cells, axis, pairs)], axis=0)]
    convert_element_type x31 -> x19, other arithmetic: 32.2 us -> 15.7 us  [the longest x10 10.5 us: per_device(): grad.astype(F32)]
  transfers between devices with their start and end apart: 11 -> 31, of which waited for: 7 -> 13; matrix products, arithmetic and copies ran while one was open for 4% -> 29% of each run, Pallas kernels for 0% -> 11%
where the time goes in v1:
time: 452 us; the launch traced here: 446 us
  waiting for transfers between devices  103 us (23%)
  starting transfers between devices  96.3 us (21%)
  matrix products  69.1 us (15%)
  other arithmetic  55.6 us (12%)
  Pallas kernels  55.4 us (12%)
  blocking collectives  34.6 us (8%)
  local copies, waits for them, and re-layouts  16.2 us (4%)
  between operations  15.3 us (3%)
    ppermute x19, starting transfers between devices, gathered(): cells = jnp.concatenate([cells, lax.ppermute(cells, axis, pairs)], axis=0)  57.3 us
    pallas_call x8, Pallas kernels, call(): pl.pallas_call(kernel, out_shape=out_shape, grid_spec=pltpu.PrefetchScala...  55.4 us
    ppermute x19, waiting for transfers between devices, gathered(): cells = jnp.concatenate([cells, lax.ppermute(cells, axis, pairs)], axis=0)  45.8 us
    psum x1, blocking collectives, per_device(): lax.psum(tuple((grad.astype(BF16) for grad in (d_w_out, d_b_out, d_ln1_ga...  34.6 us
    ppermute x3, starting transfers between devices, all_sum(): got = lax.ppermute(sent, axis, pairs_of(mask))  30.7 us
    ppermute x3, waiting for transfers between devices, all_sum(): got = lax.ppermute(sent, axis, pairs_of(mask))  26.1 us
    dot_general x4, matrix products, per_device(): jnp.einsum('tf,df->td', d_inner, up_all[part], preferred_element_type=F32)  22.1 us
    concatenate x14, other arithmetic, gathered(): cells = jnp.concatenate([cells, lax.ppermute(cells, axis, pairs)], axis=0)  20.5 us
  transfers between devices with their start and end apart: 31, of which 13 were waited for; matrix products, arithmetic and copies ran while one was open for 29% of the time, Pallas kernels for 11%

profile of v1, /device:TPU:0, one launch (start us, length us, event | category | flops | bytes accessed | tf_op | source)
XLA Modules:
  0.0 446.0 jit_solution(12743901761290219805)
XLA Ops:
  7.3 2.2 slice_bitcast_fusion.20
  10.0 4.4 shard_map.272
  14.4 2.9 collective-permute-start.12
  17.5 3.0 collective-permute-start
  21.1 2.5 shard_map.273
  23.6 1.8 collective-permute-start.10
  25.8 11.8 %collective-permute-done.3 = bf16[1,192,512]{2,1,0:T(8,128)(2,1)S(1)} collective-permute-done((bf16[1,192,512]{2,1,0:T(8,128)(2,1)}, bf16[1,192,512]{2,1,0:T(8,128)(2,1)S(1)}, u32[]{:S(2)}, u32[]{:S(2)}) %collective-permute-start.3) | collective-permute-done | bytes 196640 | tf_op jit(solution)/shard_map/ppermute | solution.py:50
  42.7 8.1 %collective-permute-done.4 = bf16[2,192,512]{2,1,0:T(8,128)(2,1)S(1)} collective-permute-done((bf16[2,192,512]{2,1,0:T(8,128)(2,1)S(1)}, bf16[2,192,512]{2,1,0:T(8,128)(2,1)S(1)}, u32[]{:S(2)}, u32[]{:S(2)}) %collective-permute-start.4) | collective-permute-done | bytes 393248 | tf_op jit(solution)/shard_map/ppermute | solution.py:50
  51.7 1.6 collective-permute-start.5
  53.3 4.0 collective-permute-done.1
  58.2 1.5 collective-permute-start.2
  61.5 4.4 shard_map.271
  69.1 3.4 collective-permute-done.5
  72.5 1.5 collective-permute-start.11
  74.1 2.4 pad_maximum_fusion.3.v_ref
  76.5 8.3 %collective-permute-done.2 = bf16[4,192,512]{2,1,0:T(8,128)(2,1)} collective-permute-done((bf16[4,192,512]{2,1,0:T(8,128)(2,1)}, bf16[4,192,512]{2,1,0:T(8,128)(2,1)}, u32[]{:S(2)}, u32[]{:S(2)}) %collective-permute-start.2) | collective-permute-done | bytes 786464 | tf_op jit(solution)/shard_map/ppermute | solution.py:50
  84.9 2.4 pad_maximum_fusion.2.k_ref
  87.3 9.8 %shard_map.274 = (bf16[512,192]{1,0:T(8,128)(2,1)}, f32[3,512,64]{2,1,0:T(8,128)}) custom-call(s32[8]{0:T(128)} %lengths_ref.5, s32[8]{0:T(128)} %fusion.211.place_ref, s32[1]{0:T(128)} %bitcast.index_ref, s32[512,1]{1,0:T(8,128)} %fusion.203.mine_ref, s32[8,1,512]{2,1,0:T(1,128)} %compare_select_fusion.items_ref, s32[4,384]{1,0:T(4,128)} %and_select_fusion.edge_ref, ...), custom_call_target="tpu_custom_call" | custom-call | flops 1610612736 | bytes 3961412 | tf_op jit(solution)/shard_map/pallas_call | solution.py:113
  100.3 3.4 collective-permute-done.6
  103.7 1.8 pad_maximum_fusion.11
  105.6 2.9 pad_maximum_fusion.1
  109.0 3.2 pad_maximum_fusion
  112.5 2.3 fusion.328
  115.9 5.9 %fusion.9 = (bf16[512,768]{1,0:T(8,128)(2,1)S(1)}, f32[512,768]{1,0:T(8,128)S(1)}) fusion(f32[768]{0:T(1024)S(1)} %copy-done.35, bf16[512,768]{1,0:T(8,128)(2,1)S(1)} %fusion.72, bf16[768,768]{1,0:T(8,128)(2,1)} %param.25), kind=kOutput, calls=%fused_computation.22 | convolution fusion | flops 629932032 | bytes 4328448 | tf_op jit(solution)/shard_map/dot_general | solution.py:446
  122.7 2.1 convolution_add_fusion.2
  124.8 5.8 %fusion.79 = f32[512,768]{1,0:T(8,128)S(1)} fusion(bf16[1,768,768]{2,1,0:T(8,128)(2,1)} %collective-permute-done.12, f32[512,768]{1,0:T(8,128)S(1)} %convolution_add_fusion.2), kind=kOutput, calls=%fused_computation.156 | convolution fusion | flops 629538816 | bytes 4325376 | tf_op jit(solution)/shard_map/dot_general | solution.py:448
  130.6 2.1 convolution_add_fusion
  132.7 2.6 convolution_add_fusion.1
  136.5 5.3 %fusion.92 = f32[512,768]{1,0:T(8,128)S(1)} fusion(bf16[2,768,768]{2,1,0:T(8,128)(2,1)} %collective-permute-done.15, f32[512,768]{1,0:T(8,128)S(1)} %convolution_add_fusion.1), kind=kOutput, calls=%fused_computation.167 | convolution fusion | flops 629538816 | bytes 4325376 | tf_op jit(solution)/shard_map/dot_general | solution.py:448
  141.8 6.0 %fusion.329 = (f32[512]{0:T(512)S(1)}, f32[512,768]{1,0:T(8,128)S(1)}) fusion(f32[768]{0:T(1024)S(1)} %copy-done.42, bf16[2,768,768]{2,1,0:T(8,128)(2,1)} %collective-permute-done.15, f32[512,768]{1,0:T(8,128)S(1)} %convolution_add_fusion, f32[512,768]{1,0:T(8,128)S(1)} %fusion.92, f32[512,768]{1,0:T(8,128)S(1)} %fusion.339, f32[512,768]{1,0:T(8,128)S(1)} %fusion.79, ...), kind=kOutput, calls=%fused_computation.459 | convolution fusion | flops 633470464 | bytes 10632192 | tf_op jit(solution)/shard_map/dot_general | solution.py:448
  149.8 1.5 fusion.323
  151.3 1.7 fusion.330
  153.9 3.4 fusion.340
  157.3 5.3 %fusion.91 = f32[512,768]{1,0:T(8,128)} fusion(bf16[2,768,768]{2,1,0:T(8,128)(2,1)} %collective-permute-done.13, f32[512,768]{1,0:T(8,128)} %copy-done.48, bf16[2,768,768]{2,1,0:T(8,128)(2,1)} %collective-permute-done.15, f32[512,768]{1,0:T(8,128)} %copy-done.5), kind=kOutput, calls=%fused_computation.166 | convolution fusion | flops 1212284928 | bytes 7077888 | tf_op jit(solution)/shard_map/tf,df->td/dot_general | solution.py:466
  162.6 5.3 %fusion.81 = f32[512,768]{1,0:T(8,128)} fusion(bf16[1,768,768]{2,1,0:T(8,128)(2,1)} %collective-permute-done.10, f32[512,768]{1,0:T(8,128)} %copy-done.47, bf16[1,768,768]{2,1,0:T(8,128)(2,1)} %collective-permute-done.12, f32[512,768]{1,0:T(8,128)} %copy-done.5), kind=kOutput, calls=%fused_computation.158 | convolution fusion | flops 1212284928 | bytes 7077888 | tf_op jit(solution)/shard_map/tf,df->td/dot_general | solution.py:466
  167.9 8.1 %multiply_reduce_fusion = (bf16[768]{0:T(1024)(128)(2,1)}, f32[512]{0:T(512)S(1)}, f32[512]{0:T(512)S(1)}, bf16[768]{0:T(1024)(128)(2,1)}, f32[512,768]{1,0:T(8,128)}) fusion(f32[512,768]{1,0:T(8,128)S(1)} %get-tuple-element.101, f32[512]{0:T(512)S(1)} %add_rsqrt_fusion.1, f32[512]{0:T(512)S(1)} %broadcast_multiply_fusion.5, f32[768]{0:T(1024)S(1)} %copy-done.31, ...), kind=kOutput, calls=%fused_computation.61 | convolution fusion | flops 1217394176 | bytes 14956544 | tf_op jit(solution)/shard_map/tf,df->td/dot_general | solution.py:466
  176.0 2.4 fusion.325
  179.3 4.3 shard_map.275
  183.7 19.2 %collective-permute-start.18 = (bf16[1,192,512]{2,1,0:T(8,128)(2,1)}, bf16[1,192,512]{2,1,0:T(8,128)(2,1)S(1)}, u32[]{:S(2)}, u32[]{:S(2)}) collective-permute-start(bf16[1,192,512]{2,1,0:T(8,128)(2,1)} %bitcast.111), channel_id=1, source_target_pairs={{0,16},{4,20},{8,24},{12,28},{16,0},{20,4},{24,8},{28,12},{1,17},{... | collective-permute-start | bytes 589832 | tf_op jit(solution)/shard_map/ppermute | solution.py:50
  202.9 10.6 %shard_map.276 = bf16[512,192]{1,0:T(8,128)(2,1)} custom-call(s32[8]{0:T(128)} %lengths_ref.5, s32[8]{0:T(128)} %fusion.211.place_ref, s32[1]{0:T(128)} %bitcast.index_ref, s32[512,1]{1,0:T(8,128)} %fusion.203.mine_ref, s32[8,1,512]{2,1,0:T(1,128)} %compare_select_fusion.items_ref, bf16[3,512,64]{2,1,0:T(8,128)(2,1)} %get-tuple-element.39.q_ref, ...), custom_call_target="tpu_custom_call" | custom-call | flops 3221225472 | bytes 4147268 | tf_op jit(solution)/shard_map/pallas_call | solution.py:113
  213.5 2.6 fusion.320
  216.2 18.7 %collective-permute-start.19 = (bf16[2,192,512]{2,1,0:T(8,128)(2,1)S(1)}, bf16[2,192,512]{2,1,0:T(8,128)(2,1)S(1)}, u32[]{:S(2)}, u32[]{:S(2)}) collective-permute-start(bf16[2,192,512]{2,1,0:T(8,128)(2,1)S(1)} %pad_maximum_fusion.15), channel_id=1, source_target_pairs={{0,8},{4,12},{8,0},{12,4},{16,24},{20,28},{24,16},{28,20},{1,9},{5... | collective-permute-start | bytes 1179656 | tf_op jit(solution)/shard_map/ppermute | solution.py:50
  236.0 1.8 convolution_convert_fusion.1
  237.8 6.8 %collective-permute-done.19 = bf16[2,192,512]{2,1,0:T(8,128)(2,1)S(1)} collective-permute-done((bf16[2,192,512]{2,1,0:T(8,128)(2,1)S(1)}, bf16[2,192,512]{2,1,0:T(8,128)(2,1)S(1)}, u32[]{:S(2)}, u32[]{:S(2)}) %collective-permute-start.19) | collective-permute-done | bytes 393248 | tf_op jit(solution)/shard_map/ppermute | solution.py:50
  245.7 2.0 collective-permute-start.20
  249.6 5.3 %collective-permute-start.16 = (bf16[192,128]{1,0:T(8,128)(2,1)}, bf16[192,128]{1,0:T(8,128)(2,1)}, u32[]{:S(2)}, u32[]{:S(2)}) collective-permute-start(bf16[192,128]{1,0:T(8,128)(2,1)} %get-tuple-element.96), channel_id=1, source_target_pairs={{0,4},{4,8},{8,12},{12,16},{16,20},{20,24},{24,28},{1,5},{5,9},{9,... | collective-permute-start | bytes 147464 | tf_op jit(solution)/shard_map/ppermute | solution.py:499
  254.9 1.8 convolution_convert_fusion
  258.0 9.4 %collective-permute-done.17 = bf16[192,128]{1,0:T(8,128)(2,1)} collective-permute-done((bf16[192,128]{1,0:T(8,128)(2,1)}, bf16[192,128]{1,0:T(8,128)(2,1)}, u32[]{:S(2)}, u32[]{:S(2)}) %collective-permute-start.17) | collective-permute-done | bytes 49184 | tf_op jit(solution)/shard_map/ppermute | solution.py:501
  267.4 3.6 collective-permute-done.16
  271.0 1.7 pad_maximum_fusion.16.turned_ref
  272.7 6.3 %shard_map.277 = (f32[3,512,64]{2,1,0:T(8,128)}, f32[3,384]{1,0:T(4,128)}) custom-call(s32[8]{0:T(128)} %fusion.211.place_ref, s32[1]{0:T(128)} %bitcast.index_ref, s32[512,1]{1,0:T(8,128)} %fusion.203.mine_ref, s32[4,384]{1,0:T(4,128)} %and_select_fusion.edge_ref, f32[3,384]{1,0:T(4,128)} %pad.11.taps_ref, f32[3,384]{1,0:T(4,128)} %pad.12.mirrored_ref, ...), custom_call_target="tpu_custom_call" | custom-call | flops 75497472 | bytes 2479652 | tf_op jit(solution)/shard_map/pallas_call | solution.py:113
  281.6 2.6 pad_maximum_fusion.4.da_ref
  284.2 13.0 %shard_map.278 = (bf16[512,192]{1,0:T(8,128)(2,1)}, bf16[512,192]{1,0:T(8,128)(2,1)}) custom-call(s32[8]{0:T(128)} %lengths_ref.5, s32[8]{0:T(128)} %fusion.211.place_ref, s32[1]{0:T(128)} %bitcast.index_ref, s32[512,1]{1,0:T(8,128)} %fusion.203.mine_ref, s32[8,1,512]{2,1,0:T(1,128)} %compare_select_fusion.items_ref, ...), custom_call_target="tpu_custom_call" | custom-call | flops 4831838208 | bytes 4737092 | tf_op jit(solution)/shard_map/pallas_call | solution.py:113
  297.1 1.6 reduce.3
  298.7 2.0 convolution_convert_fusion.3
  304.8 30.6 %collective-permute-start.24 = (bf16[320,768]{1,0:T(8,128)(2,1)S(1)}, bf16[320,768]{1,0:T(8,128)(2,1)S(1)}, u32[]{:S(2)}, u32[]{:S(2)}) collective-permute-start(bf16[320,768]{1,0:T(8,128)(2,1)S(1)} %constant_dynamic-slice_fusion), channel_id=1, source_target_pairs={{0,4},{4,0},{8,12},{12,8},{16,20},{20,16},{24,28},{28,24},{1,5},{5... | collective-permute-start | bytes 1474568 | tf_op jit(solution)/shard_map/ppermute | solution.py:75
  336.2 6.7 %collective-permute-done.24 = bf16[320,768]{1,0:T(8,128)(2,1)S(1)} collective-permute-done((bf16[320,768]{1,0:T(8,128)(2,1)S(1)}, bf16[320,768]{1,0:T(8,128)(2,1)S(1)}, u32[]{:S(2)}, u32[]{:S(2)}) %collective-permute-start.24) | collective-permute-done | bytes 491552 | tf_op jit(solution)/shard_map/ppermute | solution.py:75
  345.3 19.4 %collective-permute-done.25 = bf16[160,768]{1,0:T(8,128)(2,1)} collective-permute-done((bf16[160,768]{1,0:T(8,128)(2,1)}, bf16[160,768]{1,0:T(8,128)(2,1)}, u32[]{:S(2)}, u32[]{:S(2)}) %collective-permute-start.25) | collective-permute-done | bytes 245792 | tf_op jit(solution)/shard_map/ppermute | solution.py:75
  366.1 1.5 collective-permute-start.22
  367.6 17.8 %collective-permute-done.26 = bf16[160,768]{1,0:T(8,128)(2,1)S(1)} collective-permute-done((bf16[160,768]{1,0:T(8,128)(2,1)S(1)}, bf16[160,768]{1,0:T(8,128)(2,1)S(1)}, u32[]{:S(2)}, u32[]{:S(2)}) %collective-permute-start.26) | collective-permute-done | bytes 245792 | tf_op jit(solution)/shard_map/ppermute | solution.py:77
  386.0 34.6 %all-reduce.3 = (bf16[768]{0:T(1024)(128)(2,1)S(1)}, bf16[768]{0:T(1024)(128)(2,1)S(1)}, bf16[768]{0:T(1024)(128)(2,1)S(1)}, bf16[768]{0:T(1024)(128)(2,1)S(1)},...) all-reduce(bf16[768]{0:T(1024)(128)(2,1)S(1)} %get-tuple-element.84, ...), channel_id=1, replica_groups=mesh['seq'=8,'mp'=4] {'seq'}, use_global_device_ids=true, to_apply=%region_16.17 | all-reduce | flops 5376 | bytes 21504 | tf_op jit(solution)/shard_map/psum | solution.py:475
  428.7 1.8 convert_element_type.246
  430.5 2.9 convert_element_type.254
  433.4 1.6 convert_element_type.257
  (223 shorter events, 52.9 us)
Async XLA Ops:
  7.2 10.2 %copy-start.19 = (bf16[192,768]{1,0:T(8,128)(2,1)S(1)}, bf16[192,768]{1,0:T(8,128)(2,1)}, u32[]{:S(2)}) copy-start(bf16[192,768]{1,0:T(8,128)(2,1)} %w_out_ref.1) | copy-start | bytes 884740
  7.2 7.2 %copy-start.20 = (bf16[768,768]{1,0:T(8,128)(2,1)S(1)}, bf16[768,768]{1,0:T(8,128)(2,1)}, u32[]{:S(2)}) copy-start(bf16[768,768]{1,0:T(8,128)(2,1)} %param.27) | copy-start | bytes 3538948
  7.2 13.3 %copy-start.40 = (f32[2,192]{1,0:T(2,128)S(1)}, f32[2,192]{1,0:T(2,128)}, u32[]{:S(2)}) copy-start(f32[2,192]{1,0:T(2,128)} %param.19) | copy-start | bytes 4612
  7.2 276.9 %all-gather.3.cloned.1.call-start = ((), (), s32[]{:S(2)}) async-start(), calls=%async_computation | async-start | bytes 1769472 | tf_op jit(solution)/shard_map/all_gather | solution.py:419
  7.3 18.2 %copy-start.43 = (s32[8]{0:T(128)S(1)}, s32[8]{0:T(128)}, u32[]{:S(2)}) copy-start(s32[8]{0:T(128)} %lengths_ref.5) | copy-start | bytes 100
  14.4 25.1 %copy-start.11 = (bf16[192,512]{1,0:T(8,128)(2,1)S(1)}, bf16[192,512]{1,0:T(8,128)(2,1)}, u32[]{:S(2)}) copy-start(bf16[192,512]{1,0:T(8,128)(2,1)} %get-tuple-element.40) | copy-start | bytes 589828
  14.4 91.1 %collective-permute-start.12 = (bf16[1,768,768]{2,1,0:T(8,128)(2,1)S(1)}, bf16[1,768,768]{2,1,0:T(8,128)(2,1)}, u32[]{:S(2)}, u32[]{:S(2)}) collective-permute-start(bf16[1,768,768]{2,1,0:T(8,128)(2,1)S(1)} %bitcast.118), channel_id=1, source_target_pairs={{0,2},{1,3},{2,0},{3,1},{4,6},{5,7},{6,4},{7,5},{8,10},{9,11},{10,... | collective-permute-start | bytes 3538952 | tf_op jit(solution)/shard_map/ppermute | solution.py:50
  17.4 81.2 %collective-permute-start.8 = (bf16[1,192,768]{2,1,0:T(8,128)(2,1)S(1)}, bf16[1,192,768]{2,1,0:T(8,128)(2,1)}, u32[]{:S(2)}, u32[]{:S(2)}) collective-permute-start(bf16[1,192,768]{2,1,0:T(8,128)(2,1)S(1)} %bitcast.115), channel_id=1, source_target_pairs={{0,2},{1,3},{2,0},{3,1},{4,6},{5,7},{6,4},{7,5},{8,10},{9,11},{10,... | collective-permute-start | bytes 884744 | tf_op jit(solution)/shard_map/ppermute | solution.py:50
  17.5 22.1 %collective-permute-start = (bf16[1,192,512]{2,1,0:T(8,128)(2,1)}, bf16[1,192,512]{2,1,0:T(8,128)(2,1)S(1)}, u32[]{:S(2)}, u32[]{:S(2)}) collective-permute-start(bf16[1,192,512]{2,1,0:T(8,128)(2,1)} %bitcast.103), channel_id=1, source_target_pairs={{0,16},{4,20},{8,24},{12,28},{16,0},{20,4},{24,8},{28,12},{1,17},{... | collective-permute-start | bytes 589832 | tf_op jit(solution)/shard_map/ppermute | solution.py:50
  23.6 27.2 %copy-start.12 = (bf16[192,512]{1,0:T(8,128)(2,1)S(1)}, bf16[192,512]{1,0:T(8,128)(2,1)}, u32[]{:S(2)}) copy-start(bf16[192,512]{1,0:T(8,128)(2,1)} %get-tuple-element.42) | copy-start | bytes 589828
  23.6 14.1 %collective-permute-start.3 = (bf16[1,192,512]{2,1,0:T(8,128)(2,1)}, bf16[1,192,512]{2,1,0:T(8,128)(2,1)S(1)}, u32[]{:S(2)}, u32[]{:S(2)}) collective-permute-start(bf16[1,192,512]{2,1,0:T(8,128)(2,1)} %bitcast.107), channel_id=1, source_target_pairs={{0,16},{4,20},{8,24},{12,28},{16,0},{20,4},{24,8},{28,12},{1,17},{... | collective-permute-start | bytes 589832 | tf_op jit(solution)/shard_map/ppermute | solution.py:50
  23.6 85.4 %collective-permute-start.10 = (bf16[1,768,768]{2,1,0:T(8,128)(2,1)}, bf16[1,768,768]{2,1,0:T(8,128)(2,1)}, u32[]{:S(2)}, u32[]{:S(2)}) collective-permute-start(bf16[1,768,768]{2,1,0:T(8,128)(2,1)} %bitcast.13), channel_id=1, source_target_pairs={{0,2},{1,3},{2,0},{3,1},{4,6},{5,7},{6,4},{7,5},{8,10},{9,11},{10,... | collective-permute-start | bytes 3538952 | tf_op jit(solution)/shard_map/ppermute | solution.py:50
  38.7 12.1 %collective-permute-start.4 = (bf16[2,192,512]{2,1,0:T(8,128)(2,1)S(1)}, bf16[2,192,512]{2,1,0:T(8,128)(2,1)S(1)}, u32[]{:S(2)}, u32[]{:S(2)}) collective-permute-start(bf16[2,192,512]{2,1,0:T(8,128)(2,1)S(1)} %pad_maximum_fusion.14), channel_id=1, source_target_pairs={{0,8},{4,12},{8,0},{12,4},{16,24},{20,28},{24,16},{28,20},{1,9},{5... | collective-permute-start | bytes 1179656 | tf_op jit(solution)/shard_map/ppermute | solution.py:50
  39.6 17.7 %collective-permute-start.1 = (bf16[2,192,512]{2,1,0:T(8,128)(2,1)S(1)}, bf16[2,192,512]{2,1,0:T(8,128)(2,1)S(1)}, u32[]{:S(2)}, u32[]{:S(2)}) collective-permute-start(bf16[2,192,512]{2,1,0:T(8,128)(2,1)S(1)} %pad_maximum_fusion.13), channel_id=1, source_target_pairs={{0,8},{4,12},{8,0},{12,4},{16,24},{20,28},{24,16},{28,20},{1,9},{5... | collective-permute-start | bytes 1179656 | tf_op jit(solution)/shard_map/ppermute | solution.py:50
  42.7 17.1 %copy-start.33 = (f32[3,33]{1,0:T(4,128)S(1)}, f32[3,33]{1,0:T(4,128)}, u32[]{:S(2)}) copy-start(f32[3,33]{1,0:T(4,128)} %param.20) | copy-start | bytes 1192
  42.7 18.1 %copy-start.35 = (f32[768]{0:T(1024)S(1)}, f32[768]{0:T(1024)}, u32[]{:S(2)}) copy-start(f32[768]{0:T(1024)} %param.26) | copy-start | bytes 9220
  51.7 20.8 %collective-permute-start.5 = (bf16[4,192,512]{2,1,0:T(8,128)(2,1)}, bf16[4,192,512]{2,1,0:T(8,128)(2,1)}, u32[]{:S(2)}, u32[]{:S(2)}) collective-permute-start(bf16[4,192,512]{2,1,0:T(8,128)(2,1)} %pad_maximum_fusion.8), channel_id=1, source_target_pairs={{0,4},{4,0},{8,12},{12,8},{16,20},{20,16},{24,28},{28,24},{1,5},{5... | collective-permute-start | bytes 2359304 | tf_op jit(solution)/shard_map/ppermute | solution.py:50
  58.2 26.6 %collective-permute-start.2 = (bf16[4,192,512]{2,1,0:T(8,128)(2,1)}, bf16[4,192,512]{2,1,0:T(8,128)(2,1)}, u32[]{:S(2)}, u32[]{:S(2)}) collective-permute-start(bf16[4,192,512]{2,1,0:T(8,128)(2,1)} %pad_maximum_fusion.7), channel_id=1, source_target_pairs={{0,4},{4,0},{8,12},{12,8},{16,20},{20,16},{24,28},{28,24},{1,5},{5... | collective-permute-start | bytes 2359304 | tf_op jit(solution)/shard_map/ppermute | solution.py:50
  72.5 27.2 %collective-permute-start.11 = (f32[1,768]{1,0:T(1,128)S(1)}, f32[1,768]{1,0:T(1,128)S(1)}, u32[]{:S(2)}, u32[]{:S(2)}) collective-permute-start(f32[1,768]{1,0:T(1,128)S(1)} %broadcast_in_dim.101), channel_id=1, source_target_pairs={{0,2},{1,3},{2,0},{3,1},{4,6},{5,7},{6,4},{7,5},{8,10},{9,11},{10,... | collective-permute-start | bytes 9224 | tf_op jit(solution)/shard_map/ppermute | solution.py:50
  97.1 6.6 %collective-permute-start.6 = (bf16[1,512,192]{2,1,0:T(8,128)(2,1)}, bf16[1,512,192]{2,1,0:T(8,128)(2,1)S(1)}, u32[]{:S(2)}, u32[]{:S(2)}) collective-permute-start(bf16[1,512,192]{2,1,0:T(8,128)(2,1)} %bitcast.120), channel_id=1, source_target_pairs={{0,2},{1,3},{2,0},{3,1},{4,6},{5,7},{6,4},{7,5},{8,10},{9,11},{10,... | collective-permute-start | bytes 589832 | tf_op jit(solution)/shard_map/ppermute | solution.py:50
  99.6 12.8 %collective-permute-start.9 = (bf16[2,192,768]{2,1,0:T(8,128)(2,1)S(1)}, bf16[2,192,768]{2,1,0:T(8,128)(2,1)}, u32[]{:S(2)}, u32[]{:S(2)}) collective-permute-start(bf16[2,192,768]{2,1,0:T(8,128)(2,1)S(1)} %pad_maximum_fusion.10), channel_id=1, source_target_pairs={{0,1},{1,0},{2,3},{3,2},{4,5},{5,4},{6,7},{7,6},{8,9},{9,8},{10,11... | collective-permute-start | bytes 1769480 | tf_op jit(solution)/shard_map/ppermute | solution.py:50
  99.7 5.8 %collective-permute-start.14 = (f32[2,768]{1,0:T(2,128)S(1)}, f32[2,768]{1,0:T(2,128)S(1)}, u32[]{:S(2)}, u32[]{:S(2)}) collective-permute-start(f32[2,768]{1,0:T(2,128)S(1)} %pad_maximum_fusion.17), channel_id=1, source_target_pairs={{0,1},{1,0},{2,3},{3,2},{4,5},{5,4},{6,7},{7,6},{8,9},{9,8},{10,11... | collective-permute-start | bytes 18440 | tf_op jit(solution)/shard_map/ppermute | solution.py:50
  105.5 6.9 %collective-permute-start.7 = (bf16[2,512,192]{2,1,0:T(8,128)(2,1)}, bf16[2,512,192]{2,1,0:T(8,128)(2,1)}, u32[]{:S(2)}, u32[]{:S(2)}) collective-permute-start(bf16[2,512,192]{2,1,0:T(8,128)(2,1)} %pad_maximum_fusion.11), channel_id=1, source_target_pairs={{0,1},{1,0},{2,3},{3,2},{4,5},{5,4},{6,7},{7,6},{8,9},{9,8},{10,11... | collective-permute-start | bytes 1179656 | tf_op jit(solution)/shard_map/ppermute | solution.py:50
  108.5 26.9 %collective-permute-start.15 = (bf16[2,768,768]{2,1,0:T(8,128)(2,1)}, bf16[2,768,768]{2,1,0:T(8,128)(2,1)}, u32[]{:S(2)}, u32[]{:S(2)}) collective-permute-start(bf16[2,768,768]{2,1,0:T(8,128)(2,1)} %pad_maximum_fusion.1), channel_id=1, source_target_pairs={{0,1},{1,0},{2,3},{3,2},{4,5},{5,4},{6,7},{7,6},{8,9},{9,8},{10,11... | collective-permute-start | bytes 7077896 | tf_op jit(solution)/shard_map/ppermute | solution.py:50
  112.2 18.4 %collective-permute-start.13 = (bf16[2,768,768]{2,1,0:T(8,128)(2,1)}, bf16[2,768,768]{2,1,0:T(8,128)(2,1)}, u32[]{:S(2)}, u32[]{:S(2)}) collective-permute-start(bf16[2,768,768]{2,1,0:T(8,128)(2,1)} %pad_maximum_fusion), channel_id=1, source_target_pairs={{0,1},{1,0},{2,3},{3,2},{4,5},{5,4},{6,7},{7,6},{8,9},{9,8},{10,11... | collective-permute-start | bytes 7077896 | tf_op jit(solution)/shard_map/ppermute | solution.py:50
  112.4 316.3 %all-reduce.7.cloned.1.call-start = ((), (), s32[]{:S(2)}) async-start(), calls=%async_computation.1 | async-start | bytes 5308416 | tf_op jit(solution)/shard_map/psum | solution.py:475
  114.8 53.2 %copy-start.1 = (f32[512,768]{1,0:T(8,128)}, f32[512,768]{1,0:T(8,128)S(1)}, u32[]{:S(2)}) copy-start(f32[512,768]{1,0:T(8,128)S(1)} %get-tuple-element.101) | copy-start | bytes 4718596
  115.8 16.9 %copy-start.28 = (bf16[512,768]{1,0:T(8,128)(2,1)}, bf16[512,768]{1,0:T(8,128)(2,1)S(1)}, u32[]{:S(2)}) copy-start(bf16[512,768]{1,0:T(8,128)(2,1)S(1)} %fusion.72) | copy-start | bytes 2359300
  115.8 6.0 %copy-start.21 = (bf16[768,768]{1,0:T(8,128)(2,1)S(1)}, bf16[768,768]{1,0:T(8,128)(2,1)}, u32[]{:S(2)}) copy-start(bf16[768,768]{1,0:T(8,128)(2,1)} %param.27) | copy-start | bytes 3538948
  124.7 5.9 %copy-start.47 = (f32[512,768]{1,0:T(8,128)}, f32[512,768]{1,0:T(8,128)S(1)}, u32[]{:S(2)}) copy-start(f32[512,768]{1,0:T(8,128)S(1)} %convolution_add_fusion.2) | copy-start | bytes 4718596
  132.7 9.1 %copy-start.46 = (f32[512,768]{1,0:T(8,128)}, f32[512,768]{1,0:T(8,128)S(1)}, u32[]{:S(2)}) copy-start(f32[512,768]{1,0:T(8,128)S(1)} %convolution_add_fusion) | copy-start | bytes 4718596
  135.3 6.5 %copy-start.42 = (f32[768]{0:T(1024)S(1)}, f32[768]{0:T(1024)}, u32[]{:S(2)}) copy-start(f32[768]{0:T(1024)} %param.28) | copy-start | bytes 9220
  183.7 32.5 %collective-permute-start.18 = (bf16[1,192,512]{2,1,0:T(8,128)(2,1)}, bf16[1,192,512]{2,1,0:T(8,128)(2,1)S(1)}, u32[]{:S(2)}, u32[]{:S(2)}) collective-permute-start(bf16[1,192,512]{2,1,0:T(8,128)(2,1)} %bitcast.111), channel_id=1, source_target_pairs={{0,16},{4,20},{8,24},{12,28},{16,0},{20,4},{24,8},{28,12},{1,17},{... | collective-permute-start | bytes 589832 | tf_op jit(solution)/shard_map/ppermute | solution.py:50
  213.5 21.4 %copy-start.9 = (bf16[512,192]{1,0:T(8,128)(2,1)S(1)}, bf16[512,192]{1,0:T(8,128)(2,1)}, u32[]{:S(2)}) copy-start(bf16[512,192]{1,0:T(8,128)(2,1)} %shard_map.276) | copy-start | bytes 589828
  216.1 19.9 %copy-start.29 = (bf16[512,768]{1,0:T(8,128)(2,1)S(1)}, bf16[512,768]{1,0:T(8,128)(2,1)}, u32[]{:S(2)}) copy-start(bf16[512,768]{1,0:T(8,128)(2,1)} %copy-done.28) | copy-start | bytes 2359300
  216.1 19.9 %copy-start.45 = (bf16[512,768]{1,0:T(8,128)(2,1)S(1)}, bf16[512,768]{1,0:T(8,128)(2,1)}, u32[]{:S(2)}) copy-start(bf16[512,768]{1,0:T(8,128)(2,1)} %copy-done.44) | copy-start | bytes 2359300
  216.1 28.5 %copy-start.15 = (bf16[1,192,512]{2,1,0:T(8,128)(2,1)}, bf16[1,192,512]{2,1,0:T(8,128)(2,1)S(1)}, u32[]{:S(2)}) copy-start(bf16[1,192,512]{2,1,0:T(8,128)(2,1)S(1)} %collective-permute-done.18) | copy-start | bytes 589828
  216.2 28.4 %collective-permute-start.19 = (bf16[2,192,512]{2,1,0:T(8,128)(2,1)S(1)}, bf16[2,192,512]{2,1,0:T(8,128)(2,1)S(1)}, u32[]{:S(2)}, u32[]{:S(2)}) collective-permute-start(bf16[2,192,512]{2,1,0:T(8,128)(2,1)S(1)} %pad_maximum_fusion.15), channel_id=1, source_target_pairs={{0,8},{4,12},{8,0},{12,4},{16,24},{20,28},{24,16},{28,20},{1,9},{5... | collective-permute-start | bytes 1179656 | tf_op jit(solution)/shard_map/ppermute | solution.py:50
  236.0 11.7 %copy-start.30 = (bf16[192,512]{1,0:T(8,128)(2,1)S(1)}, bf16[192,512]{1,0:T(8,128)(2,1)}, u32[]{:S(2)}) copy-start(bf16[192,512]{1,0:T(8,128)(2,1)} %get-tuple-element.56) | copy-start | bytes 589828
  236.0 18.9 %copy-start.27 = (bf16[512,768]{1,0:T(8,128)(2,1)S(1)}, bf16[512,768]{1,0:T(8,128)(2,1)}, u32[]{:S(2)}) copy-start(bf16[512,768]{1,0:T(8,128)(2,1)} %copy-done.26) | copy-start | bytes 2359300
  237.8 17.1 %copy-start.6 = (f32[512,768]{1,0:T(8,128)S(1)}, f32[512,768]{1,0:T(8,128)}, u32[]{:S(2)}) copy-start(f32[512,768]{1,0:T(8,128)} %copy-done.5) | copy-start | bytes 4718596
  245.7 35.9 %collective-permute-start.20 = (bf16[4,192,512]{2,1,0:T(8,128)(2,1)}, bf16[4,192,512]{2,1,0:T(8,128)(2,1)}, u32[]{:S(2)}, u32[]{:S(2)}) collective-permute-start(bf16[4,192,512]{2,1,0:T(8,128)(2,1)} %pad_maximum_fusion.9), channel_id=1, source_target_pairs={{0,4},{4,0},{8,12},{12,8},{16,20},{20,16},{24,28},{28,24},{1,5},{5... | collective-permute-start | bytes 2359304 | tf_op jit(solution)/shard_map/ppermute | solution.py:50
  248.3 19.1 %collective-permute-start.17 = (bf16[192,128]{1,0:T(8,128)(2,1)}, bf16[192,128]{1,0:T(8,128)(2,1)}, u32[]{:S(2)}, u32[]{:S(2)}) collective-permute-start(bf16[192,128]{1,0:T(8,128)(2,1)} %get-tuple-element.97), channel_id=1, source_target_pairs={{4,0},{8,4},{12,8},{16,12},{20,16},{24,20},{28,24},{5,1},{9,5},{13... | collective-permute-start | bytes 147464 | tf_op jit(solution)/shard_map/ppermute | solution.py:501
  249.6 7.2 %copy-start.2 = (bf16[512,768]{1,0:T(8,128)(2,1)S(1)}, bf16[512,768]{1,0:T(8,128)(2,1)}, u32[]{:S(2)}) copy-start(bf16[512,768]{1,0:T(8,128)(2,1)} %convert_element_type.216.d_first_ref) | copy-start | bytes 2359300
  249.6 7.1 %copy-start.24 = (bf16[512,192]{1,0:T(8,128)(2,1)S(1)}, bf16[512,192]{1,0:T(8,128)(2,1)}, u32[]{:S(2)}) copy-start(bf16[512,192]{1,0:T(8,128)(2,1)} %get-tuple-element.44) | copy-start | bytes 589828
  249.6 21.4 %collective-permute-start.16 = (bf16[192,128]{1,0:T(8,128)(2,1)}, bf16[192,128]{1,0:T(8,128)(2,1)}, u32[]{:S(2)}, u32[]{:S(2)}) collective-permute-start(bf16[192,128]{1,0:T(8,128)(2,1)} %get-tuple-element.96), channel_id=1, source_target_pairs={{0,4},{4,8},{8,12},{12,16},{16,20},{20,24},{24,28},{1,5},{5,9},{9,... | collective-permute-start | bytes 147464 | tf_op jit(solution)/shard_map/ppermute | solution.py:499
  258.0 23.6 %copy-start.14 = (bf16[192,512]{1,0:T(8,128)(2,1)S(1)}, bf16[192,512]{1,0:T(8,128)(2,1)}, u32[]{:S(2)}) copy-start(bf16[192,512]{1,0:T(8,128)(2,1)} %get-tuple-element.59) | copy-start | bytes 589828
  258.0 23.6 %copy-start.16 = (bf16[1,192,512]{2,1,0:T(8,128)(2,1)S(1)}, bf16[1,192,512]{2,1,0:T(8,128)(2,1)}, u32[]{:S(2)}) copy-start(bf16[1,192,512]{2,1,0:T(8,128)(2,1)} %copy-done.15) | copy-start | bytes 589828
  297.1 6.4 %copy-start.22 = (bf16[192,768]{1,0:T(8,128)(2,1)S(1)}, bf16[192,768]{1,0:T(8,128)(2,1)}, u32[]{:S(2)}) copy-start(bf16[192,768]{1,0:T(8,128)(2,1)} %convolution_convert_fusion.5) | copy-start | bytes 884740
  303.5 31.9 %copy-start.7 = (bf16[3,768,192]{1,2,0:T(8,128)(2,1)S(1)}, bf16[3,768,192]{1,2,0:T(8,128)(2,1)}, u32[]{:S(2)}) copy-start(bf16[3,768,192]{1,2,0:T(8,128)(2,1)} %param.18) | copy-start | bytes 2654212
  303.6 31.9 %copy-start.25 = (bf16[512,192]{1,0:T(8,128)(2,1)S(1)}, bf16[512,192]{1,0:T(8,128)(2,1)}, u32[]{:S(2)}) copy-start(bf16[512,192]{1,0:T(8,128)(2,1)} %get-tuple-element.60) | copy-start | bytes 589828
  304.7 31.1 %copy-start.4 = (f32[512,768]{1,0:T(8,128)S(1)}, f32[512,768]{1,0:T(8,128)}, u32[]{:S(2)}) copy-start(f32[512,768]{1,0:T(8,128)} %fusion.320) | copy-start | bytes 4718596
  304.7 31.1 %copy-start.8 = (bf16[512,192]{1,0:T(8,128)(2,1)S(1)}, bf16[512,192]{1,0:T(8,128)(2,1)}, u32[]{:S(2)}) copy-start(bf16[512,192]{1,0:T(8,128)(2,1)} %get-tuple-element.61) | copy-start | bytes 589828
  304.8 38.1 %collective-permute-start.24 = (bf16[320,768]{1,0:T(8,128)(2,1)S(1)}, bf16[320,768]{1,0:T(8,128)(2,1)S(1)}, u32[]{:S(2)}, u32[]{:S(2)}) collective-permute-start(bf16[320,768]{1,0:T(8,128)(2,1)S(1)} %constant_dynamic-slice_fusion), channel_id=1, source_target_pairs={{0,4},{4,0},{8,12},{12,8},{16,20},{20,16},{24,28},{28,24},{1,5},{5... | collective-permute-start | bytes 1474568 | tf_op jit(solution)/shard_map/ppermute | solution.py:75
  344.5 20.2 %collective-permute-start.25 = (bf16[160,768]{1,0:T(8,128)(2,1)}, bf16[160,768]{1,0:T(8,128)(2,1)}, u32[]{:S(2)}, u32[]{:S(2)}) collective-permute-start(bf16[160,768]{1,0:T(8,128)(2,1)} %constant_dynamic-slice_fusion.2), channel_id=1, source_target_pairs={{0,8},{4,12},{8,0},{12,4},{16,24},{20,28},{24,16},{28,20},{1,9},{5... | collective-permute-start | bytes 737288 | tf_op jit(solution)/shard_map/ppermute | solution.py:75
  345.3 20.6 %collective-permute-start.21 = (bf16[256,768]{1,0:T(8,128)(2,1)}, bf16[256,768]{1,0:T(8,128)(2,1)S(1)}, u32[]{:S(2)}, u32[]{:S(2)}) collective-permute-start(bf16[256,768]{1,0:T(8,128)(2,1)} %constant_dynamic-slice_fusion.1), channel_id=1, source_target_pairs={{0,1},{1,0},{2,3},{3,2},{4,5},{5,4},{6,7},{7,6},{8,9},{9,8},{10,11... | collective-permute-start | bytes 1179656 | tf_op jit(solution)/shard_map/ppermute | solution.py:75
  365.9 19.6 %collective-permute-start.26 = (bf16[160,768]{1,0:T(8,128)(2,1)S(1)}, bf16[160,768]{1,0:T(8,128)(2,1)S(1)}, u32[]{:S(2)}, u32[]{:S(2)}) collective-permute-start(bf16[160,768]{1,0:T(8,128)(2,1)S(1)} %add_convert_fusion.7), channel_id=1, source_target_pairs={{0,16},{4,20},{8,24},{12,28},{16,0},{20,4},{24,8},{28,12},{1,17},{... | collective-permute-start | bytes 737288 | tf_op jit(solution)/shard_map/ppermute | solution.py:77
  366.1 19.9 %copy-start.37 = (bf16[768]{0:T(1024)(128)(2,1)S(1)}, bf16[768]{0:T(1024)(128)(2,1)}, u32[]{:S(2)}) copy-start(bf16[768]{0:T(1024)(128)(2,1)} %get-tuple-element.107) | copy-start | bytes 4612
  366.1 19.9 %copy-start.38 = (bf16[768]{0:T(1024)(128)(2,1)S(1)}, bf16[768]{0:T(1024)(128)(2,1)}, u32[]{:S(2)}) copy-start(bf16[768]{0:T(1024)(128)(2,1)} %get-tuple-element.63) | copy-start | bytes 4612
  366.1 19.9 %copy-start.39 = (bf16[768]{0:T(1024)(128)(2,1)S(1)}, bf16[768]{0:T(1024)(128)(2,1)}, u32[]{:S(2)}) copy-start(bf16[768]{0:T(1024)(128)(2,1)} %get-tuple-element.68) | copy-start | bytes 4612
  366.1 19.5 %collective-permute-start.22 = (bf16[256,768]{1,0:T(8,128)(2,1)S(1)}, bf16[256,768]{1,0:T(8,128)(2,1)S(1)}, u32[]{:S(2)}, u32[]{:S(2)}) collective-permute-start(bf16[256,768]{1,0:T(8,128)(2,1)S(1)} %add_convert_fusion.5), channel_id=1, source_target_pairs={{0,2},{1,3},{2,0},{3,1},{4,6},{5,7},{6,4},{7,5},{8,10},{9,11},{10,... | collective-permute-start | bytes 1179656 | tf_op jit(solution)/shard_map/ppermute | solution.py:77
  385.5 39.2 %collective-permute-start.27 = (bf16[160,768]{1,0:T(8,128)(2,1)S(1)}, bf16[160,768]{1,0:T(8,128)(2,1)}, u32[]{:S(2)}, u32[]{:S(2)}) collective-permute-start(bf16[160,768]{1,0:T(8,128)(2,1)S(1)} %add_convert_fusion.6), channel_id=1, source_target_pairs={{0,8},{4,12},{8,0},{12,4},{16,24},{20,28},{24,16},{28,20},{1,9},{5... | collective-permute-start | bytes 737288 | tf_op jit(solution)/shard_map/ppermute | solution.py:81
  385.7 40.8 %collective-permute-start.23 = (bf16[256,768]{1,0:T(8,128)(2,1)S(1)}, bf16[256,768]{1,0:T(8,128)(2,1)}, u32[]{:S(2)}, u32[]{:S(2)}) collective-permute-start(bf16[256,768]{1,0:T(8,128)(2,1)S(1)} %add_convert_fusion.4), channel_id=1, source_target_pairs={{0,1},{1,0},{2,3},{3,2},{4,5},{5,4},{6,7},{7,6},{8,9},{9,8},{10,11... | collective-permute-start | bytes 1179656 | tf_op jit(solution)/shard_map/ppermute | solution.py:81
  426.5 9.0 %collective-permute-start.28 = (bf16[320,768]{1,0:T(8,128)(2,1)}, bf16[320,768]{1,0:T(8,128)(2,1)S(1)}, u32[]{:S(2)}, u32[]{:S(2)}) collective-permute-start(bf16[320,768]{1,0:T(8,128)(2,1)} %pad_maximum_fusion.12), channel_id=1, source_target_pairs={{0,4},{4,0},{8,12},{12,8},{16,20},{20,16},{24,28},{28,24},{1,5},{5... | collective-permute-start | bytes 1474568 | tf_op jit(solution)/shard_map/ppermute | solution.py:81
  (16 other events, 33.2 us)
Sparse Core Ops, SparseCore 0:
  112.5 60.0 all-gather.2
  258.1 127.7 all-reduce.6

commit v2 on v0

v2 whole, which is shorter than its diff:
```python
import functools
import math

import jax
import jax.numpy as jnp
from jax import lax
from jax.experimental import pallas as pl
from jax.experimental.pallas import tpu as pltpu
from jax.sharding import PartitionSpec as P

SHRINK = 0.95
NORM_EPS = 1e-06
LAYER_EPS = 1e-05
F32 = jnp.float32
BF16 = jnp.bfloat16
KEYS = 256
CHUNK = 256
EDGE = 128
BAND = 3 * EDGE
MIDDLE = 256
WINDOW = 9216
VMEM_BYTES = 56 * 1024 * 1024
SQUARE_OF_V = (
    0.9999936361319989,
    -1.2731008162270503,
    0.4040306859655804,
    -0.20598641392473288,
    0.11615118744625774,
    -0.05772567810293111,
    0.02001158958170149,
    -0.00337422878652264,
)
SQUARE = tuple(factor * (0.5 * SHRINK) ** (0.5 * power) for power, factor in enumerate(SQUARE_OF_V))
SLOPE = 8.0 / math.pi
TAIL_AT = 0.2316419
TAIL = (0.319381530, -0.356563782, 1.781477937, -1.821255978, 1.330274429)


def dot(left, right, left_dim=1, right_dim=0):
    return lax.dot_general(
        left, right, (((left_dim,), (right_dim,)), ((), ())), preferred_element_type=F32
    )


def flipped(cells, axis, mask):
    return lax.ppermute(cells, axis, [(i, i ^ mask) for i in range(lax.axis_size(axis))])


def masks_of(axis):
    return [1 << bit for bit in range(lax.axis_size(axis).bit_length() - 2, -1, -1)]


def block_places(axis, masks):
    apart = jnp.arange(lax.axis_size(axis), dtype=jnp.int32) ^ lax.axis_index(axis).astype(jnp.int32)
    place = jnp.zeros_like(apart)
    for bit, mask in enumerate(masks):
        place = place | (jnp.where((apart & mask) != 0, 1, 0) << bit)
    return place


def all_sum(cells, axis, holds=()):
    index = lax.axis_index(axis)
    masks = masks_of(axis)[::-1]
    waits, stages = iter(holds), []

    def exchanged(array, mask):
        got = flipped(array, axis, mask)
        held = next(waits, ())
        stages.append(after(got, *held) if held else got)
        return stages[-1]

    for mask in masks[:-1]:
        half = cells.shape[0] // 2
        upper = (index & mask) != 0
        sent = lax.dynamic_slice_in_dim(cells, jnp.where(upper, 0, half), half)
        kept = lax.dynamic_slice_in_dim(cells, jnp.where(upper, half, 0), half)
        cells = (kept.astype(F32) + exchanged(sent, mask).astype(F32)).astype(BF16)
    cells = (cells.astype(F32) + exchanged(cells, masks[-1]).astype(F32)).astype(BF16)
    for mask in masks[-2::-1]:
        upper = (index & mask) != 0
        got = exchanged(cells, mask)
        cells = jnp.concatenate([jnp.where(upper, got, cells), jnp.where(upper, cells, got)], axis=0)
    return cells, stages


def after(array, *earlier):
    return lax.optimization_barrier((array, *earlier))[0]


def joined(*arrays):
    return lax.optimization_barrier(arrays)


def stacked(*cells):
    return jnp.concatenate([part if part.ndim == 3 else part[None] for part in cells], axis=0)


def item_index(positions, ends):
    inside = (positions >= 0) & (positions < ends[-1])
    counted = jnp.sum((positions[:, None] >= ends[None, :]).astype(jnp.int32), axis=1)
    return jnp.where(inside, counted, -1)


def call(kernel, out_shape, *args, grid=(), in_specs=None, out_specs=None, scalars=0, flops=0, scratch=()):
    whole = lambda a: pl.BlockSpec(a.shape, lambda *_, n=len(a.shape): (0,) * n)
    ins = [whole(a) if s is None else s for a, s in zip(args[scalars:], in_specs or [None] * 99)]
    outs = [whole(a) if s is None else s for a, s in zip(out_shape, out_specs or [None] * 99)]
    moved = sum(a.size * a.dtype.itemsize for a in (*args, *out_shape))
    return pl.pallas_call(
        kernel,
        out_shape=out_shape,
        grid_spec=pltpu.PrefetchScalarGridSpec(
            num_scalar_prefetch=scalars,
            grid=grid,
            in_specs=ins,
            out_specs=outs,
            scratch_shapes=list(scratch),
        ),
        compiler_params=pltpu.CompilerParams(vmem_limit_bytes=VMEM_BYTES),
        cost_estimate=pl.CostEstimate(flops=1, bytes_accessed=1, transcendentals=0),
    )(*args)


def project_kernel(unit, raw, own, turned, tokens_ref, w_ref, bias_ref, *out_refs):
    out_refs = list(out_refs)
    raw_ref = out_refs.pop(0) if raw else None
    own_ref = out_refs.pop(0) if own else None
    turned_ref = out_refs.pop(0) if turned else None
    product = dot(w_ref[0], tokens_ref[...], 1, 1) + bias_ref[...]
    size = HEAD
    for head in range(product.shape[0] // size):
        part = product[head * size : (head + 1) * size, :]
        if raw:
            raw_ref[head] = part.T
        if unit:
            part = part * lax.rsqrt(jnp.sum(part * part, axis=0, keepdims=True) + NORM_EPS)
        if turned:
            turned_ref[head * size : (head + 1) * size, :] = part.astype(BF16)
        if own:
            own_ref[head] = part.T.astype(BF16)


def square_of(half):
    root = half * lax.rsqrt(half)
    square = jnp.full_like(root, SQUARE[-1])
    for factor in SQUARE[-2::-1]:
        square = square * root + factor
    return square


def tile_of(span_ref):
    return span_ref[0] + jnp.minimum(pl.program_id(0), span_ref[1] - 1)


def held_at(far, near_ref, far_ref, group):
    return jnp.where(far, far_ref[0, group, :], near_ref[0, group, :])


def is_far(span_ref, place_ref, rows):
    return place_ref[tile_of(span_ref) // (rows // KEYS)] >= (place_ref.shape[0] - 1) // 2


def by_chunks(span_ref, rows, work):
    tile = span_ref[0] + pl.program_id(0)
    here = pl.program_id(0) < span_ref[1]
    meets = [
        (tile >= span_ref[2 + 2 * chunk]) & (tile < span_ref[3 + 2 * chunk]) for chunk in range(rows // CHUNK)
    ]
    every = functools.reduce(lambda x, y: x & y, meets)

    @pl.when(here & every)
    def _():
        work(slice(0, rows))

    for chunk, meet in enumerate(meets):

        @pl.when(here & meet & jnp.logical_not(every))
        def _(chunk=chunk):
            work(slice(chunk * CHUNK, (chunk + 1) * CHUNK))


def weights_kernel(
    span_ref, place_ref, v_place_ref, mine_ref, items_ref, own_ref, near_ref, far_ref, weight_ref, slope_ref
):
    heads, rows, size = own_ref.shape
    far = is_far(span_ref, place_ref, rows)

    def work(part):
        same = mine_ref[part, :] == items_ref[0]
        for head in range(heads):
            scores = dot(own_ref[head, part, :], held_at(far, near_ref, far_ref, slice(head * size, (head + 1) * size)))
            half = 1.0 / SHRINK - scores
            square = square_of(half)
            fourth = square * square
            weight = jnp.where(same, fourth * fourth, 0.0)
            weight_ref[0, head, part, :] = weight.astype(BF16)
            slope = weight * lax.rsqrt(square * (half * (1.0 / SHRINK + scores)))
            slope_ref[0, head, part, :] = slope.astype(BF16)

    by_chunks(span_ref, rows, work)


def unit_back(grad, raw):
    scale = lax.rsqrt(jnp.sum(raw * raw, axis=-1, keepdims=True) + NORM_EPS)
    unit = raw * scale
    return scale * (grad - unit * jnp.sum(unit * grad, axis=-1, keepdims=True))


def split_low(wide):
    high = wide.astype(BF16)
    return high, (wide - high.astype(F32)).astype(BF16)


def band_of(taps_row):
    return pltpu.roll(jnp.broadcast_to(taps_row, (EDGE, BAND)), 0, 1, stride=1, stride_axis=0)


def around_of(mine_ref, rim_ref, start):
    return mine_ref[start : start + EDGE, :] == rim_ref[:, start : start + BAND]


def band_sums(taps_ref, head, mine_ref, rim_ref, values):
    band = band_of(taps_ref[head : head + 1, :])
    out = []
    for start in range(0, mine_ref.shape[0], EDGE):
        high, low = split_low(jnp.where(around_of(mine_ref, rim_ref, start), band, 0.0))
        near = values[:, start : start + BAND]
        out.append(dot(high, near, 1, 1) + dot(low, near, 1, 1))
    return jnp.concatenate(out, axis=0)


def rim_values(v_place_ref, sides, own_ref, group):
    index, blocks, rows = v_place_ref[v_place_ref.shape[0] - 1], v_place_ref.shape[0] - 1, own_ref.shape[1]
    ends = []
    for (near_ref, far_ref), beside, part in zip(sides, (-1, 1), (slice(rows - EDGE, rows), slice(0, EDGE))):
        far = v_place_ref[jnp.clip(index + beside, 0, blocks - 1)] >= blocks // 2
        ends.append(jnp.where(far, far_ref[0, group, part], near_ref[0, group, part]))
    return jnp.concatenate([ends[0], own_ref[group, :], ends[1]], axis=1)


def attend_kernel(
    span_ref, place_ref, v_place_ref, weight_ref, v_near_ref, v_far_ref, mine_ref, rim_ref, taps_ref, own_ref,
    before_near_ref, before_far_ref, after_near_ref, after_far_ref, context_ref, raw_ref, v_rim_ref, sum_ref, conv_ref,
):
    heads, rows, size = raw_ref.shape
    far = is_far(span_ref, v_place_ref, rows)

    @pl.when(pl.program_id(0) == 0)
    def _():
        sides = ((before_near_ref, before_far_ref), (after_near_ref, after_far_ref))
        for head in range(heads):
            group = slice(head * size, (head + 1) * size)
            values = rim_values(v_place_ref, sides, own_ref, group)
            v_rim_ref[group, :] = values
            conv_ref[head] = band_sums(taps_ref, head, mine_ref, rim_ref, values)
        sum_ref[...] = jnp.zeros_like(sum_ref)

    def work(part):
        for head in range(heads):
            values = held_at(far, v_near_ref, v_far_ref, slice(head * size, (head + 1) * size))
            sum_ref[head, part, :] += dot(weight_ref[0, head, part, :], values, 1, 1)

    by_chunks(span_ref, rows, work)

    @pl.when(pl.program_id(0) == pl.num_programs(0) - 1)
    def _():
        context = []
        for head in range(heads):
            raw = sum_ref[head]
            raw_ref[head] = raw
            unit = raw * lax.rsqrt(jnp.sum(raw * raw, axis=-1, keepdims=True) + NORM_EPS)
            context.append(unit + conv_ref[head])
        context_ref[...] = jnp.concatenate(context, axis=1).astype(BF16)


def finished(grad, tokens_ref, low_ref, weight_ref, start):
    turned = grad.T.astype(BF16)
    low_ref[...] = grad.astype(BF16)
    weight_ref[start : start + turned.shape[0], :] = dot(turned, tokens_ref[...]).astype(BF16)
    return row_sum(grad.astype(BF16).astype(F32))


def query_back_kernel(
    span_ref, place_ref, v_place_ref, slope_ref, k_near_ref, k_far_ref, v_near_ref, v_far_ref, da_ref, raw_ref,
    tokens_ref, dq_ref, d_w_ref, d_b_ref, sum_ref,
):
    heads, rows, size = raw_ref.shape
    far = is_far(span_ref, place_ref, rows)
    v_far = is_far(span_ref, v_place_ref, rows)

    @pl.when(pl.program_id(0) == 0)
    def _():
        sum_ref[...] = jnp.zeros_like(sum_ref)

    def work(part):
        for head in range(heads):
            group = slice(head * size, (head + 1) * size)
            slope = slope_ref[0, head, part, :].astype(F32)
            d_weights = dot(da_ref[head, part, :], held_at(v_far, v_near_ref, v_far_ref, group))
            d_scores = (d_weights * slope).astype(BF16)
            sum_ref[head, part, :] += dot(d_scores, held_at(far, k_near_ref, k_far_ref, group), 1, 1)

    by_chunks(span_ref, rows, work)

    @pl.when(pl.program_id(0) == pl.num_programs(0) - 1)
    def _():
        grads = [unit_back(sum_ref[head] * SLOPE, raw_ref[head]) for head in range(heads)]
        bias = finished(jnp.concatenate(grads, axis=1), tokens_ref, dq_ref, d_w_ref, 0)
        d_b_ref[...] = jnp.zeros_like(d_b_ref)
        d_b_ref[0:1, : bias.shape[1]] = bias


def key_back_kernel(
    span_ref, place_ref, v_place_ref, weight_ref, slope_ref, q_near_ref, q_far_ref, da_near_ref, da_far_ref, v_ref,
    raw_ref, dv_conv_ref, d_taps_ref, d_b_q_ref, d_w_q_ref, tokens_ref, dk_ref, dv_ref, late_ref, sum_ref, value_ref,
):
    heads, rows, size = raw_ref.shape
    columns = heads * size
    far = is_far(span_ref, place_ref, rows)

    @pl.when(pl.program_id(0) == 0)
    def _():
        sum_ref[...] = jnp.zeros_like(sum_ref)
        value_ref[...] = dv_conv_ref[...]

    def work(part):
        for head in range(heads):
            group = slice(head * size, (head + 1) * size)
            d_attn = held_at(far, da_near_ref, da_far_ref, group)
            slope = slope_ref[0, head, part, :].astype(F32)
            d_scores = (dot(v_ref[head, part, :], d_attn) * slope).astype(BF16)
            sum_ref[head, part, :] += dot(d_scores, held_at(far, q_near_ref, q_far_ref, group), 1, 1)
            value_ref[head, part, :] += dot(weight_ref[0, head, part, :], d_attn, 1, 1)

    by_chunks(span_ref, rows, work)

    @pl.when(pl.program_id(0) == pl.num_programs(0) - 1)
    def _():
        more = 3 * columns
        late_ref[more:, :] = jnp.zeros((late_ref.shape[0] - more, late_ref.shape[1]), BF16)
        late_ref[:columns, :] = d_w_q_ref[...]
        grads = [unit_back(sum_ref[head] * SLOPE, raw_ref[head]) for head in range(heads)]
        finished(jnp.concatenate(grads, axis=1), tokens_ref, dk_ref, late_ref, columns)
        grads = jnp.concatenate([value_ref[head] for head in range(heads)], axis=1)
        bias = finished(grads, tokens_ref, dv_ref, late_ref, 2 * columns)
        late_ref[more : more + 2, :columns] = jnp.concatenate(
            [d_b_q_ref[0:1, :columns], bias], axis=0
        ).astype(BF16)
        late_ref[more + 16 : more + 16 + heads, : d_taps_ref.shape[1]] = d_taps_ref[...].astype(BF16)


def conv_back_kernel(mine_ref, rim_ref, taps_ref, values_ref, d_context_ref, turned_ref, dv_ref, d_taps_ref):
    heads, rows, size = d_context_ref.shape
    for head in range(heads):
        group = slice(head * size, (head + 1) * size)
        dv_ref[head] = band_sums(taps_ref, head, mine_ref, rim_ref, turned_ref[group, :])
        values = values_ref[group, :]
        lined = jnp.zeros((8, BAND), F32)
        for start in range(0, rows, EDGE):
            pairs = dot(d_context_ref[head, start : start + EDGE, :], values[:, start : start + BAND])
            pairs = jnp.where(around_of(mine_ref, rim_ref, start), pairs, 0.0)
            for row in range(0, EDGE, 8):
                part = pairs[row : row + 8, :]
                lined = lined + (pltpu.roll(part, BAND - row, 1) if row else part)
        total = lined[0:1, :]
        for row in range(1, 8):
            total = total + pltpu.roll(lined[row : row + 1, :], BAND - row, 1)
        d_taps_ref[head : head + 1, :] = total


def normal_of(u):
    density = jnp.exp(u * u * -0.5) * (1.0 / math.sqrt(2.0 * math.pi))
    ratio = 1.0 / (1.0 + TAIL_AT * jnp.abs(u))
    tail = jnp.full_like(ratio, TAIL[-1])
    for factor in TAIL[-2::-1]:
        tail = tail * ratio + factor
    tail = tail * (ratio * density)
    return jnp.where(u >= 0.0, 1.0 - tail, tail), density


def normed_of(hidden):
    center = hidden - jnp.mean(hidden, axis=-1, keepdims=True)
    scale = lax.rsqrt(jnp.mean(center * center, axis=-1, keepdims=True) + LAYER_EPS)
    return center * scale, scale


def normed_back(grad, normed, scale, gain):
    d_normed = grad * gain
    centered = d_normed - jnp.mean(d_normed, axis=-1, keepdims=True)
    return scale * (centered - normed * jnp.mean(d_normed * normed, axis=-1, keepdims=True))


def row_sum(array):
    return jnp.sum(array, axis=0, keepdims=True)


def middle_kernel(parts, *refs):
    tokens_ref, near_ref, far_ref, vectors_ref, d_out_ref, raw_ref = refs[:6]
    contexts = [half.at[i] for half in (near_ref, far_ref) for i in range(parts // 2)]
    (
        result_ref, y_low_ref, act_ref, d_second_low_ref, d_inner_ref, d_first_ref, d_first_low_ref, sums_ref,
        d_context_ref, turned_ref, da_ref, da_turned_ref,
        normed_ref, scale_ref, mixed_ref, factor_ref, out_ref, up_ref, down_ref, sem_ref,
    ) = refs[6 + 5 * parts :]
    heads, rows, size = raw_ref.shape
    columns = heads * size
    b_out, gain_one, bias_one, b_down, gain_two, bias_two = [vectors_ref[i : i + 1, :] for i in range(6)]
    chunks = [slice(start, start + MIDDLE) for start in range(0, rows, MIDDLE)]
    targets = [(out_ref, 0, out_ref.shape[1])]
    for to in (up_ref, down_ref):
        targets += [(to, start, to.shape[1] // 2) for start in (0, to.shape[1] // 2)]
    copies = [
        [
            pltpu.make_async_copy(
                refs[6 + piece * parts + part], to.at[part, start : start + count, :], sem_ref.at[piece, part]
            )
            for part in range(parts)
        ]
        for piece, (to, start, count) in enumerate(targets)
    ]
    for of in copies:
        for part in range(parts):
            of[part].start()

    for part in range(parts):
        copies[0][part].wait()
    for chunk in chunks:
        hidden = tokens_ref[chunk, :].astype(F32) + b_out
        for part in range(parts):
            hidden = hidden + dot(contexts[part][chunk, :], out_ref[part, :columns, :])
        normed, scale = normed_of(hidden)
        normed_ref[chunk, :] = normed
        scale_ref[chunk, :] = scale
        first = normed * gain_one + bias_one
        y_low_ref[chunk, :] = first.astype(BF16)
        mixed_ref[chunk, :] = first + b_down

    for part in range(parts):
        for of in copies[1:]:
            of[part].wait()
        b_up = row_sum(out_ref[part, columns : columns + 16, :].astype(F32))
        for chunk in chunks:
            inner = dot(y_low_ref[chunk, :], up_ref[part]) + b_up
            share, density = normal_of(inner)
            act = (inner * share).astype(BF16)
            factor_ref[part, chunk, :] = share + inner * density
            if part == 0:
                act_ref[chunk, :] = act
            mixed_ref[chunk, :] += dot(act, down_ref[part])

    sums = [0.0] * 7
    for chunk in chunks:
        normed, scale = normed_of(mixed_ref[chunk, :])
        result_ref[chunk, :] = (normed * gain_two + bias_two).astype(BF16)
        grad = d_out_ref[chunk, :].astype(F32)
        d_second = normed_back(grad, normed, scale, gain_two)
        d_second_low_ref[chunk, :] = d_second.astype(BF16)
        mixed_ref[chunk, :] = d_second
        for i, array in enumerate((grad * normed, grad, d_second)):
            sums[i] = sums[i] + row_sum(array)

    for part in range(parts):
        for chunk in chunks:
            d_act = dot(d_second_low_ref[chunk, :], down_ref[part], 1, 1)
            d_inner = (d_act * factor_ref[part, chunk, :]).astype(BF16)
            if part == 0:
                d_inner_ref[chunk, :] = d_inner
                sums[6] = sums[6] + row_sum(d_inner.astype(F32))
            mixed_ref[chunk, :] += dot(d_inner, up_ref[part], 1, 1)

    for chunk in chunks:
        grad = mixed_ref[chunk, :]
        normed = normed_ref[chunk, :]
        d_first = normed_back(grad, normed, scale_ref[chunk, :], gain_one)
        d_first_ref[chunk, :] = d_first
        d_first_low = d_first.astype(BF16)
        d_first_low_ref[chunk, :] = d_first_low
        for i, array in enumerate((grad * normed, grad, d_first)):
            sums[3 + i] = sums[3 + i] + row_sum(array)
        d_context = dot(d_first_low, out_ref[0, :columns, :], 1, 1).astype(BF16).astype(F32)
        turned_ref[:, chunk] = d_context.T.astype(BF16)
        grads = []
        for head in range(heads):
            grad = d_context[:, head * size : (head + 1) * size]
            d_context_ref[head, chunk, :] = grad.astype(BF16)
            grad = unit_back(grad, raw_ref[head, chunk, :])
            da_ref[head, chunk, :] = grad.astype(BF16)
            grads.append(grad)
        da_turned_ref[:, chunk] = jnp.concatenate(grads, axis=1).T.astype(BF16)
    sums_ref[...] = jnp.zeros_like(sums_ref)
    for i in range(7):
        sums_ref[i : i + 1, :] = sums[i]


def results_kernel(
    out_ref, up_ref, down_ref, late_ref, vectors_ref, d_out_ref, d_up_ref, d_down_ref, d_qkv_ref, more_ref
):
    columns = d_out_ref.shape[0]
    d_out_ref[...] = out_ref[:columns, :].astype(F32)
    vectors_ref[...] = out_ref[columns:, :].astype(F32)
    d_up_ref[...] = up_ref[...].astype(F32)
    d_down_ref[...] = down_ref[...].astype(F32)
    for i in range(3):
        d_qkv_ref[i] = late_ref[i * columns : (i + 1) * columns, :].astype(F32)
    more_ref[...] = late_ref[3 * columns :, :].astype(F32)


HEAD = 64


def per_device(
    tokens, item_lengths, w_qkv, b_qv, taps, w_out, b_out, ln1_gain, ln1_bias, w_up, b_up, w_down, b_down,
    ln2_gain, ln2_bias, d_out,
):
    rows, features = tokens.shape
    heads, kernel = taps.shape
    radius = (kernel - 1) // 2
    columns = w_qkv.shape[2]
    size = columns // heads
    hidden = w_up.shape[1]
    blocks = lax.axis_size("seq")
    total = blocks * rows
    index = lax.axis_index("seq").astype(jnp.int32)
    first_row = index * rows
    shape = jax.ShapeDtypeStruct
    heads_wide, heads_low = shape((heads, rows, size), F32), shape((heads, rows, size), BF16)
    turned_shape, row_shape = shape((columns, rows), BF16), shape((rows, columns), BF16)
    wide_shape, low_shape = shape((rows, features), F32), shape((rows, features), BF16)

    w_turned = jnp.swapaxes(w_qkv, 1, 2)
    biases = jnp.stack([b_qv[0], jnp.zeros_like(b_qv[0]), b_qv[1]])[:, :, None]

    def project(x, which, unit, outs, *flags):
        return call(
            functools.partial(project_kernel, unit, *flags), outs, x, w_turned, biases[which],
            grid=(1,),
            in_specs=[None, pl.BlockSpec((1, columns, features), lambda *_: (which, 0, 0)), None],
            flops=2 * rows * columns * features,
        )

    masks = masks_of("seq")
    v_masks = masks[-1:] + masks[:-1]
    ahead = [(i, i + 1) for i in range(blocks - 1)]
    behind = [(i + 1, i) for i in range(blocks - 1)]

    def rimmed(turned):
        return jnp.concatenate(
            [
                lax.ppermute(turned[:, rows - EDGE :], "seq", ahead), turned,
                lax.ppermute(turned[:, :EDGE], "seq", behind),
            ],
            axis=1,
        )

    reach = EDGE - radius
    banded = jnp.pad(taps, ((0, 0), (reach, BAND - reach - kernel)))
    mirrored = jnp.pad(taps[:, ::-1], ((0, 0), (reach, BAND - reach - kernel)))
    vectors = jnp.stack([b_out, ln1_gain, ln1_bias, b_down, ln2_gain, ln2_bias, b_out, b_out])

    steps = min(total, WINDOW) // KEYS
    per = rows // KEYS
    at_of = lambda i, span_ref: span_ref[0] + jnp.minimum(i, span_ref[1] - 1)
    tile_spec = pl.BlockSpec(
        (1, heads, rows, KEYS), lambda i, span_ref, *_: (jnp.minimum(i, span_ref[1] - 1), 0, 0, 0)
    )
    items_spec = pl.BlockSpec((1, 1, KEYS), lambda i, span_ref, *_: (at_of(i, span_ref), 0, 0))
    half = blocks // 2

    def halves_of(which):
        def spec(index_of):
            return pl.BlockSpec(
                (1, columns, KEYS),
                lambda i, *refs: (index_of(refs[which][at_of(i, refs[0]) // per]), 0, at_of(i, refs[0]) % per),
            )

        return [spec(lambda place: jnp.minimum(place, half - 1)), spec(lambda place: jnp.maximum(place - half, 0))]

    def side_of(beside):
        def spec(index_of):
            return pl.BlockSpec(
                (1, columns, rows),
                lambda i, *refs: (index_of(refs[2][jnp.clip(refs[2][blocks] + beside, 0, blocks - 1)]), 0, 0),
            )

        return [spec(lambda place: jnp.minimum(place, half - 1)), spec(lambda place: jnp.maximum(place - half, 0))]

    placed, v_placed = halves_of(1), halves_of(2)
    ordered = pl.BlockSpec((1, columns, KEYS), lambda i, *refs: (at_of(i, refs[0]) // per, 0, at_of(i, refs[0]) % per))
    tiles = shape((steps, heads, rows, KEYS), BF16)
    sums = pltpu.VMEM((heads, rows, size), F32)
    pair_flops = 2 * rows * (total // 2) * columns

    def tables(item_lengths):
        count = item_lengths.shape[0]
        upto = jnp.arange(count)[None, :] <= jnp.arange(count)[:, None]
        ends = jnp.sum(jnp.where(upto, item_lengths[None, :], 0), axis=1)
        starts = first_row + CHUNK * jnp.arange(rows // CHUNK, dtype=jnp.int32)[:, None]
        lows = jnp.max(jnp.where(ends[None, :] <= starts, ends[None, :], 0), axis=1)
        highs = jnp.min(jnp.where(ends[None, :] >= starts + CHUNK, ends[None, :], total), axis=1)
        bounds = jnp.stack([lows // KEYS, (highs + KEYS - 1) // KEYS], axis=1)
        span = jnp.concatenate(
            [jnp.stack([bounds[0, 0], bounds[-1, 1] - bounds[0, 0]]), bounds.reshape(-1)]
        ).astype(jnp.int32)
        items = item_index(jnp.arange(total, dtype=jnp.int32), ends).reshape(total // KEYS, 1, KEYS)
        rim = item_index(first_row - EDGE + jnp.arange(rows + 2 * EDGE, dtype=jnp.int32), ends)[None, :]
        mine = item_index(first_row + jnp.arange(rows, dtype=jnp.int32), ends)[:, None]
        place, v_place = [jnp.concatenate([block_places("seq", order), index[None]]) for order in (masks, v_masks)]
        return (span, place, v_place), items, rim, mine, banded, mirrored, vectors

    [k_turned] = project(tokens, 1, True, [turned_shape], False, False, True)
    k_got = flipped(k_turned, "seq", masks[0])
    v_own, v_turned = project(after(tokens, k_turned), 2, False, [heads_low, turned_shape], False, True, True)
    v_got = flipped(v_turned, "seq", v_masks[0])
    far, close = masks_of("mp")
    b_high = lax.reduce_precision(b_up, 8, 7)
    b_mid = lax.reduce_precision(b_up - b_high, 8, 7)
    b_split = jnp.stack([b_high, b_mid, b_up - b_high - b_mid]).astype(BF16)
    w_out_more = jnp.concatenate([w_out, b_split, jnp.zeros((13, features), BF16)])
    up_half, down_half = w_up.shape[0] // 2, w_down.shape[0] // 2
    own = [w_out_more, w_up[:up_half], w_up[up_half:], w_down[:down_half], w_down[down_half:]]
    far_got, close_got, last_got = [], [], []
    k_got, v_got, late_tokens, own[0], own[1] = joined(k_got, v_got, tokens, own[0], own[1])
    far_got.append(flipped(own[0], "mp", far))
    k_cells = stacked(k_turned, k_got)
    v_cells = stacked(v_turned, v_got)
    for mask in masks[1:-1]:
        k_got = flipped(k_cells, "seq", mask)
        q_raw, q_own, q_turned = project(late_tokens, 0, True, [heads_wide, heads_low, turned_shape], True, True, True)
        k_raw, k_own = project(late_tokens, 1, True, [heads_wide, heads_low], True, True, False)
        if mask == masks[1]:
            far_got.append(flipped(own[1], "mp", far))
        k_got, q_own, k_own, v_cells, late_lengths, far_got[0], far_got[1], own[2] = joined(
            k_got, q_own, k_own, v_cells, item_lengths, far_got[0], far_got[1], own[2]
        )
        k_cells = stacked(k_cells, k_got)
    k_got = flipped(k_cells, "seq", masks[-1])
    for mask in v_masks[1:-1]:
        v_got = flipped(v_cells, "seq", mask)
        v_got, v_before = joined(v_got, v_cells)
        v_cells = stacked(v_before, v_got)
    scalars, items, rim, mine, banded, mirrored, vectors = tables(late_lengths)
    far_got.append(flipped(own[2], "mp", far))
    last_got += [flipped(far_got[0], "mp", close), flipped(far_got[1], "mp", close)]
    close_got = [flipped(after(array, q_own), "mp", close) for array in own]
    k_got, v_cells, mine, items, rim, vectors, close_got, far_got[2], last_got, own[3] = joined(
        k_got, v_cells, mine, items, rim, vectors, close_got, far_got[2], last_got, own[3]
    )
    v_got = flipped(v_cells, "seq", v_masks[-1])
    keys = (k_cells, k_got)
    weights, slopes = call(
        weights_kernel, [tiles, tiles], *scalars, mine, items, q_own, *keys,
        grid=(steps,), scalars=3,
        in_specs=[None, items_spec, None, *placed],
        out_specs=[tile_spec, tile_spec],
        flops=8 * pair_flops,
    )
    far_got.append(flipped(own[3], "mp", far))
    last_got.append(flipped(far_got[2], "mp", close))
    v_got, weights, q_turned, far_got[3], last_got[2], own[4] = joined(
        v_got, weights, q_turned, far_got[3], last_got[2], own[4]
    )
    values = (v_cells, v_got)
    far_got.append(flipped(own[4], "mp", far))
    last_got.append(flipped(far_got[3], "mp", close))
    q_got = flipped(q_turned, "seq", masks[0])
    context, attended, v_rim = call(
        attend_kernel, [row_shape, heads_wide, shape((columns, rows + 2 * EDGE), BF16)],
        *scalars, weights, *values, mine, rim, banded, v_turned, *values, *values,
        grid=(steps,), scalars=3,
        in_specs=[tile_spec, *v_placed, None, None, None, None, *side_of(-1), *side_of(1)],
        flops=pair_flops, scratch=[sums, sums],
    )
    q_got, context, far_got[4], last_got[3] = joined(q_got, context, far_got[4], last_got[3])
    q_cells = stacked(q_turned, q_got)
    for mask in masks[1:-1]:
        q_got = flipped(q_cells, "seq", mask)
        q_cells, q_got = joined(q_cells, q_got)
        q_cells = stacked(q_cells, q_got)
    context_got = flipped(context, "mp", far)
    last_got.append(flipped(far_got[4], "mp", close))
    parts = 4
    held = [kind[piece] for piece in range(len(own)) for kind in (own, far_got, close_got, last_got)]
    context_got, q_cells, held = joined(context_got, q_cells, held)
    context_cells = stacked(context, context_got)
    contexts = (context_cells, flipped(context_cells, "mp", close))
    q_got = flipped(q_cells, "seq", masks[-1])

    vmem = lambda a, *lead: pltpu.VMEM((*lead, *a.shape), a.dtype)
    anywhere = pl.BlockSpec(memory_space=pl.ANY)
    hidden_shape = shape((rows, hidden), BF16)
    (
        layer_output, first_low, act_own, d_second_low, d_inner_own, d_first, d_first_low, vector_sums,
        d_context, d_context_turned, da_own, da_turned,
    ) = call(
        functools.partial(middle_kernel, parts),
        [
            low_shape, low_shape, hidden_shape, low_shape, hidden_shape, wide_shape, low_shape,
            shape((16, features), F32), heads_low, turned_shape, heads_low, turned_shape,
        ],
        tokens, *contexts, vectors, d_out, attended, *held,
        grid=(1,),
        in_specs=[None] * 6 + [anywhere] * len(held),
        flops=8 * rows * parts * w_up.size,
        scratch=[
            pltpu.VMEM((rows, features), F32), pltpu.VMEM((rows, 1), F32), pltpu.VMEM((rows, features), F32),
            pltpu.VMEM((parts, rows, hidden), F32), pltpu.VMEM((parts, columns + 16, features), BF16), vmem(w_up, parts), vmem(w_down, parts),
            pltpu.SemaphoreType.DMA((len(own), parts)),
        ],
    )
    d_w_down = jnp.einsum("tf,td->fd", act_own, d_second_low, preferred_element_type=F32).astype(BF16)
    d_w_up = jnp.einsum("td,tf->df", first_low, d_inner_own, preferred_element_type=F32).astype(BF16)
    d_w_out = jnp.einsum("tc,td->cd", context, d_first_low, preferred_element_type=F32).astype(BF16)

    early = lax.psum((jnp.concatenate([d_w_out, vector_sums.astype(BF16)]), d_w_up, d_w_down), "seq")
    da_got = flipped(da_turned, "seq", masks[0])
    da_got, d_w_up, d_w_down, d_w_out, q_got, da_own, d_context_turned = joined(
        da_got, d_w_up, d_w_down, d_w_out, q_got, da_own, d_context_turned
    )
    context_rim = rimmed(d_context_turned)
    queries = (q_cells, q_got)
    da_cells = stacked(da_turned, da_got)
    [dq, d_w_q, d_b_q] = call(
        query_back_kernel, [row_shape, shape((columns, features), BF16), shape((16, features), F32)],
        *scalars, slopes, *keys, *values, da_own, q_raw, tokens,
        grid=(steps,), scalars=3,
        in_specs=[tile_spec, *placed, *v_placed, None, None, None],
        flops=3 * pair_flops, scratch=[sums],
    )
    for mask in masks[1:-1]:
        da_got = flipped(da_cells, "seq", mask)
        da_got, dq, context_rim, k_own = joined(da_got, dq, context_rim, k_own)
        da_cells = stacked(da_cells, da_got)
    da_got = flipped(da_cells, "seq", masks[-1])
    weights_back, slopes_back = call(
        weights_kernel, [tiles, tiles], *scalars, mine, items, k_own, *queries,
        grid=(steps,), scalars=3,
        in_specs=[None, items_spec, None, *placed],
        out_specs=[tile_spec, tile_spec],
        flops=8 * pair_flops,
    )
    dv_conv, d_taps_wide = call(
        conv_back_kernel, [heads_wide, shape((heads, BAND), F32)],
        mine, rim, mirrored, v_rim, d_context, context_rim,
        grid=(1,),
        flops=2 * rows * BAND * columns,
    )
    d_attended = (da_cells, da_got)
    dk, dv, late = call(
        key_back_kernel, [row_shape, row_shape, shape((3 * columns + 64, features), BF16)],
        *scalars, weights_back, slopes_back, *queries, *d_attended, v_own, k_raw, dv_conv, d_taps_wide, d_b_q, d_w_q, tokens,
        grid=(steps,), scalars=3,
        in_specs=[tile_spec, tile_spec, *placed, *placed] + [None] * 7,
        flops=4 * pair_flops, scratch=[sums, sums],
    )
    late_sum, late_stages = all_sum(late, "seq")
    d_tokens_part = sum(
        jnp.dot(part, w_turned[i], preferred_element_type=F32) for i, part in enumerate((dq, dk, dv))
    )
    d_tokens = (d_first + all_sum(d_tokens_part.astype(BF16), "mp")[0].astype(F32)).astype(BF16)
    out_and_vectors, d_w_up, d_w_down = lax.optimization_barrier((late_stages[-1], *early))[1:]
    vectors, d_w_out, d_w_up, d_w_down, d_w_qkv, more = call(
        results_kernel,
        [
            shape((16, features), F32), shape(w_out.shape, F32), shape(w_up.shape, F32), shape(w_down.shape, F32),
            shape((3, columns, features), F32), shape((64, features), F32),
        ],
        out_and_vectors, d_w_up, d_w_down, late_sum,
        grid=(1,),
    )
    d_ln2_gain, d_ln2_bias, d_b_down, d_ln1_gain, d_ln1_bias, d_b_out, d_b_up = [vectors[i] for i in range(7)]
    d_b_qv, d_taps = more[:2, :columns], more[16 : 16 + heads, reach : reach + kernel]
    return (
        layer_output, d_tokens, jnp.swapaxes(d_w_qkv, 1, 2), d_b_qv, d_taps, d_w_out, d_b_out, d_ln1_gain,
        d_ln1_bias, d_w_up, d_b_up, d_w_down, d_b_down, d_ln2_gain, d_ln2_bias,
    )


def solution(mesh):
    placed = (
        P("seq", None), P(), P(None, None, "mp"), P(None, "mp"), P("mp", None), P("mp", None), P(), P(), P(),
        P(None, "mp"), P("mp"), P("mp", None), P(), P(), P(), P("seq", None),
    )
    given = (
        P("seq", None), P("seq", None), P(None, None, "mp"), P(None, "mp"), P("mp", None), P("mp", None), P(),
        P(), P(), P(None, "mp"), P("mp"), P("mp", None), P(), P(), P(),
    )
    return jax.shard_map(per_device, mesh=mesh, in_specs=placed, out_specs=given, check_vma=False)
```

time: 961 us -> 349 us (0.36)
  matrix products: 353 us -> 7.49 us
  waiting for transfers between devices: 387 us -> 116 us
  Pallas kernels: 0 us -> 94.1 us
  other arithmetic: 82.8 us -> 13.4 us
  starting transfers between devices: 11.1 us -> 75.7 us
  local copies, waits for them, and re-layouts: 59.3 us -> 19.4 us
  blocking collectives: 34.6 us -> 0 us
  loops' own time: 12.2 us -> 0 us
    dot_general x36 -> x6, matrix products: 353 us -> 7.49 us  [the longest x1 3.31 us: per_device(): jnp.einsum('tf,td->fd', act_own, d_second_low, preferred_element_type=F32)]
    psum x5 -> x1, waiting for transfers between devices: 245 us -> 32.9 us  [per_device(): lax.psum((jnp.concatenate([d_w_out, vector_sums.astype(BF16)]), d_w_up, d...]
    all_gather x2 -> x0, waiting for transfers between devices: 138 us -> none  [the longest x1 85.7 us: per_device(): lax.all_gather(both_packed, 'seq', axis=0, tiled=True)]
    pallas_call x0 -> x12, Pallas kernels: none -> 94.1 us  [call(): pl.pallas_call(kernel, out_shape=out_shape, grid_spec=pltpu.PrefetchScala...]
    ppermute x4 -> x39, waiting for transfers between devices: 3.83 us -> 83.5 us  [the longest x37 83.5 us: flipped(): lax.ppermute(cells, axis, [(i, i ^ mask) for i in range(lax.axis_size(axi...]
    ppermute x4 -> x39, starting transfers between devices: 10.8 us -> 75.7 us  [the longest x37 70.7 us: flipped(): lax.ppermute(cells, axis, [(i, i ^ mask) for i in range(lax.axis_size(axi...]
    psum x1 -> x0, blocking collectives: 34.6 us -> none  [per_device(): lax.psum(d_b_qv.astype(jnp.bfloat16), 'seq').astype(jnp.float32)]
    convert_element_type x31 -> x7, other arithmetic: 32.2 us -> 1.52 us  [the longest x1 1.05 us: per_device(): (d_first + all_sum(d_tokens_part.astype(BF16), 'mp')[0].astype(F32)).asty...]
  transfers between devices with their start and end apart: 11 -> 40, of which waited for: 7 -> 13; matrix products, arithmetic and copies ran while one was open for 4% -> 9% of each run, Pallas kernels for 0% -> 25%
where the time goes in v2:
time: 349 us; the launch traced here: 342 us
  waiting for transfers between devices  116 us (33%)
  Pallas kernels  94.1 us (27%)
  starting transfers between devices  75.7 us (22%)
  local copies, waits for them, and re-layouts  19.4 us (6%)
  between operations  15.9 us (5%)
  other arithmetic  13.4 us (4%)
  matrix products  7.49 us (2%)
    pallas_call x12, Pallas kernels, call(): pl.pallas_call(kernel, out_shape=out_shape, grid_spec=pltpu.PrefetchScala...  94.1 us
    ppermute x37, waiting for transfers between devices, flipped(): lax.ppermute(cells, axis, [(i, i ^ mask) for i in range(lax.axis_size(axi...  83.5 us
    ppermute x37, starting transfers between devices, flipped(): lax.ppermute(cells, axis, [(i, i ^ mask) for i in range(lax.axis_size(axi...  70.7 us
    psum x1, waiting for transfers between devices, per_device(): lax.psum((jnp.concatenate([d_w_out, vector_sums.astype(BF16)]), d_w_up, d...  32.9 us
  transfers between devices with their start and end apart: 40, of which 13 were waited for; matrix products, arithmetic and copies ran while one was open for 9% of the time, Pallas kernels for 25%

profile of v2, /device:TPU:0, one launch (start us, length us, event | category | flops | bytes accessed | tf_op | source)
XLA Modules:
  0.0 342.4 jit_solution(9649223267503009023)
XLA Ops:
  7.9 2.4 shard_map.271
  10.3 4.0 %collective-permute-start = (bf16[192,512]{1,0:T(8,128)(2,1)}, bf16[192,512]{1,0:T(8,128)(2,1)S(1)}, u32[]{:S(2)}, u32[]{:S(2)}) collective-permute-start(bf16[192,512]{1,0:T(8,128)(2,1)} %shard_map.271), channel_id=1, source_target_pairs={{0,16},{4,20},{8,24},{12,28},{16,0},{20,4},{24,8},{28,12},{1,17},{... | collective-permute-start | bytes 589832 | tf_op jit(solution)/shard_map/ppermute | solution.py:46
  14.3 0.8 copy.36.bias_ref
  15.1 2.5 shard_map.272
  17.6 1.5 collective-permute-start.1
  20.2 1.5 fusion.11
  21.7 2.5 collective-permute-done.1
  24.2 1.6 collective-permute-start.4
  25.8 1.6 collective-permute-start.2
  30.1 2.4 fusion.10
  32.4 3.0 shard_map.274
  35.4 3.0 shard_map.273
  38.5 6.5 %collective-permute-done.3.refs_7_ = bf16[208,768]{1,0:T(8,128)(2,1)S(1)} collective-permute-done((bf16[208,768]{1,0:T(8,128)(2,1)S(1)}, bf16[208,768]{1,0:T(8,128)(2,1)S(1)}, u32[]{:S(2)}, u32[]{:S(2)}) %collective-permute-start.3) | collective-permute-done | bytes 319520 | tf_op jit(solution)/shard_map/ppermute | solution.py:46
  46.5 1.2 pad_maximum_fusion.1.near_ref.k_near_ref
  49.4 1.2 and_select_fusion.rim_ref
  50.7 1.3 collective-permute-start.5
  51.9 1.3 compare_select_fusion.items_ref
  53.2 1.6 collective-permute-start.12
  54.7 11.7 %collective-permute-done.6 = bf16[2,192,512]{2,1,0:T(8,128)(2,1)S(1)} collective-permute-done((bf16[2,192,512]{2,1,0:T(8,128)(2,1)S(1)}, bf16[2,192,512]{2,1,0:T(8,128)(2,1)S(1)}, u32[]{:S(2)}, u32[]{:S(2)}) %collective-permute-start.6) | collective-permute-done | bytes 393248 | tf_op jit(solution)/shard_map/ppermute | solution.py:46
  67.7 1.4 fusion.6.mine_ref
  69.1 1.1 pad_maximum_fusion.2.v_near_ref.before_near_ref.after_near_ref
  70.3 0.9 copy-done.27
  71.3 3.5 %collective-permute-start.15 = (bf16[4,192,512]{2,1,0:T(8,128)(2,1)S(1)}, bf16[4,192,512]{2,1,0:T(8,128)(2,1)S(1)}, u32[]{:S(2)}, u32[]{:S(2)}) collective-permute-start(bf16[4,192,512]{2,1,0:T(8,128)(2,1)S(1)} %pad_maximum_fusion.2.v_near_ref.before_near_ref.after_near_ref), channel_id=1, source_target_pairs={{0,8},{4,12},{8,0},{12,4},{16,24},{20,28},{24,16},{28,20},{1,9},{5... | collective-permute-start | bytes 2359304 | tf_op jit(solution)/shard_map/ppermute | solution.py:46
  74.8 1.6 collective-permute-start.16
  78.5 9.1 %shard_map.275 = (bf16[16,3,512,256]{3,2,1,0:T(8,128)(2,1)}, bf16[16,3,512,256]{3,2,1,0:T(8,128)(2,1)}) custom-call(s32[6]{0:T(128)} %pad_add_fusion.1.span_ref, s32[9]{0:T(128)} %pad_add_fusion.2.place_ref, s32[9]{0:T(128)} %pad_add_fusion.3.v_place_ref, s32[512,1]{1,0:T(8,128)} %fusion.6.mine_ref, s32[16,1,256]{2,1,0:T(1,128)} %compare_select_fusion.items_ref, ...), custom_call_target="tpu_custom_call" | custom-call | flops 1 | bytes 1 | tf_op jit(solution)/shard_map/pallas_call | solution.py:109
  87.6 2.2 collective-permute-done.16.refs_19_
  89.8 2.4 collective-permute-done.15.v_far_ref.before_far_ref.after_far_ref
  92.2 1.5 collective-permute-start.19
  93.7 4.6 %collective-permute-start.18 = (bf16[192,512]{1,0:T(8,128)(2,1)}, bf16[192,512]{1,0:T(8,128)(2,1)S(1)}, u32[]{:S(2)}, u32[]{:S(2)}) collective-permute-start(bf16[192,512]{1,0:T(8,128)(2,1)} %get-tuple-element.167), channel_id=1, source_target_pairs={{0,16},{4,20},{8,24},{12,28},{16,0},{20,4},{24,8},{28,12},{1,17},{... | collective-permute-start | bytes 589832 | tf_op jit(solution)/shard_map/ppermute | solution.py:46
  98.9 9.7 %shard_map.276 = (bf16[512,192]{1,0:T(8,128)(2,1)}, f32[3,512,64]{2,1,0:T(8,128)}, bf16[192,768]{1,0:T(8,128)(2,1)}) custom-call(s32[6]{0:T(128)} %pad_add_fusion.1.span_ref, s32[9]{0:T(128)} %pad_add_fusion.2.place_ref, s32[9]{0:T(128)} %pad_add_fusion.3.v_place_ref, bf16[16,3,512,256]{3,2,1,0:T(8,128)(2,1)} %get-tuple-element.168.weight_ref, ...), custom_call_target="tpu_custom_call" | custom-call | flops 1 | bytes 1 | tf_op jit(solution)/shard_map/pallas_call | solution.py:109
  109.4 1.5 collective-permute-start.21
  110.9 9.5 %collective-permute-done.22 = bf16[2,192,512]{2,1,0:T(8,128)(2,1)S(1)} collective-permute-done((bf16[2,192,512]{2,1,0:T(8,128)(2,1)S(1)}, bf16[2,192,512]{2,1,0:T(8,128)(2,1)S(1)}, u32[]{:S(2)}, u32[]{:S(2)}) %collective-permute-start.22) | collective-permute-done | bytes 393248 | tf_op jit(solution)/shard_map/ppermute | solution.py:46
  120.7 8.1 %collective-permute-start.26 = (bf16[4,192,512]{2,1,0:T(8,128)(2,1)S(1)}, bf16[4,192,512]{2,1,0:T(8,128)(2,1)S(1)}, u32[]{:S(2)}, u32[]{:S(2)}) collective-permute-start(bf16[4,192,512]{2,1,0:T(8,128)(2,1)S(1)} %pad_maximum_fusion.3.near_ref.q_near_ref), channel_id=1, source_target_pairs={{0,4},{4,0},{8,12},{12,8},{16,20},{20,16},{24,28},{28,24},{1,5},{5... | collective-permute-start | bytes 2359304 | tf_op jit(solution)/shard_map/ppermute | solution.py:46
  128.8 0.8 copy-done.31
  129.6 24.5 %shard_map.277 = (bf16[512,768]{1,0:T(8,128)(2,1)}, bf16[512,768]{1,0:T(8,128)(2,1)}, bf16[512,768]{1,0:T(8,128)(2,1)}, bf16[512,768]{1,0:T(8,128)(2,1)}, bf16[5...) custom-call(bf16[512,768]{1,0:T(8,128)(2,1)} %tokens_ref.8, ...), custom_call_target="tpu_custom_call" | custom-call | flops 1 | bytes 1 | tf_op jit(solution)/shard_map/pallas_call | solution.py:109
  154.2 1.4 collective-permute-start.25
  155.6 3.3 convolution_convert_fusion
  158.9 1.8 convolution_convert_fusion.1
  161.1 5.5 %collective-permute-done.25 = bf16[192,512]{1,0:T(8,128)(2,1)S(1)} collective-permute-done((bf16[192,512]{1,0:T(8,128)(2,1)}, bf16[192,512]{1,0:T(8,128)(2,1)S(1)}, u32[]{:S(2)}, u32[]{:S(2)}) %collective-permute-start.25) | collective-permute-done | bytes 196640 | tf_op jit(solution)/shard_map/ppermute | solution.py:46
  166.7 3.7 %collective-permute-start.28 = (bf16[192,128]{1,0:T(8,128)(2,1)S(1)}, bf16[192,128]{1,0:T(8,128)(2,1)S(1)}, u32[]{:S(2)}, u32[]{:S(2)}) collective-permute-start(bf16[192,128]{1,0:T(8,128)(2,1)S(1)} %get-tuple-element.279), channel_id=1, source_target_pairs={{0,4},{4,8},{8,12},{12,16},{16,20},{20,24},{24,28},{1,5},{5,9},{9,... | collective-permute-start | bytes 147464 | tf_op jit(solution)/shard_map/ppermute | solution.py:549
  170.4 1.3 collective-permute-start.29
  171.7 9.4 %shard_map.278 = (bf16[512,192]{1,0:T(8,128)(2,1)}, bf16[192,768]{1,0:T(8,128)(2,1)}, f32[16,768]{1,0:T(8,128)}) custom-call(s32[6]{0:T(128)} %pad_add_fusion.1.span_ref, s32[9]{0:T(128)} %pad_add_fusion.2.place_ref, s32[9]{0:T(128)} %pad_add_fusion.3.v_place_ref, bf16[16,3,512,256]{3,2,1,0:T(8,128)(2,1)} %get-tuple-element.223.slope_ref, ...), custom_call_target="tpu_custom_call" | custom-call | flops 1 | bytes 1 | tf_op jit(solution)/shard_map/pallas_call | solution.py:109
  182.0 4.7 %collective-permute-start.30 = (bf16[4,192,512]{2,1,0:T(8,128)(2,1)S(1)}, bf16[4,192,512]{2,1,0:T(8,128)(2,1)S(1)}, u32[]{:S(2)}, u32[]{:S(2)}) collective-permute-start(bf16[4,192,512]{2,1,0:T(8,128)(2,1)S(1)} %pad_maximum_fusion.4.da_near_ref), channel_id=1, source_target_pairs={{0,4},{4,0},{8,12},{12,8},{16,20},{20,16},{24,28},{28,24},{1,5},{5... | collective-permute-start | bytes 2359304 | tf_op jit(solution)/shard_map/ppermute | solution.py:46
  188.3 9.3 %shard_map.279 = (bf16[16,3,512,256]{3,2,1,0:T(8,128)(2,1)}, bf16[16,3,512,256]{3,2,1,0:T(8,128)(2,1)}) custom-call(s32[6]{0:T(128)} %pad_add_fusion.1.span_ref, s32[9]{0:T(128)} %pad_add_fusion.2.place_ref, s32[9]{0:T(128)} %pad_add_fusion.3.v_place_ref, s32[512,1]{1,0:T(8,128)} %fusion.6.mine_ref, s32[16,1,256]{2,1,0:T(1,128)} %compare_select_fusion.items_ref, ...), custom_call_target="tpu_custom_call" | custom-call | flops 1 | bytes 1 | tf_op jit(solution)/shard_map/pallas_call | solution.py:109
  197.6 4.3 %shard_map.280 = (f32[3,512,64]{2,1,0:T(8,128)}, f32[3,384]{1,0:T(4,128)}) custom-call(s32[512,1]{1,0:T(8,128)} %fusion.6.mine_ref, s32[1,768]{1,0:T(1,128)} %and_select_fusion.rim_ref, f32[3,384]{1,0:T(4,128)} %pad.8.taps_ref, bf16[192,768]{1,0:T(8,128)(2,1)} %get-tuple-element.237.values_ref, bf16[3,512,64]{2,1,0:T(8,128)(2,1)} %get-tuple-element.238.d_context_ref, ...), custom_call_target="tpu_custom_call" | custom-call | flops 1 | bytes 1 | tf_op jit(solution)/shard_map/pallas_call | solution.py:109
  202.2 7.2 %collective-permute-done.30.da_far_ref = bf16[4,192,512]{2,1,0:T(8,128)(2,1)S(1)} collective-permute-done((bf16[4,192,512]{2,1,0:T(8,128)(2,1)S(1)}, bf16[4,192,512]{2,1,0:T(8,128)(2,1)S(1)}, u32[]{:S(2)}, u32[]{:S(2)}) %collective-permute-start.30) | collective-permute-done | bytes 786464 | tf_op jit(solution)/shard_map/ppermute | solution.py:46
  209.4 0.9 copy-done.21
  210.3 11.9 %shard_map.281 = (bf16[512,192]{1,0:T(8,128)(2,1)}, bf16[512,192]{1,0:T(8,128)(2,1)}, bf16[640,768]{1,0:T(8,128)(2,1)}) custom-call(s32[6]{0:T(128)} %pad_add_fusion.1.span_ref, s32[9]{0:T(128)} %pad_add_fusion.2.place_ref, s32[9]{0:T(128)} %pad_add_fusion.3.v_place_ref, bf16[16,3,512,256]{3,2,1,0:T(8,128)(2,1)} %get-tuple-element.232.weight_ref, ...), custom_call_target="tpu_custom_call" | custom-call | flops 1 | bytes 1 | tf_op jit(solution)/shard_map/pallas_call | solution.py:109
  222.3 1.1 constant_dynamic-slice_fusion.1
  223.4 5.2 %collective-permute-start.34 = (bf16[320,768]{1,0:T(8,128)(2,1)S(1)}, bf16[320,768]{1,0:T(8,128)(2,1)S(1)}, u32[]{:S(2)}, u32[]{:S(2)}) collective-permute-start(bf16[320,768]{1,0:T(8,128)(2,1)S(1)} %constant_dynamic-slice_fusion.1), channel_id=1, source_target_pairs={{0,4},{4,0},{8,12},{12,8},{16,20},{20,16},{24,28},{28,24},{1,5},{5... | collective-permute-start | bytes 1474568 | tf_op jit(solution)/shard_map/ppermute | solution.py:46
  228.7 1.3 fusion.1
  230.3 5.1 %collective-permute-done.34 = bf16[320,768]{1,0:T(8,128)(2,1)S(1)} collective-permute-done((bf16[320,768]{1,0:T(8,128)(2,1)S(1)}, bf16[320,768]{1,0:T(8,128)(2,1)S(1)}, u32[]{:S(2)}, u32[]{:S(2)}) %collective-permute-start.34) | collective-permute-done | bytes 491552 | tf_op jit(solution)/shard_map/ppermute | solution.py:46
  235.6 21.9 %collective-permute-start.35 = (bf16[160,768]{1,0:T(8,128)(2,1)S(1)}, bf16[160,768]{1,0:T(8,128)(2,1)S(1)}, u32[]{:S(2)}, u32[]{:S(2)}) collective-permute-start(bf16[160,768]{1,0:T(8,128)(2,1)S(1)} %constant_dynamic-slice_fusion), channel_id=1, source_target_pairs={{0,8},{4,12},{8,0},{12,4},{16,24},{20,28},{24,16},{28,20},{1,9},{5... | collective-permute-start | bytes 737288 | tf_op jit(solution)/shard_map/ppermute | solution.py:46
  257.7 5.5 %collective-permute-done.35 = bf16[160,768]{1,0:T(8,128)(2,1)S(1)} collective-permute-done((bf16[160,768]{1,0:T(8,128)(2,1)S(1)}, bf16[160,768]{1,0:T(8,128)(2,1)S(1)}, u32[]{:S(2)}, u32[]{:S(2)}) %collective-permute-start.35) | collective-permute-done | bytes 245792 | tf_op jit(solution)/shard_map/ppermute | solution.py:46
  263.4 1.5 collective-permute-start.32
  265.0 18.6 %collective-permute-done.36 = bf16[160,768]{1,0:T(8,128)(2,1)S(1)} collective-permute-done((bf16[160,768]{1,0:T(8,128)(2,1)S(1)}, bf16[160,768]{1,0:T(8,128)(2,1)S(1)}, u32[]{:S(2)}, u32[]{:S(2)}) %collective-permute-start.36) | collective-permute-done | bytes 245792 | tf_op jit(solution)/shard_map/ppermute | solution.py:46
  283.9 6.7 %collective-permute-done.37 = bf16[160,768]{1,0:T(8,128)(2,1)S(1)} collective-permute-done((bf16[160,768]{1,0:T(8,128)(2,1)S(1)}, bf16[160,768]{1,0:T(8,128)(2,1)S(1)}, u32[]{:S(2)}, u32[]{:S(2)}) %collective-permute-start.37) | collective-permute-done | bytes 245792 | tf_op jit(solution)/shard_map/ppermute | solution.py:46
  290.9 1.0 add_convert_fusion
  292.0 32.9 %all-reduce.5.cloned.1.call-done = (bf16[208,768]{1,0:T(8,128)(2,1)}, bf16[768,768]{1,0:T(8,128)(2,1)}, bf16[768,768]{1,0:T(8,128)(2,1)}) async-done(((bf16[208,768]{1,0:T(8,128)(2,1)}, bf16[768,768]{1,0:T(8,128)(2,1)}, bf16[768,768]{1,0:T(8,128)(2,1)}), (bf16[208,768]{1,0:T(8,128)(2,1)}, bf16[768,768]{1,0:T(8,128)(2,1)}, bf16[768,768]{1,0:T(8,128)(2,1)})) %all-reduce.5.cloned.1.call-update) | async-done | bytes 2678800 | tf_op jit(solution)/shard_map/psum | solution.py:714
  325.0 1.0 pad_maximum_fusion.late_ref
  326.1 5.0 %shard_map.282 = (f32[16,768]{1,0:T(8,128)}, f32[192,768]{1,0:T(8,128)}, f32[768,768]{1,0:T(8,128)}, f32[768,768]{1,0:T(8,128)}, f32[3,192,768]{2,1,0:T(8,128)}, /*index=5*/f32[64,768]{1,0:T(8,128)}) custom-call(bf16[208,768]{1,0:T(8,128)(2,1)} %get-tuple-element.248.out_ref, bf16[768,768]{1,0:T(8,128)(2,1)} %get-tuple-element.249.up_ref, ...), custom_call_target="tpu_custom_call" | custom-call | flops 1 | bytes 1 | tf_op jit(solution)/shard_map/pallas_call | solution.py:109
  331.1 1.3 slice.95
  332.3 1.3 slice.96
  333.7 1.7 slice_reduce_fusion
  (228 shorter events, 16.8 us)
Async XLA Ops:
  7.2 317.7 %all-reduce.5.cloned.1.call-start = ((), (), s32[]{:S(2)}) async-start(), calls=%async_computation | async-start | bytes 5357568 | tf_op jit(solution)/shard_map/psum | solution.py:714
  7.9 11.3 %copy-start.51 = (f32[768]{0:T(1024)S(1)}, f32[768]{0:T(1024)}, u32[]{:S(2)}) copy-start(f32[768]{0:T(1024)} %param.26) | copy-start | bytes 9220
  7.9 11.9 %copy-start.37 = (bf16[192,768]{1,0:T(8,128)(2,1)S(1)}, bf16[192,768]{1,0:T(8,128)(2,1)}, u32[]{:S(2)}) copy-start(bf16[192,768]{1,0:T(8,128)(2,1)} %param.21) | copy-start | bytes 884740
  10.3 13.9 %collective-permute-start = (bf16[192,512]{1,0:T(8,128)(2,1)}, bf16[192,512]{1,0:T(8,128)(2,1)S(1)}, u32[]{:S(2)}, u32[]{:S(2)}) collective-permute-start(bf16[192,512]{1,0:T(8,128)(2,1)} %shard_map.271), channel_id=1, source_target_pairs={{0,16},{4,20},{8,24},{12,28},{16,0},{20,4},{24,8},{28,12},{1,17},{... | collective-permute-start | bytes 589832 | tf_op jit(solution)/shard_map/ppermute | solution.py:46
  17.6 6.6 %collective-permute-start.1 = (bf16[192,512]{1,0:T(8,128)(2,1)}, bf16[192,512]{1,0:T(8,128)(2,1)S(1)}, u32[]{:S(2)}, u32[]{:S(2)}) collective-permute-start(bf16[192,512]{1,0:T(8,128)(2,1)} %get-tuple-element.137.own_ref), channel_id=1, source_target_pairs={{0,4},{4,0},{8,12},{12,8},{16,20},{20,16},{24,28},{28,24},{1,5},{5... | collective-permute-start | bytes 589832 | tf_op jit(solution)/shard_map/ppermute | solution.py:46
  20.1 27.7 %copy-start.14 = (bf16[208,768]{1,0:T(8,128)(2,1)}, bf16[208,768]{1,0:T(8,128)(2,1)S(1)}, u32[]{:S(2)}) copy-start(bf16[208,768]{1,0:T(8,128)(2,1)S(1)} %concatenate.57.refs_6_) | copy-start | bytes 958468
  20.2 8.7 %copy-start.48 = (f32[768]{0:T(1024)S(1)}, f32[768]{0:T(1024)}, u32[]{:S(2)}) copy-start(f32[768]{0:T(1024)} %param.28) | copy-start | bytes 9220
  20.2 8.7 %copy-start.49 = (f32[768]{0:T(1024)S(1)}, f32[768]{0:T(1024)}, u32[]{:S(2)}) copy-start(f32[768]{0:T(1024)} %param.29) | copy-start | bytes 9220
  20.2 8.7 %copy-start.50 = (f32[768]{0:T(1024)S(1)}, f32[768]{0:T(1024)}, u32[]{:S(2)}) copy-start(f32[768]{0:T(1024)} %param.30) | copy-start | bytes 9220
  21.7 26.1 %copy-start.9 = (bf16[384,768]{1,0:T(8,128)(2,1)}, bf16[384,768]{1,0:T(8,128)(2,1)S(1)}, u32[]{:S(2)}) copy-start(bf16[384,768]{1,0:T(8,128)(2,1)S(1)} %get-tuple-element.195.refs_10_) | copy-start | bytes 1769476
  21.7 31.5 %copy-start.8 = (bf16[384,768]{1,0:T(8,128)(2,1)}, bf16[384,768]{1,0:T(8,128)(2,1)S(1)}, u32[]{:S(2)}) copy-start(bf16[384,768]{1,0:T(8,128)(2,1)S(1)} %get-tuple-element.199.refs_14_) | copy-start | bytes 1769476
  24.2 20.8 %collective-permute-start.4 = (bf16[384,768]{1,0:T(8,128)(2,1)S(1)}, bf16[384,768]{1,0:T(8,128)(2,1)S(1)}, u32[]{:S(2)}, u32[]{:S(2)}) collective-permute-start(bf16[384,768]{1,0:T(8,128)(2,1)S(1)} %get-tuple-element.195.refs_10_), channel_id=1, source_target_pairs={{0,2},{1,3},{2,0},{3,1},{4,6},{5,7},{6,4},{7,5},{8,10},{9,11},{10,... | collective-permute-start | bytes 1769480 | tf_op jit(solution)/shard_map/ppermute | solution.py:46
  25.8 19.2 %collective-permute-start.2 = (bf16[2,192,512]{2,1,0:T(8,128)(2,1)S(1)}, bf16[2,192,512]{2,1,0:T(8,128)(2,1)}, u32[]{:S(2)}, u32[]{:S(2)}) collective-permute-start(bf16[2,192,512]{2,1,0:T(8,128)(2,1)S(1)} %pad_maximum_fusion.7), channel_id=1, source_target_pairs={{0,8},{4,12},{8,0},{12,4},{16,24},{20,28},{24,16},{28,20},{1,9},{5... | collective-permute-start | bytes 1179656 | tf_op jit(solution)/shard_map/ppermute | solution.py:46
  29.6 15.5 %collective-permute-start.3 = (bf16[208,768]{1,0:T(8,128)(2,1)S(1)}, bf16[208,768]{1,0:T(8,128)(2,1)S(1)}, u32[]{:S(2)}, u32[]{:S(2)}) collective-permute-start(bf16[208,768]{1,0:T(8,128)(2,1)S(1)} %concatenate.57.refs_6_), channel_id=1, source_target_pairs={{0,2},{1,3},{2,0},{3,1},{4,6},{5,7},{6,4},{7,5},{8,10},{9,11},{10,... | collective-permute-start | bytes 958472 | tf_op jit(solution)/shard_map/ppermute | solution.py:46
  35.4 9.6 %copy-start.57 = (s32[8]{0:T(128)S(1)}, s32[8]{0:T(128)}, u32[]{:S(2)}) copy-start(s32[8]{0:T(128)} %param.17) | copy-start | bytes 100
  38.5 28.6 %copy-start.13 = (bf16[2,192,512]{2,1,0:T(8,128)(2,1)}, bf16[2,192,512]{2,1,0:T(8,128)(2,1)S(1)}, u32[]{:S(2)}) copy-start(bf16[2,192,512]{2,1,0:T(8,128)(2,1)S(1)} %pad_maximum_fusion.8) | copy-start | bytes 1179652
  45.2 21.2 %collective-permute-start.9 = (bf16[384,768]{1,0:T(8,128)(2,1)S(1)}, bf16[384,768]{1,0:T(8,128)(2,1)}, u32[]{:S(2)}, u32[]{:S(2)}) collective-permute-start(bf16[384,768]{1,0:T(8,128)(2,1)S(1)} %get-tuple-element.199.refs_14_), channel_id=1, source_target_pairs={{0,1},{1,0},{2,3},{3,2},{4,5},{5,4},{6,7},{7,6},{8,9},{9,8},{10,11... | collective-permute-start | bytes 1769480 | tf_op jit(solution)/shard_map/ppermute | solution.py:46
  45.9 20.5 %collective-permute-start.6 = (bf16[2,192,512]{2,1,0:T(8,128)(2,1)S(1)}, bf16[2,192,512]{2,1,0:T(8,128)(2,1)S(1)}, u32[]{:S(2)}, u32[]{:S(2)}) collective-permute-start(bf16[2,192,512]{2,1,0:T(8,128)(2,1)S(1)} %pad_maximum_fusion.8), channel_id=1, source_target_pairs={{0,16},{4,20},{8,24},{12,28},{16,0},{20,4},{24,8},{28,12},{1,17},{... | collective-permute-start | bytes 1179656 | tf_op jit(solution)/shard_map/ppermute | solution.py:46
  46.5 20.4 %copy-start.23 = (bf16[384,768]{1,0:T(8,128)(2,1)S(1)}, bf16[384,768]{1,0:T(8,128)(2,1)}, u32[]{:S(2)}) copy-start(bf16[384,768]{1,0:T(8,128)(2,1)} %copy-done.22) | copy-start | bytes 1769476
  47.7 30.7 %copy-start.3 = (bf16[4,192,512]{2,1,0:T(8,128)(2,1)}, bf16[4,192,512]{2,1,0:T(8,128)(2,1)S(1)}, u32[]{:S(2)}) copy-start(bf16[4,192,512]{2,1,0:T(8,128)(2,1)S(1)} %pad_maximum_fusion.1.near_ref.k_near_ref) | copy-start | bytes 2359300
  47.7 19.2 %collective-permute-start.8 = (bf16[384,768]{1,0:T(8,128)(2,1)S(1)}, bf16[384,768]{1,0:T(8,128)(2,1)S(1)}, u32[]{:S(2)}, u32[]{:S(2)}) collective-permute-start(bf16[384,768]{1,0:T(8,128)(2,1)S(1)} %get-tuple-element.195.refs_10_), channel_id=1, source_target_pairs={{0,1},{1,0},{2,3},{3,2},{4,5},{5,4},{6,7},{7,6},{8,9},{9,8},{10,11... | collective-permute-start | bytes 1769480 | tf_op jit(solution)/shard_map/ppermute | solution.py:46
  47.8 2.8 collective-permute-start.7
  48.3 4.9 %collective-permute-start.13 = (bf16[208,768]{1,0:T(8,128)(2,1)S(1)}, bf16[208,768]{1,0:T(8,128)(2,1)S(1)}, u32[]{:S(2)}, u32[]{:S(2)}) collective-permute-start(bf16[208,768]{1,0:T(8,128)(2,1)S(1)} %copy-done.34), channel_id=1, source_target_pairs={{0,1},{1,0},{2,3},{3,2},{4,5},{5,4},{6,7},{7,6},{8,9},{9,8},{10,11... | collective-permute-start | bytes 958472 | tf_op jit(solution)/shard_map/ppermute | solution.py:46
  48.6 18.5 %copy-start.53 = (s32[2]{0:T(128)}, s32[2]{0:T(128)S(1)}, u32[]{:S(2)}) copy-start(s32[2]{0:T(128)S(1)} %get-tuple-element.265) | copy-start | bytes 28
  50.7 20.6 %collective-permute-start.5 = (bf16[4,192,512]{2,1,0:T(8,128)(2,1)S(1)}, bf16[4,192,512]{2,1,0:T(8,128)(2,1)S(1)}, u32[]{:S(2)}, u32[]{:S(2)}) collective-permute-start(bf16[4,192,512]{2,1,0:T(8,128)(2,1)S(1)} %pad_maximum_fusion.1.near_ref.k_near_ref), channel_id=1, source_target_pairs={{0,4},{4,0},{8,12},{12,8},{16,20},{20,16},{24,28},{28,24},{1,5},{5... | collective-permute-start | bytes 2359304 | tf_op jit(solution)/shard_map/ppermute | solution.py:46
  53.2 13.2 %copy-start.36 = (bf16[208,768]{1,0:T(8,128)(2,1)}, bf16[208,768]{1,0:T(8,128)(2,1)S(1)}, u32[]{:S(2)}) copy-start(bf16[208,768]{1,0:T(8,128)(2,1)S(1)} %collective-permute-done.13.refs_9_) | copy-start | bytes 958468
  53.2 17.1 %collective-permute-start.12 = (bf16[384,768]{1,0:T(8,128)(2,1)S(1)}, bf16[384,768]{1,0:T(8,128)(2,1)}, u32[]{:S(2)}, u32[]{:S(2)}) collective-permute-start(bf16[384,768]{1,0:T(8,128)(2,1)S(1)} %get-tuple-element.199.refs_14_), channel_id=1, source_target_pairs={{0,2},{1,3},{2,0},{3,1},{4,6},{5,7},{6,4},{7,5},{8,10},{9,11},{10,... | collective-permute-start | bytes 1769480 | tf_op jit(solution)/shard_map/ppermute | solution.py:46
  66.4 3.9 %collective-permute-start.10 = (bf16[384,768]{1,0:T(8,128)(2,1)}, bf16[384,768]{1,0:T(8,128)(2,1)S(1)}, u32[]{:S(2)}, u32[]{:S(2)}) collective-permute-start(bf16[384,768]{1,0:T(8,128)(2,1)} %get-tuple-element.203.refs_18_), channel_id=1, source_target_pairs={{0,1},{1,0},{2,3},{3,2},{4,5},{5,4},{6,7},{7,6},{8,9},{9,8},{10,11... | collective-permute-start | bytes 1769480 | tf_op jit(solution)/shard_map/ppermute | solution.py:46
  66.4 3.9 %collective-permute-start.11 = (bf16[384,768]{1,0:T(8,128)(2,1)}, bf16[384,768]{1,0:T(8,128)(2,1)S(1)}, u32[]{:S(2)}, u32[]{:S(2)}) collective-permute-start(bf16[384,768]{1,0:T(8,128)(2,1)} %get-tuple-element.207.refs_22_), channel_id=1, source_target_pairs={{0,1},{1,0},{2,3},{3,2},{4,5},{5,4},{6,7},{7,6},{8,9},{9,8},{10,11... | collective-permute-start | bytes 1769480 | tf_op jit(solution)/shard_map/ppermute | solution.py:46
  66.9 3.4 collective-permute-start.14
  69.1 29.1 %copy-start.44 = (f32[3,33]{1,0:T(4,128)S(1)}, f32[3,33]{1,0:T(4,128)}, u32[]{:S(2)}) copy-start(f32[3,33]{1,0:T(4,128)} %param.20) | copy-start | bytes 1192
  70.2 28.7 %copy-start.1 = (bf16[4,192,512]{2,1,0:T(8,128)(2,1)}, bf16[4,192,512]{2,1,0:T(8,128)(2,1)S(1)}, u32[]{:S(2)}) copy-start(bf16[4,192,512]{2,1,0:T(8,128)(2,1)S(1)} %pad_maximum_fusion.2.v_near_ref.before_near_ref.after_near_ref) | copy-start | bytes 2359300
  71.3 20.8 %collective-permute-start.15 = (bf16[4,192,512]{2,1,0:T(8,128)(2,1)S(1)}, bf16[4,192,512]{2,1,0:T(8,128)(2,1)S(1)}, u32[]{:S(2)}, u32[]{:S(2)}) collective-permute-start(bf16[4,192,512]{2,1,0:T(8,128)(2,1)S(1)} %pad_maximum_fusion.2.v_near_ref.before_near_ref.after_near_ref), channel_id=1, source_target_pairs={{0,8},{4,12},{8,0},{12,4},{16,24},{20,28},{24,16},{28,20},{1,9},{5... | collective-permute-start | bytes 2359304 | tf_op jit(solution)/shard_map/ppermute | solution.py:46
  74.8 15.0 %collective-permute-start.16 = (bf16[384,768]{1,0:T(8,128)(2,1)}, bf16[384,768]{1,0:T(8,128)(2,1)}, u32[]{:S(2)}, u32[]{:S(2)}) collective-permute-start(bf16[384,768]{1,0:T(8,128)(2,1)} %get-tuple-element.203.refs_18_), channel_id=1, source_target_pairs={{0,2},{1,3},{2,0},{3,1},{4,6},{5,7},{6,4},{7,5},{8,10},{9,11},{10,... | collective-permute-start | bytes 1769480 | tf_op jit(solution)/shard_map/ppermute | solution.py:46
  76.4 13.4 %collective-permute-start.17 = (bf16[384,768]{1,0:T(8,128)(2,1)}, bf16[384,768]{1,0:T(8,128)(2,1)}, u32[]{:S(2)}, u32[]{:S(2)}) collective-permute-start(bf16[384,768]{1,0:T(8,128)(2,1)} %collective-permute-done.12.refs_15_), channel_id=1, source_target_pairs={{0,1},{1,0},{2,3},{3,2},{4,5},{5,4},{6,7},{7,6},{8,9},{9,8},{10,11... | collective-permute-start | bytes 1769480 | tf_op jit(solution)/shard_map/ppermute | solution.py:46
  92.2 16.5 %collective-permute-start.19 = (bf16[384,768]{1,0:T(8,128)(2,1)}, bf16[384,768]{1,0:T(8,128)(2,1)S(1)}, u32[]{:S(2)}, u32[]{:S(2)}) collective-permute-start(bf16[384,768]{1,0:T(8,128)(2,1)} %get-tuple-element.207.refs_22_), channel_id=1, source_target_pairs={{0,2},{1,3},{2,0},{3,1},{4,6},{5,7},{6,4},{7,5},{8,10},{9,11},{10,... | collective-permute-start | bytes 1769480 | tf_op jit(solution)/shard_map/ppermute | solution.py:46
  93.7 15.0 %collective-permute-start.20 = (bf16[384,768]{1,0:T(8,128)(2,1)}, bf16[384,768]{1,0:T(8,128)(2,1)S(1)}, u32[]{:S(2)}, u32[]{:S(2)}) collective-permute-start(bf16[384,768]{1,0:T(8,128)(2,1)} %collective-permute-done.16.refs_19_), channel_id=1, source_target_pairs={{0,1},{1,0},{2,3},{3,2},{4,5},{5,4},{6,7},{7,6},{8,9},{9,8},{10,11... | collective-permute-start | bytes 1769480 | tf_op jit(solution)/shard_map/ppermute | solution.py:46
  93.7 15.0 %collective-permute-start.18 = (bf16[192,512]{1,0:T(8,128)(2,1)}, bf16[192,512]{1,0:T(8,128)(2,1)S(1)}, u32[]{:S(2)}, u32[]{:S(2)}) collective-permute-start(bf16[192,512]{1,0:T(8,128)(2,1)} %get-tuple-element.167), channel_id=1, source_target_pairs={{0,16},{4,20},{8,24},{12,28},{16,0},{20,4},{24,8},{28,12},{1,17},{... | collective-permute-start | bytes 589832 | tf_op jit(solution)/shard_map/ppermute | solution.py:46
  98.9 9.8 %copy-start.40 = (bf16[192,512]{1,0:T(8,128)(2,1)S(1)}, bf16[192,512]{1,0:T(8,128)(2,1)}, u32[]{:S(2)}) copy-start(bf16[192,512]{1,0:T(8,128)(2,1)} %get-tuple-element.167) | copy-start | bytes 589828
  108.6 11.9 %copy-start.15 = (bf16[512,192]{1,0:T(8,128)(2,1)S(1)}, bf16[512,192]{1,0:T(8,128)(2,1)}, u32[]{:S(2)}) copy-start(bf16[512,192]{1,0:T(8,128)(2,1)} %get-tuple-element.174) | copy-start | bytes 589828
  108.6 12.0 %copy-start.28 = (bf16[384,768]{1,0:T(8,128)(2,1)}, bf16[384,768]{1,0:T(8,128)(2,1)S(1)}, u32[]{:S(2)}) copy-start(bf16[384,768]{1,0:T(8,128)(2,1)S(1)} %collective-permute-done.19.refs_23_) | copy-start | bytes 1769476
  108.7 12.0 %copy-start.29 = (bf16[384,768]{1,0:T(8,128)(2,1)}, bf16[384,768]{1,0:T(8,128)(2,1)S(1)}, u32[]{:S(2)}) copy-start(bf16[384,768]{1,0:T(8,128)(2,1)S(1)} %collective-permute-done.20.refs_21_) | copy-start | bytes 1769476
  108.7 11.8 %collective-permute-start.23 = (bf16[384,768]{1,0:T(8,128)(2,1)S(1)}, bf16[384,768]{1,0:T(8,128)(2,1)S(1)}, u32[]{:S(2)}, u32[]{:S(2)}) collective-permute-start(bf16[384,768]{1,0:T(8,128)(2,1)S(1)} %collective-permute-done.19.refs_23_), channel_id=1, source_target_pairs={{0,1},{1,0},{2,3},{3,2},{4,5},{5,4},{6,7},{7,6},{8,9},{9,8},{10,11... | collective-permute-start | bytes 1769480 | tf_op jit(solution)/shard_map/ppermute | solution.py:46
  108.8 11.6 %collective-permute-start.22 = (bf16[2,192,512]{2,1,0:T(8,128)(2,1)S(1)}, bf16[2,192,512]{2,1,0:T(8,128)(2,1)S(1)}, u32[]{:S(2)}, u32[]{:S(2)}) collective-permute-start(bf16[2,192,512]{2,1,0:T(8,128)(2,1)S(1)} %pad_maximum_fusion.9), channel_id=1, source_target_pairs={{0,8},{4,12},{8,0},{12,4},{16,24},{20,28},{24,16},{28,20},{1,9},{5... | collective-permute-start | bytes 1179656 | tf_op jit(solution)/shard_map/ppermute | solution.py:46
  109.4 11.1 %collective-permute-start.21 = (bf16[512,192]{1,0:T(8,128)(2,1)}, bf16[512,192]{1,0:T(8,128)(2,1)S(1)}, u32[]{:S(2)}, u32[]{:S(2)}) collective-permute-start(bf16[512,192]{1,0:T(8,128)(2,1)} %get-tuple-element.174), channel_id=1, source_target_pairs={{0,2},{1,3},{2,0},{3,1},{4,6},{5,7},{6,4},{7,5},{8,10},{9,11},{10,... | collective-permute-start | bytes 589832 | tf_op jit(solution)/shard_map/ppermute | solution.py:46
  120.5 33.7 %copy-start.4 = (bf16[4,192,512]{2,1,0:T(8,128)(2,1)}, bf16[4,192,512]{2,1,0:T(8,128)(2,1)S(1)}, u32[]{:S(2)}) copy-start(bf16[4,192,512]{2,1,0:T(8,128)(2,1)S(1)} %pad_maximum_fusion.3.near_ref.q_near_ref) | copy-start | bytes 2359300
  120.6 8.2 %collective-permute-start.24 = (bf16[2,512,192]{2,1,0:T(8,128)(2,1)S(1)}, bf16[2,512,192]{2,1,0:T(8,128)(2,1)S(1)}, u32[]{:S(2)}, u32[]{:S(2)}) collective-permute-start(bf16[2,512,192]{2,1,0:T(8,128)(2,1)S(1)} %pad_maximum_fusion.5.refs_1_), channel_id=1, source_target_pairs={{0,1},{1,0},{2,3},{3,2},{4,5},{5,4},{6,7},{7,6},{8,9},{9,8},{10,11... | collective-permute-start | bytes 1179656 | tf_op jit(solution)/shard_map/ppermute | solution.py:46
  120.7 45.8 %collective-permute-start.26 = (bf16[4,192,512]{2,1,0:T(8,128)(2,1)S(1)}, bf16[4,192,512]{2,1,0:T(8,128)(2,1)S(1)}, u32[]{:S(2)}, u32[]{:S(2)}) collective-permute-start(bf16[4,192,512]{2,1,0:T(8,128)(2,1)S(1)} %pad_maximum_fusion.3.near_ref.q_near_ref), channel_id=1, source_target_pairs={{0,4},{4,0},{8,12},{12,8},{16,20},{20,16},{24,28},{28,24},{1,5},{5... | collective-permute-start | bytes 2359304 | tf_op jit(solution)/shard_map/ppermute | solution.py:46
  154.2 12.4 %collective-permute-start.25 = (bf16[192,512]{1,0:T(8,128)(2,1)}, bf16[192,512]{1,0:T(8,128)(2,1)S(1)}, u32[]{:S(2)}, u32[]{:S(2)}) collective-permute-start(bf16[192,512]{1,0:T(8,128)(2,1)} %get-tuple-element.213), channel_id=1, source_target_pairs={{0,16},{4,20},{8,24},{12,28},{16,0},{20,4},{24,8},{28,12},{1,17},{... | collective-permute-start | bytes 589832 | tf_op jit(solution)/shard_map/ppermute | solution.py:46
  166.6 14.6 %copy-start.6 = (bf16[4,192,512]{2,1,0:T(8,128)(2,1)}, bf16[4,192,512]{2,1,0:T(8,128)(2,1)S(1)}, u32[]{:S(2)}) copy-start(bf16[4,192,512]{2,1,0:T(8,128)(2,1)S(1)} %collective-permute-done.26.far_ref.q_far_ref) | copy-start | bytes 2359300
  166.6 15.3 %collective-permute-start.27 = (bf16[2,192,512]{2,1,0:T(8,128)(2,1)S(1)}, bf16[2,192,512]{2,1,0:T(8,128)(2,1)S(1)}, u32[]{:S(2)}, u32[]{:S(2)}) collective-permute-start(bf16[2,192,512]{2,1,0:T(8,128)(2,1)S(1)} %pad_maximum_fusion.10), channel_id=1, source_target_pairs={{0,8},{4,12},{8,0},{12,4},{16,24},{20,28},{24,16},{28,20},{1,9},{5... | collective-permute-start | bytes 1179656 | tf_op jit(solution)/shard_map/ppermute | solution.py:46
  166.7 14.4 %collective-permute-start.28 = (bf16[192,128]{1,0:T(8,128)(2,1)S(1)}, bf16[192,128]{1,0:T(8,128)(2,1)S(1)}, u32[]{:S(2)}, u32[]{:S(2)}) collective-permute-start(bf16[192,128]{1,0:T(8,128)(2,1)S(1)} %get-tuple-element.279), channel_id=1, source_target_pairs={{0,4},{4,8},{8,12},{12,16},{16,20},{20,24},{24,28},{1,5},{5,9},{9,... | collective-permute-start | bytes 147464 | tf_op jit(solution)/shard_map/ppermute | solution.py:549
  170.4 10.7 %collective-permute-start.29 = (bf16[192,128]{1,0:T(8,128)(2,1)S(1)}, bf16[192,128]{1,0:T(8,128)(2,1)S(1)}, u32[]{:S(2)}, u32[]{:S(2)}) collective-permute-start(bf16[192,128]{1,0:T(8,128)(2,1)S(1)} %get-tuple-element.280), channel_id=1, source_target_pairs={{4,0},{8,4},{12,8},{16,12},{20,16},{24,20},{28,24},{5,1},{9,5},{13... | collective-permute-start | bytes 147464 | tf_op jit(solution)/shard_map/ppermute | solution.py:550
  182.0 27.4 %collective-permute-start.30 = (bf16[4,192,512]{2,1,0:T(8,128)(2,1)S(1)}, bf16[4,192,512]{2,1,0:T(8,128)(2,1)S(1)}, u32[]{:S(2)}, u32[]{:S(2)}) collective-permute-start(bf16[4,192,512]{2,1,0:T(8,128)(2,1)S(1)} %pad_maximum_fusion.4.da_near_ref), channel_id=1, source_target_pairs={{0,4},{4,0},{8,12},{12,8},{16,20},{20,16},{24,28},{28,24},{1,5},{5... | collective-permute-start | bytes 2359304 | tf_op jit(solution)/shard_map/ppermute | solution.py:46
  188.3 13.6 %copy-start = (bf16[3,768,192]{1,2,0:T(8,128)(2,1)S(1)}, bf16[3,768,192]{1,2,0:T(8,128)(2,1)}, u32[]{:S(2)}) copy-start(bf16[3,768,192]{1,2,0:T(8,128)(2,1)} %param.18) | copy-start | bytes 2654212
  188.3 13.6 %copy-start.39 = (bf16[512,192]{1,0:T(8,128)(2,1)S(1)}, bf16[512,192]{1,0:T(8,128)(2,1)}, u32[]{:S(2)}) copy-start(bf16[512,192]{1,0:T(8,128)(2,1)} %get-tuple-element.229) | copy-start | bytes 589828
  223.4 12.0 %collective-permute-start.34 = (bf16[320,768]{1,0:T(8,128)(2,1)S(1)}, bf16[320,768]{1,0:T(8,128)(2,1)S(1)}, u32[]{:S(2)}, u32[]{:S(2)}) collective-permute-start(bf16[320,768]{1,0:T(8,128)(2,1)S(1)} %constant_dynamic-slice_fusion.1), channel_id=1, source_target_pairs={{0,4},{4,0},{8,12},{12,8},{16,20},{20,16},{24,28},{28,24},{1,5},{5... | collective-permute-start | bytes 1474568 | tf_op jit(solution)/shard_map/ppermute | solution.py:46
  235.6 27.5 %collective-permute-start.35 = (bf16[160,768]{1,0:T(8,128)(2,1)S(1)}, bf16[160,768]{1,0:T(8,128)(2,1)S(1)}, u32[]{:S(2)}, u32[]{:S(2)}) collective-permute-start(bf16[160,768]{1,0:T(8,128)(2,1)S(1)} %constant_dynamic-slice_fusion), channel_id=1, source_target_pairs={{0,8},{4,12},{8,0},{12,4},{16,24},{20,28},{24,16},{28,20},{1,9},{5... | collective-permute-start | bytes 737288 | tf_op jit(solution)/shard_map/ppermute | solution.py:46
  257.6 5.7 %collective-permute-start.31 = (bf16[256,768]{1,0:T(8,128)(2,1)S(1)}, bf16[256,768]{1,0:T(8,128)(2,1)S(1)}, u32[]{:S(2)}, u32[]{:S(2)}) collective-permute-start(bf16[256,768]{1,0:T(8,128)(2,1)S(1)} %constant_dynamic-slice_fusion.2), channel_id=1, source_target_pairs={{0,1},{1,0},{2,3},{3,2},{4,5},{5,4},{6,7},{7,6},{8,9},{9,8},{10,11... | collective-permute-start | bytes 1179656 | tf_op jit(solution)/shard_map/ppermute | solution.py:46
  263.2 20.3 %collective-permute-start.36 = (bf16[160,768]{1,0:T(8,128)(2,1)S(1)}, bf16[160,768]{1,0:T(8,128)(2,1)S(1)}, u32[]{:S(2)}, u32[]{:S(2)}) collective-permute-start(bf16[160,768]{1,0:T(8,128)(2,1)S(1)} %add_convert_fusion.6), channel_id=1, source_target_pairs={{0,16},{4,20},{8,24},{12,28},{16,0},{20,4},{24,8},{28,12},{1,17},{... | collective-permute-start | bytes 737288 | tf_op jit(solution)/shard_map/ppermute | solution.py:46
  263.4 20.3 %collective-permute-start.32 = (bf16[256,768]{1,0:T(8,128)(2,1)S(1)}, bf16[256,768]{1,0:T(8,128)(2,1)S(1)}, u32[]{:S(2)}, u32[]{:S(2)}) collective-permute-start(bf16[256,768]{1,0:T(8,128)(2,1)S(1)} %add_convert_fusion.4), channel_id=1, source_target_pairs={{0,2},{1,3},{2,0},{3,1},{4,6},{5,7},{6,4},{7,5},{8,10},{9,11},{10,... | collective-permute-start | bytes 1179656 | tf_op jit(solution)/shard_map/ppermute | solution.py:46
  283.6 7.0 %collective-permute-start.37 = (bf16[160,768]{1,0:T(8,128)(2,1)S(1)}, bf16[160,768]{1,0:T(8,128)(2,1)S(1)}, u32[]{:S(2)}, u32[]{:S(2)}) collective-permute-start(bf16[160,768]{1,0:T(8,128)(2,1)S(1)} %add_convert_fusion.5), channel_id=1, source_target_pairs={{0,8},{4,12},{8,0},{12,4},{16,24},{20,28},{24,16},{28,20},{1,9},{5... | collective-permute-start | bytes 737288 | tf_op jit(solution)/shard_map/ppermute | solution.py:46
  283.9 7.0 %collective-permute-start.33 = (bf16[256,768]{1,0:T(8,128)(2,1)S(1)}, bf16[256,768]{1,0:T(8,128)(2,1)S(1)}, u32[]{:S(2)}, u32[]{:S(2)}) collective-permute-start(bf16[256,768]{1,0:T(8,128)(2,1)S(1)} %add_convert_fusion.3), channel_id=1, source_target_pairs={{0,1},{1,0},{2,3},{3,2},{4,5},{5,4},{6,7},{7,6},{8,9},{9,8},{10,11... | collective-permute-start | bytes 1179656 | tf_op jit(solution)/shard_map/ppermute | solution.py:46
  290.7 34.1 %collective-permute-start.38 = (bf16[320,768]{1,0:T(8,128)(2,1)S(1)}, bf16[320,768]{1,0:T(8,128)(2,1)S(1)}, u32[]{:S(2)}, u32[]{:S(2)}) collective-permute-start(bf16[320,768]{1,0:T(8,128)(2,1)S(1)} %pad_maximum_fusion.6), channel_id=1, source_target_pairs={{0,4},{4,0},{8,12},{12,8},{16,20},{20,16},{24,28},{28,24},{1,5},{5... | collective-permute-start | bytes 1474568 | tf_op jit(solution)/shard_map/ppermute | solution.py:46
  (34 other events, 176.8 us)
Sparse Core Ops, SparseCore 0:
  188.4 136.4 all-reduce.4
